TPU v7x, 32 devices: a whole 2x2x4 slice. The times are simulated.
32 devices in a mesh: dp: 16 (over z, y, x), dim: 2 (over core).
Axes of the slice: x: 2, y: 2, z: 4, core: 2. Of those that a mesh axis runs over, the one named last changes fastest.
Arguments:
- tokens: bfloat16 [49152, 768], P(('dp', 'dim')), may hold values from -6 to 6
- doc_lengths: int32 [16, 2], P('dp'), may hold values from 1024 to 1820, as said below
- pair_index: int32 [32], P('dp'), may hold values from 0 to 255
- target_bank: bfloat16 [256, 768], P(None, 'dim'), may hold values from -6 to 6
- mixer_in: float32 [1, 768, 2304], P(None, ('dp', 'dim')), may hold values from -0.21875 to 0.21875
- mixer_out: float32 [1, 768, 768], P(None, ('dp', 'dim')), may hold values from -1.75 to 1.75
- expand: float32 [1, 768, 6144], P(None, ('dp', 'dim')), may hold values from -0.21875 to 0.21875
- contract: float32 [1, 3072, 768], P(None, ('dp', 'dim')), may hold values from -0.109375 to 0.109375
- norm_params: float32 [1, 4, 768], P(None, None, ('dp', 'dim')), as said below
- mixer_in_moment: float32 [1, 768, 2304], P(None, ('dp', 'dim')), may hold values from -64 to 64
- mixer_out_moment: float32 [1, 768, 768], P(None, ('dp', 'dim')), may hold values from -64 to 64
- expand_moment: float32 [1, 768, 6144], P(None, ('dp', 'dim')), may hold values from -64 to 64
- contract_moment: float32 [1, 3072, 768], P(None, ('dp', 'dim')), may hold values from -64 to 64
- norm_moment: float32 [1, 4, 768], P(None, None, ('dp', 'dim')), may hold values from -128 to 128
- mixer_in_average: float32 [1, 768, 2304], P(None, ('dp', 'dim')), may hold values from -0.21875 to 0.21875
- mixer_out_average: float32 [1, 768, 768], P(None, ('dp', 'dim')), may hold values from -1.75 to 1.75
- expand_average: float32 [1, 768, 6144], P(None, ('dp', 'dim')), may hold values from -0.21875 to 0.21875
- contract_average: float32 [1, 3072, 768], P(None, ('dp', 'dim')), may hold values from -0.109375 to 0.109375
- norm_average: float32 [1, 4, 768], P(None, None, ('dp', 'dim')), as said below
Outputs:
- embeddings: float32 [32, 768], P('dp', 'dim')
- token_grads: float32 [49152, 768], P(('dp', 'dim'))
- mixer_in_grad: float32 [1, 768, 2304], P(None, ('dp', 'dim'))
- mixer_out_grad: float32 [1, 768, 768], P(None, ('dp', 'dim'))
- expand_grad: float32 [1, 768, 6144], P(None, ('dp', 'dim'))
- contract_grad: float32 [1, 3072, 768], P(None, ('dp', 'dim'))
- norm_grad: float32 [1, 4, 768], P(None, None, ('dp', 'dim'))
- mixer_in_next: float32 [1, 768, 2304], P(None, ('dp', 'dim'))
- mixer_out_next: float32 [1, 768, 768], P(None, ('dp', 'dim'))
- expand_next: float32 [1, 768, 6144], P(None, ('dp', 'dim'))
- contract_next: float32 [1, 3072, 768], P(None, ('dp', 'dim'))
- norm_next: float32 [1, 4, 768], P(None, None, ('dp', 'dim'))
- mixer_in_moment_next: float32 [1, 768, 2304], P(None, ('dp', 'dim'))
- mixer_out_moment_next: float32 [1, 768, 768], P(None, ('dp', 'dim'))
- expand_moment_next: float32 [1, 768, 6144], P(None, ('dp', 'dim'))
- contract_moment_next: float32 [1, 3072, 768], P(None, ('dp', 'dim'))
- norm_moment_next: float32 [1, 4, 768], P(None, None, ('dp', 'dim'))
- mixer_in_average_next: float32 [1, 768, 2304], P(None, ('dp', 'dim'))
- mixer_out_average_next: float32 [1, 768, 768], P(None, ('dp', 'dim'))
- expand_average_next: float32 [1, 768, 6144], P(None, ('dp', 'dim'))
- contract_average_next: float32 [1, 3072, 768], P(None, ('dp', 'dim'))
- norm_average_next: float32 [1, 4, 768], P(None, None, ('dp', 'dim'))
- mixer_in_copy: bfloat16 [1, 768, 2304], P(None, ('dp', 'dim'))
- mixer_out_copy: bfloat16 [1, 768, 768], P(None, ('dp', 'dim'))
- expand_copy: bfloat16 [1, 768, 6144], P(None, ('dp', 'dim'))
- contract_copy: bfloat16 [1, 3072, 768], P(None, ('dp', 'dim'))
- norm_copy: bfloat16 [1, 4, 768], P(None, None, ('dp', 'dim'))
Inputs may be any that keep to these rules, and one draw needn't show every extreme that they name: `doc_lengths`: each document of a group holds at least 1024 rows, and a group's documents together hold fewer than 3072 rows. `norm_params`: rows 0 and 2 of each layer are gains, rows 1 and 3 biases. `norm_average`: laid out as norm_params.
All inputs are finite; a program needn't handle non-finite values.
Results may differ from a plain program's by a relative error of at most 0.015.
Values may be sent and summed in bfloat16 or wider, within the bound.
A program may use at most 256 MiB of HBM per device.

v0:
```python
import math

import jax
import jax.numpy as jnp
from jax import lax
from jax.sharding import PartitionSpec as P

HEAD = 64


NORM_EPSILON = 1e-05
COSINE_EPSILON = 1e-06
MOMENTUM = 0.5
AVERAGE_DECAY = 0.5
PRECISE = lax.Precision.HIGHEST
MASKED = -1e30


def matmul(left_op, right_op):
    return jnp.dot(left_op, right_op, preferred_element_type=jnp.float32)


def matmul_exact(left_op, right_op):
    return jnp.dot(left_op, right_op, precision=PRECISE, preferred_element_type=jnp.float32)


def inner_rows(left_op, right_op):
    return lax.dot_general(
        left_op, right_op, (((0,), (0,)), ((), ())), preferred_element_type=jnp.float32
    )


def inner_cols(left_op, right_op):
    return lax.dot_general(
        left_op, right_op, (((1,), (1,)), ((), ())), preferred_element_type=jnp.float32
    )


def rotate(values, cosines, sines):
    row_count = values.shape[0]
    shaped = values.reshape(row_count, -1, 2, HEAD // 2)
    former = shaped[:, :, 0, :]
    latter = shaped[:, :, 1, :]
    cosine_b = cosines[:, None, :]
    sine_b = sines[:, None, :]
    turned = jnp.stack(
        [former * cosine_b - latter * sine_b, latter * cosine_b + former * sine_b], axis=2
    )
    return turned.reshape(values.shape)


def rotate_back(grads_in, cosines, sines):
    row_count = grads_in.shape[0]
    shaped = grads_in.reshape(row_count, -1, 2, HEAD // 2)
    former = shaped[:, :, 0, :]
    latter = shaped[:, :, 1, :]
    cosine_b = cosines[:, None, :]
    sine_b = sines[:, None, :]
    turned = jnp.stack(
        [former * cosine_b + latter * sine_b, latter * cosine_b - former * sine_b], axis=2
    )
    return turned.reshape(grads_in.shape)


def normalize(summed, gain_vec, bias_vec):
    centred = summed - jnp.mean(summed, axis=1, keepdims=True)
    scaling = lax.rsqrt(jnp.mean(centred * centred, axis=1, keepdims=True) + NORM_EPSILON)
    return centred * scaling * gain_vec + bias_vec


def normalize_back(grad_in, summed, gain_vec):
    centred = summed - jnp.mean(summed, axis=1, keepdims=True)
    scaling = lax.rsqrt(jnp.mean(centred * centred, axis=1, keepdims=True) + NORM_EPSILON)
    unit = centred * scaling
    grad_unit = grad_in * gain_vec
    grad_sum = scaling * (
        grad_unit
        - jnp.mean(grad_unit, axis=1, keepdims=True)
        - unit * jnp.mean(grad_unit * unit, axis=1, keepdims=True)
    )
    return (grad_sum, jnp.sum(grad_in * unit, axis=0), jnp.sum(grad_in, axis=0))


def flatten(stacked):
    return stacked.transpose(1, 0, 2).reshape(stacked.shape[1], -1)


def attend(q_rot, all_keys, all_values, same_doc):
    head_count = q_rot.shape[1] // HEAD

    def one_head(head_pos):
        offset = head_pos * HEAD
        query_part = lax.dynamic_slice_in_dim(q_rot, offset, HEAD, 1)
        key_part = lax.dynamic_slice_in_dim(all_keys, offset, HEAD, 1)
        value_part = lax.dynamic_slice_in_dim(all_values, offset, HEAD, 1)
        scores = jnp.where(same_doc, inner_cols(query_part, key_part) * 0.125, MASKED)
        row_max = jnp.max(scores, axis=1, keepdims=True)
        exponent = jnp.exp(scores - row_max)
        row_total = jnp.sum(exponent, axis=1, keepdims=True)
        attn_probs = (exponent / row_total).astype(jnp.bfloat16)
        return (matmul(attn_probs, value_part), (row_max + jnp.log(row_total))[:, 0])

    outputs, log_totals = lax.map(one_head, jnp.arange(head_count, dtype=jnp.int32))
    return (flatten(outputs), log_totals)


def attend_back(q_rot, all_keys, all_values, same_doc, grad_out, log_totals):
    head_count = q_rot.shape[1] // HEAD

    def one_head(pack):
        head_pos, log_total = pack
        offset = head_pos * HEAD
        query_part = lax.dynamic_slice_in_dim(q_rot, offset, HEAD, 1)
        key_part = lax.dynamic_slice_in_dim(all_keys, offset, HEAD, 1)
        value_part = lax.dynamic_slice_in_dim(all_values, offset, HEAD, 1)
        grad_part = lax.dynamic_slice_in_dim(grad_out, offset, HEAD, 1)
        scores = jnp.where(same_doc, inner_cols(query_part, key_part) * 0.125, MASKED)
        attn_probs = jnp.exp(scores - log_total[:, None])
        grad_probs = inner_cols(grad_part, value_part)
        row_dot = jnp.sum(attn_probs * grad_probs, axis=1, keepdims=True)
        grad_scores = (attn_probs * (grad_probs - row_dot)).astype(jnp.bfloat16)
        grad_query = matmul(grad_scores, key_part) * 0.125
        grad_key = inner_rows(grad_scores, query_part) * 0.125
        grad_value = inner_rows(attn_probs.astype(jnp.bfloat16), grad_part)
        return (grad_query, grad_key, grad_value)

    mapped = lax.map(one_head, (jnp.arange(head_count, dtype=jnp.int32), log_totals))
    return (flatten(mapped[0]), flatten(mapped[1]), flatten(mapped[2]))


def advance(weight, moment, average, grad_in, rate):
    moment_next = MOMENTUM * moment + grad_in
    weight_next = weight - rate * (grad_in + MOMENTUM * moment_next)
    average_next = AVERAGE_DECAY * average + (1.0 - AVERAGE_DECAY) * weight_next
    return (weight_next, moment_next, average_next, weight_next.astype(jnp.bfloat16))


def body(
    tokens,
    doc_lengths,
    pair_index,
    target_bank,
    mixer_in,
    mixer_out,
    expand,
    contract,
    norm_params,
    mixer_in_moment,
    mixer_out_moment,
    expand_moment,
    contract_moment,
    norm_moment,
    mixer_in_average,
    mixer_out_average,
    expand_average,
    contract_average,
    norm_average,
):
    local_rows, model_width = tokens.shape
    slices = lax.axis_size("dim")
    group_rows = local_rows * slices
    position = lax.axis_index("dim")
    layer_count = mixer_in.shape[0]
    doc_count = doc_lengths.shape[1]
    lengths = doc_lengths[0]
    doc_ends = jnp.cumsum(lengths)
    doc_starts = doc_ends - lengths
    row_ids = position * local_rows + jnp.arange(local_rows, dtype=jnp.int32)
    key_ids = jnp.arange(group_rows, dtype=jnp.int32)
    seg_rows = jnp.sum((row_ids[:, None] >= doc_ends[None, :]).astype(jnp.int32), axis=1)
    seg_keys = jnp.sum((key_ids[:, None] >= doc_ends[None, :]).astype(jnp.int32), axis=1)
    first_rows = jnp.concatenate([doc_starts, doc_ends[-1:]])
    segment_ids = jnp.arange(doc_count + 1, dtype=jnp.int32)
    row_begin = jnp.sum(
        jnp.where(seg_rows[:, None] == segment_ids[None, :], first_rows[None, :], 0), axis=1
    )
    frequency = jnp.power(1000.0, -jnp.arange(0, HEAD, 2).astype(jnp.float32) / HEAD)
    angles = (row_ids - row_begin).astype(jnp.float32)[:, None] * frequency[None, :]
    cosines = jnp.cos(angles)
    sines = jnp.sin(angles)
    same_doc = seg_rows[:, None] == seg_keys[None, :]
    stream = tokens.astype(jnp.float32)
    layer_pos = 0
    layer_weights = (
        lax.all_gather(mixer_in[layer_pos].astype(jnp.bfloat16), ("dp", "dim"), axis=0, tiled=True),
        lax.all_gather(
            mixer_out[layer_pos].astype(jnp.bfloat16), ("dp", "dim"), axis=0, tiled=True
        ),
        lax.all_gather(expand[layer_pos].astype(jnp.bfloat16), ("dp", "dim"), axis=0, tiled=True),
        lax.all_gather(contract[layer_pos].astype(jnp.bfloat16), ("dp", "dim"), axis=0, tiled=True),
        lax.all_gather(
            norm_params[layer_pos].astype(jnp.bfloat16), ("dp", "dim"), axis=1, tiled=True
        ),
    )
    w_mix, w_out, w_exp, w_con, w_norm = layer_weights
    norm_gains = w_norm.astype(jnp.float32)
    x_low = stream.astype(jnp.bfloat16)
    mixed = matmul(x_low, w_mix)
    q_rot = rotate(mixed[:, 0:model_width], cosines, sines).astype(jnp.bfloat16)
    k_rot = rotate(mixed[:, model_width : 2 * model_width], cosines, sines).astype(jnp.bfloat16)
    v_low = mixed[:, 2 * model_width : 3 * model_width].astype(jnp.bfloat16)
    all_keys = lax.all_gather(k_rot, "dim", axis=0, tiled=True)
    all_values = lax.all_gather(v_low, "dim", axis=0, tiled=True)
    attended, log_totals = attend(q_rot, all_keys, all_values, same_doc)
    att_low = attended.astype(jnp.bfloat16)
    first_sum = stream + matmul(att_low, w_out)
    normed = normalize(first_sum, norm_gains[0], norm_gains[1])
    y_low = normed.astype(jnp.bfloat16)
    gate_up = matmul(y_low, w_exp)
    half = gate_up.shape[1] // 2
    hidden = (jax.nn.silu(gate_up[:, 0:half]) * gate_up[:, half : 2 * half]).astype(jnp.bfloat16)
    second_sum = normed + matmul(hidden, w_con)
    saved = [
        (
            stream,
            layer_weights,
            q_rot,
            k_rot,
            v_low,
            all_keys,
            all_values,
            log_totals,
            attended,
            att_low,
            first_sum,
            normed,
            y_low,
            gate_up,
            hidden,
            second_sum,
        )
    ]
    stream = normalize(second_sum, norm_gains[2], norm_gains[3])
    member = (seg_rows[None, :] == jnp.arange(doc_count, dtype=jnp.int32)[:, None]).astype(
        jnp.float32
    )
    partial_value = matmul_exact(member, stream)
    pooled = lax.psum_scatter(partial_value, "dim", scatter_dimension=1, tiled=True)
    length_f = lengths.astype(jnp.float32)
    embeddings = pooled / length_f[:, None]
    share = embeddings.shape[1]
    pick = (
        pair_index[:, None] == jnp.arange(target_bank.shape[0], dtype=jnp.int32)[None, :]
    ).astype(jnp.bfloat16)
    targets = matmul(pick, target_bank)
    feature_ids = position * share + jnp.arange(share, dtype=jnp.int32)
    cuts = jnp.array(
        [model_width // 12, model_width // 6, model_width // 3, 2 * model_width // 3, model_width],
        dtype=jnp.int32,
    )
    masks = (feature_ids[None, :] < cuts[:, None]).astype(jnp.float32)
    cross = matmul_exact(embeddings * targets, masks.T)
    own = matmul_exact(embeddings * embeddings, masks.T)
    other = matmul_exact(targets * targets, masks.T)
    cross, own, other = lax.psum((cross, own, other), "dim")
    own_root = lax.rsqrt(own + COSINE_EPSILON)
    other_root = lax.rsqrt(other + COSINE_EPSILON)
    cosine = cross * own_root * other_root
    coef_target = -length_f[:, None] * own_root * other_root
    coef_self = length_f[:, None] * cosine * own_root * own_root
    grad_emb = (
        matmul_exact(coef_target, masks) * targets + matmul_exact(coef_self, masks) * embeddings
    )
    grad_full = lax.all_gather(grad_emb, "dim", axis=1, tiled=True)
    spread_rows = member / length_f[:, None]
    grad_stream = lax.dot_general(
        spread_rows,
        grad_full,
        (((0,), (0,)), ((), ())),
        precision=PRECISE,
        preferred_element_type=jnp.float32,
    )
    grad_list = [None] * layer_count
    for layer_pos in reversed(range(layer_count)):
        (
            layer_input,
            layer_weights,
            q_rot,
            k_rot,
            v_low,
            all_keys,
            all_values,
            log_totals,
            attended,
            att_low,
            first_sum,
            normed,
            y_low,
            gate_up,
            hidden,
            second_sum,
        ) = saved[layer_pos]
        w_mix = lax.all_gather(
            mixer_in[layer_pos].astype(jnp.bfloat16), ("dp", "dim"), axis=0, tiled=True
        )
        w_out = lax.all_gather(
            mixer_out[layer_pos].astype(jnp.bfloat16), ("dp", "dim"), axis=0, tiled=True
        )
        w_exp = lax.all_gather(
            expand[layer_pos].astype(jnp.bfloat16), ("dp", "dim"), axis=0, tiled=True
        )
        w_con = lax.all_gather(
            contract[layer_pos].astype(jnp.bfloat16), ("dp", "dim"), axis=0, tiled=True
        )
        w_norm = lax.all_gather(
            norm_params[layer_pos].astype(jnp.bfloat16), ("dp", "dim"), axis=1, tiled=True
        )
        norm_gains = w_norm.astype(jnp.float32)
        grad_second, grad_gain2, grad_bias2 = normalize_back(grad_stream, second_sum, norm_gains[2])
        grad_m_low = grad_second.astype(jnp.bfloat16)
        grad_con = inner_rows(hidden, grad_m_low)
        grad_hidden = inner_cols(grad_m_low, w_con)
        half = gate_up.shape[1] // 2
        gate_part = gate_up[:, 0:half]
        up_part = gate_up[:, half : 2 * half]
        sigmoid_gate = jax.nn.sigmoid(gate_part)
        activated = gate_part * sigmoid_gate
        grad_gate = grad_hidden * up_part * sigmoid_gate * (1.0 + gate_part * (1.0 - sigmoid_gate))
        grad_up = grad_hidden * activated
        grad_both = jnp.concatenate([grad_gate, grad_up], axis=1).astype(jnp.bfloat16)
        grad_exp = inner_rows(y_low, grad_both)
        grad_normed = grad_second + inner_cols(grad_both, w_exp)
        grad_first, grad_gain1, grad_bias1 = normalize_back(grad_normed, first_sum, norm_gains[0])
        grad_a_low = grad_first.astype(jnp.bfloat16)
        grad_out = inner_rows(att_low, grad_a_low)
        grad_attended = inner_cols(grad_a_low, w_out).astype(jnp.bfloat16)
        keys_back, values_back = (
            lax.all_gather(k_rot, "dim", axis=0, tiled=True),
            lax.all_gather(v_low, "dim", axis=0, tiled=True),
        )
        grad_query, grad_key_all, grad_value_all = attend_back(
            q_rot, keys_back, values_back, same_doc, grad_attended, log_totals
        )
        grad_kv = lax.psum_scatter(
            jnp.concatenate([grad_key_all, grad_value_all], axis=1).astype(jnp.bfloat16),
            "dim",
            scatter_dimension=0,
            tiled=True,
        ).astype(jnp.float32)
        grad_mixed = jnp.concatenate(
            [
                rotate_back(grad_query, cosines, sines),
                rotate_back(grad_kv[:, 0:model_width], cosines, sines),
                grad_kv[:, model_width : 2 * model_width],
            ],
            axis=1,
        ).astype(jnp.bfloat16)
        x_low = layer_input.astype(jnp.bfloat16)
        grad_mix = inner_rows(x_low, grad_mixed)
        grad_stream = grad_first + inner_cols(grad_mixed, w_mix)
        grad_norm = jnp.stack([grad_gain1, grad_bias1, grad_gain2, grad_bias2])
        grad_list[layer_pos] = (
            lax.psum_scatter(grad_mix, ("dp", "dim"), scatter_dimension=0, tiled=True),
            lax.psum_scatter(grad_out, ("dp", "dim"), scatter_dimension=0, tiled=True),
            lax.psum_scatter(grad_exp, ("dp", "dim"), scatter_dimension=0, tiled=True),
            lax.psum_scatter(grad_con, ("dp", "dim"), scatter_dimension=0, tiled=True),
            lax.psum_scatter(grad_norm, ("dp", "dim"), scatter_dimension=1, tiled=True),
        )
    total_rows = group_rows * lax.axis_size("dp")
    matrix_rate = 1.0 / math.sqrt(total_rows)
    norm_rate = 0.3 / math.sqrt(total_rows)
    grads = [jnp.stack([grad_list[0][kind]]) for kind in range(5)]
    weights = (mixer_in, mixer_out, expand, contract, norm_params)
    moments = (mixer_in_moment, mixer_out_moment, expand_moment, contract_moment, norm_moment)
    averages = (mixer_in_average, mixer_out_average, expand_average, contract_average, norm_average)
    rates = (matrix_rate, matrix_rate, matrix_rate, matrix_rate, norm_rate)
    results = [
        advance(weights[kind], moments[kind], averages[kind], grads[kind], rates[kind])
        for kind in range(5)
    ]
    return (
        embeddings,
        grad_stream,
        grads[0],
        grads[1],
        grads[2],
        grads[3],
        grads[4],
        results[0][0],
        results[1][0],
        results[2][0],
        results[3][0],
        results[4][0],
        results[0][1],
        results[1][1],
        results[2][1],
        results[3][1],
        results[4][1],
        results[0][2],
        results[1][2],
        results[2][2],
        results[3][2],
        results[4][2],
        results[0][3],
        results[1][3],
        results[2][3],
        results[3][3],
        results[4][3],
    )


def solution(mesh):
    placed = (
        P(("dp", "dim"), None),
        P("dp", None),
        P("dp"),
        P(None, "dim"),
        P(None, ("dp", "dim"), None),
        P(None, ("dp", "dim"), None),
        P(None, ("dp", "dim"), None),
        P(None, ("dp", "dim"), None),
        P(None, None, ("dp", "dim")),
        P(None, ("dp", "dim"), None),
        P(None, ("dp", "dim"), None),
        P(None, ("dp", "dim"), None),
        P(None, ("dp", "dim"), None),
        P(None, None, ("dp", "dim")),
        P(None, ("dp", "dim"), None),
        P(None, ("dp", "dim"), None),
        P(None, ("dp", "dim"), None),
        P(None, ("dp", "dim"), None),
        P(None, None, ("dp", "dim")),
    )
    return jax.shard_map(
        body,
        mesh=mesh,
        in_specs=placed,
        out_specs=(
            P("dp", "dim"),
            P(("dp", "dim"), None),
            P(None, ("dp", "dim"), None),
            P(None, ("dp", "dim"), None),
            P(None, ("dp", "dim"), None),
            P(None, ("dp", "dim"), None),
            P(None, None, ("dp", "dim")),
            P(None, ("dp", "dim"), None),
            P(None, ("dp", "dim"), None),
            P(None, ("dp", "dim"), None),
            P(None, ("dp", "dim"), None),
            P(None, None, ("dp", "dim")),
            P(None, ("dp", "dim"), None),
            P(None, ("dp", "dim"), None),
            P(None, ("dp", "dim"), None),
            P(None, ("dp", "dim"), None),
            P(None, None, ("dp", "dim")),
            P(None, ("dp", "dim"), None),
            P(None, ("dp", "dim"), None),
            P(None, ("dp", "dim"), None),
            P(None, ("dp", "dim"), None),
            P(None, None, ("dp", "dim")),
            P(None, ("dp", "dim"), None),
            P(None, ("dp", "dim"), None),
            P(None, ("dp", "dim"), None),
            P(None, ("dp", "dim"), None),
            P(None, None, ("dp", "dim")),
        ),
        check_vma=False,
    )
```

profile of v0, /device:TPU:0, one launch (start us, length us, event | category | flops | bytes accessed | tf_op | source)
XLA Modules:
  0.0 2074.2 jit_solution(18148415352444536729)
XLA Ops:
  12.8 61.5 %all-gather.16.cloned.1.call-done = bf16[1,768,2304]{2,1,0:T(8,128)(2,1)} async-done(((bf16[1,24,2304]{2,1,0:T(8,128)(2,1)}), bf16[1,768,2304]{2,1,0:T(8,128)(2,1)}) %all-gather.16.cloned.1.call-update) | async-done | bytes 3538960 | tf_op jit(solution)/shard_map/all_gather | solution.py:185
  122.6 40.7 %all-gather.2 = bf16[1,4,768]{1,0,2:T(2,128)(2,1)S(1)} all-gather(bf16[1,4,24]{1,0,2:T(2,128)(2,1)S(1)} %copy.154), channel_id=4, replica_groups=mesh['dp'=16,'dim'=2] {'dp','dim'}, dimensions={2}, use_global_device_ids=true | all-gather | bytes 6336 | tf_op jit(solution)/shard_map/all_gather | solution.py:191
  187.4 371.3 %while.30 = (s32[]{:T(128)}, bf16[12,1536,64]{1,2,0:T(8,128)(2,1)}, f32[12,1536]{1,0:T(8,128)}, s32[12]{0:T(128)S(1)}, bf16[1536,768]{1,0:T(8,128)(2,1)S(1)}, /*...) while((s32[]{:T(128)}, bf16[12,1536,64]{1,2,0:T(8,128)(2,1)}, ...), condition=%wide.region_7.8_spmd.clone.clone, body=%wide.region_4.7_spmd.clone.sunk.clone | while | flops 1250425344 | bytes 59078312 | solution.py:103
  567.4 24.3 %fusion.42 = f32[1536,6144]{1,0:T(8,128)} fusion(bf16[1,768,6144]{2,1,0:T(8,128)(2,1)} %all-gather.20.cloned.1.call-done, f32[1536,768]{0,1:T(8,128)} %copy-done.4, f32[768]{0:T(1024)S(1)} %copy-done.48, f32[768]{0:T(1024)S(1)} %copy-done.43, f32[1536]{0:T(1024)S(1)} %add_rsqrt_fusion.1, f32[1536]{0:T(1024)S(1)} %broadcast_multiply_fusion.5), kind=kOutput, calls=%fused_computation.52 | convolution fusion | flops 14501412864 | bytes 51922944 | tf_op jit(solution)/shard_map/dot_general | solution.py:20
  591.7 17.4 multiply_convert_fusion.3
  660.9 30.5 %multiply_convert_fusion.2 = (bf16[1536,3072]{1,0:T(8,128)(2,1)}, bf16[1536,3072]{1,0:T(8,128)(2,1)}) fusion(f32[1536,6144]{1,0:T(8,128)} %fusion.42, bf16[1,3072,768]{2,1,0:T(8,128)(2,1)} %all-gather.22.cloned.1.call-done, f32[1536,768]{0,1:T(8,128)} %subtract_multiply_fusion.1), kind=kOutput, calls=%fused_computation.44 | convolution fusion | flops 7310278656 | bytes 66060288 | tf_op jit(solution)/shard_map/dot_general | solution.py:34
  691.3 24.2 %multiply_reduce_fusion.2 = (f32[768]{0:T(1024)}, f32[1536]{0:T(1024)S(1)}, f32[1536]{0:T(1024)S(1)}, f32[768]{0:T(1024)}, f32[1536,768]{0,1:T(8,128)S(1)}) fusion(f32[1536,768]{0,1:T(8,128)} %copy-done.4, f32[1536]{0:T(1024)S(1)} %add_rsqrt_fusion.1, f32[1536]{0:T(1024)S(1)} %broadcast_multiply_fusion.5, f32[768]{0:T(1024)S(1)} %copy-done.43, ...), kind=kOutput, calls=%fused_computation.62 | convolution fusion | flops 14545054720 | bytes 42501120 | tf_op jit(solution)/shard_map/dot_general | solution.py:34
  721.5 727.4 %while.31 = (s32[]{:T(128)}, f32[12,1536,64]{1,2,0:T(8,128)}, bf16[12,3072,64]{1,2,0:T(8,128)(2,1)}, bf16[12,3072,64]{1,2,0:T(8,128)(2,1)}, s32[12]{0:T(128)S(1)...) while((s32[]{:T(128)}, f32[12,1536,64]{1,2,0:T(8,128)}, ...), condition=%wide.region_22.23_spmd.clone.clone, body=%wide.region_20.22_spmd.clone.sunk.clone | while | flops 3067378176 | bytes 204132176 | solution.py:127
  746.6 18.3 multiply_convert_fusion.6
  807.1 18.3 multiply_convert_fusion.6
  853.9 13.8 multiply_reduce_fusion.11
  867.8 18.3 multiply_convert_fusion.6
  914.6 13.8 multiply_reduce_fusion.11
  928.4 18.3 multiply_convert_fusion.6
  989.0 18.3 multiply_convert_fusion.6
  1049.6 18.3 multiply_convert_fusion.6
  1096.4 13.8 multiply_reduce_fusion.11
  1110.2 18.3 multiply_convert_fusion.6
  1157.0 13.8 multiply_reduce_fusion.11
  1170.8 18.3 multiply_convert_fusion.6
  1231.4 18.3 multiply_convert_fusion.6
  1292.0 18.3 multiply_convert_fusion.6
  1338.8 13.8 multiply_reduce_fusion.11
  1352.6 18.3 multiply_convert_fusion.6
  1399.4 13.8 multiply_reduce_fusion.11
  1413.2 18.3 multiply_convert_fusion.6
  1465.6 15.2 fusion.73
  1481.6 22.4 %fusion.39 = f32[768,6144]{1,0:T(8,128)} fusion(bf16[1536,3072]{1,0:T(8,128)(2,1)} %get-tuple-element.528, bf16[1536,3072]{1,0:T(8,128)(2,1)} %get-tuple-element.527, f32[1536,768]{0,1:T(8,128)} %copy-done.4, f32[768]{0:T(1024)S(1)} %copy-done.49, f32[768]{0:T(1024)S(1)} %copy-done.44, f32[1536]{0:T(1024)S(1)} %copy-done.40, f32[1536]{0:T(1024)S(1)} %copy-done.35), kind=kOutput, calls=%fused_computation.48 | convolution fusion | flops 14539161600 | bytes 42485760 | tf_op jit(solution)/shard_map/dot_general | solution.py:28
  1534.5 40.7 %all-reduce = f32[4,768]{1,0:T(4,128)S(1)} all-reduce(f32[4,768]{1,0:T(4,128)S(1)} %pad_maximum_fusion.13), channel_id=13, replica_groups=mesh['dp'=16,'dim'=2] {'dp','dim'}, use_global_device_ids=true, to_apply=%region_32.33.clone | all-reduce | flops 3072 | bytes 24576
  1586.5 138.7 %reduce-scatter.18.cloned.1.call-done = f32[96,768]{1,0:T(8,128)} async-done(((f32[3072,768]{1,0:T(8,128)}), f32[96,768]{1,0:T(8,128)}) %reduce-scatter.18.cloned.1.call-update) | async-done | bytes 294928 | tf_op jit(solution)/shard_map/reduce_scatter | solution.py:356
  1746.1 193.1 %reduce-scatter.16.cloned.1.call-done = f32[24,6144]{1,0:T(8,128)} async-done(((f32[768,6144]{1,0:T(8,128)}), f32[24,6144]{1,0:T(8,128)}) %reduce-scatter.16.cloned.1.call-update) | async-done | bytes 589840 | tf_op jit(solution)/shard_map/reduce_scatter | solution.py:355
  1942.3 122.2 %reduce-scatter.22.cloned.1.call-done = f32[24,2304]{1,0:T(8,128)} async-done(((f32[768,2304]{1,0:T(8,128)}), f32[24,2304]{1,0:T(8,128)}) %reduce-scatter.22.cloned.1.call-update) | async-done | bytes 221200 | tf_op jit(solution)/shard_map/reduce_scatter | solution.py:353
  (561 shorter events, 1009.1 us)
Async XLA Ops:
  7.2 167.4 %copy-start = (bf16[256,384]{1,0:T(8,128)(2,1)S(1)}, bf16[256,384]{1,0:T(8,128)(2,1)}, u32[]{:S(2)}) copy-start(bf16[256,384]{1,0:T(8,128)(2,1)} %param.27) | copy-start | bytes 589828
  7.2 67.1 %all-gather.16.cloned.1.call-start = ((), (), s32[]{:S(2)}) async-start(), calls=%async_computation.12 | async-start | bytes 3649536 | tf_op jit(solution)/shard_map/all_gather | solution.py:185
  8.9 171.9 %all-gather.12.cloned.1.call-start = ((), (), s32[]{:S(2)}) async-start(), calls=%async_computation.6 | async-start | bytes 7077888 | tf_op jit(solution)/shard_map/all_gather | solution.py:202
  12.7 90.2 %copy-start.15 = (f32[1536,32]{0,1:T(8,128)}, f32[1536,32]{0,1:T(8,128)S(1)}, u32[]{:S(2)}) copy-start(f32[1536,32]{0,1:T(8,128)S(1)} %get-tuple-element.545) | copy-start | bytes 589828
  12.8 90.2 %copy-start.17 = (f32[1536,32]{0,1:T(8,128)}, f32[1536,32]{0,1:T(8,128)S(1)}, u32[]{:S(2)}) copy-start(f32[1536,32]{0,1:T(8,128)S(1)} %get-tuple-element.546) | copy-start | bytes 589828
  109.1 78.3 %all-gather.14.cloned.1.call-start = ((), (), s32[]{:S(2)}) async-start(), calls=%async_computation.7 | async-start | bytes 7077888 | tf_op jit(solution)/shard_map/all_gather | solution.py:203
  113.4 445.3 %all-gather.18.cloned.1.call-start = ((), (), s32[]{:S(2)}) async-start(), calls=%async_computation.13 | async-start | bytes 1216512 | tf_op jit(solution)/shard_map/all_gather | solution.py:186
  114.1 453.3 %all-gather.20.cloned.1.call-start = ((), (), s32[]{:S(2)}) async-start(), calls=%async_computation.14 | async-start | bytes 9732096 | tf_op jit(solution)/shard_map/all_gather | solution.py:189
  114.9 494.2 %all-gather.22.cloned.1.call-start = ((), (), s32[]{:S(2)}) async-start(), calls=%async_computation.15 | async-start | bytes 4866048 | tf_op jit(solution)/shard_map/all_gather | solution.py:190
  115.7 516.9 %reduce-scatter.20.cloned.1.call-start = ((), (), s32[]{:S(2)}) async-start(), calls=%async_computation.16 | async-start | bytes 589824
  115.9 58.7 %copy-start.61 = (s32[2]{0:T(128)S(1)}, s32[2]{0:T(128)}, u32[]{:S(2)}) copy-start(s32[2]{0:T(128)} %param.26) | copy-start | bytes 28
  115.9 59.3 %copy-start.64 = (s32[5]{0:T(128)S(1)}, s32[5]{0:T(128)}, u32[]{:S(2)}) copy-start(s32[5]{0:T(128)} %constant.106.clone) | copy-start | bytes 64
  564.7 150.8 %copy-start.34 = (f32[1536]{0:T(1024)}, f32[1536]{0:T(1024)S(1)}, u32[]{:S(2)}) copy-start(f32[1536]{0:T(1024)S(1)} %broadcast_multiply_fusion.5) | copy-start | bytes 18436
  567.4 148.2 %copy-start.39 = (f32[1536]{0:T(1024)}, f32[1536]{0:T(1024)S(1)}, u32[]{:S(2)}) copy-start(f32[1536]{0:T(1024)S(1)} %add_rsqrt_fusion.1) | copy-start | bytes 18436
  628.1 876.2 %reduce-scatter.12.cloned.1.call-start = ((), (), s32[]{:S(2)}) async-start(), calls=%async_computation.8 | async-start | bytes 14155776 | tf_op jit(solution)/shard_map/reduce_scatter | solution.py:334
  1458.1 126.2 %reduce-scatter.14.cloned.1.call-start = ((), (), s32[]{:S(2)}) async-start(), calls=%async_computation.9 | async-start | bytes 2433024 | tf_op jit(solution)/shard_map/reduce_scatter | solution.py:354
  1465.5 259.6 %reduce-scatter.18.cloned.1.call-start = ((), (), s32[]{:S(2)}) async-start(), calls=%async_computation.11 | async-start | bytes 9732096 | tf_op jit(solution)/shard_map/reduce_scatter | solution.py:356
  1480.9 458.3 %reduce-scatter.16.cloned.1.call-start = ((), (), s32[]{:S(2)}) async-start(), calls=%async_computation.10 | async-start | bytes 19464192 | tf_op jit(solution)/shard_map/reduce_scatter | solution.py:355
  1504.0 560.5 %reduce-scatter.22.cloned.1.call-start = ((), (), s32[]{:S(2)}) async-start(), calls=%async_computation.17 | async-start | bytes 7299072 | tf_op jit(solution)/shard_map/reduce_scatter | solution.py:353
  1533.8 52.0 %copy-start.37 = (f32[1,24,768]{2,1,0:T(8,128)S(1)}, f32[1,24,768]{2,1,0:T(8,128)}, u32[]{:S(2)}) copy-start(f32[1,24,768]{2,1,0:T(8,128)} %param.39) | copy-start | bytes 221188
  1533.9 191.3 %copy-start.23 = (f32[1,96,768]{2,1,0:T(8,128)S(1)}, f32[1,96,768]{2,1,0:T(8,128)}, u32[]{:S(2)}) copy-start(f32[1,96,768]{2,1,0:T(8,128)} %param.31) | copy-start | bytes 884740
  1533.9 191.3 %copy-start.28 = (f32[1,96,768]{2,1,0:T(8,128)S(1)}, f32[1,96,768]{2,1,0:T(8,128)}, u32[]{:S(2)}) copy-start(f32[1,96,768]{2,1,0:T(8,128)} %param.36) | copy-start | bytes 884740
  1576.0 163.6 %copy-start.45 = (f32[1,4,24]{2,1,0:T(4,128)}, f32[1,4,24]{2,1,0:T(4,128)S(1)}, u32[]{:S(2)}) copy-start(f32[1,4,24]{2,1,0:T(4,128)S(1)} %get-tuple-element.508) | copy-start | bytes 1156
  1585.8 153.7 %copy-start.29 = (f32[1,24,768]{2,1,0:T(8,128)}, f32[1,24,768]{2,1,0:T(8,128)S(1)}, u32[]{:S(2)}) copy-start(f32[1,24,768]{2,1,0:T(8,128)S(1)} %get-tuple-element.518) | copy-start | bytes 221188
  1739.5 199.7 %copy-start.10 = (f32[1,24,6144]{2,1,0:T(8,128)S(1)}, f32[1,24,6144]{2,1,0:T(8,128)}, u32[]{:S(2)}) copy-start(f32[1,24,6144]{2,1,0:T(8,128)} %param.30) | copy-start | bytes 1769476
  1739.5 199.7 %copy-start.26 = (f32[1,24,6144]{2,1,0:T(8,128)S(1)}, f32[1,24,6144]{2,1,0:T(8,128)}, u32[]{:S(2)}) copy-start(f32[1,24,6144]{2,1,0:T(8,128)} %param.35) | copy-start | bytes 1769476
  1739.5 201.8 %copy-start.27 = (f32[1,24,6144]{2,1,0:T(8,128)S(1)}, f32[1,24,6144]{2,1,0:T(8,128)}, u32[]{:S(2)}) copy-start(f32[1,24,6144]{2,1,0:T(8,128)} %param.40) | copy-start | bytes 1769476
  1739.6 327.4 %copy-start.1 = (bf16[256,384]{1,0:T(8,128)(2,1)S(1)}, bf16[256,384]{1,0:T(8,128)(2,1)}, u32[]{:S(2)}) copy-start(bf16[256,384]{1,0:T(8,128)(2,1)} %param.27) | copy-start | bytes 589828
  1746.1 318.3 %copy-start.24 = (f32[1,24,2304]{2,1,0:T(8,128)S(1)}, f32[1,24,2304]{2,1,0:T(8,128)}, u32[]{:S(2)}) copy-start(f32[1,24,2304]{2,1,0:T(8,128)} %param.28) | copy-start | bytes 663556
  1746.1 318.3 %copy-start.32 = (f32[1,24,2304]{2,1,0:T(8,128)S(1)}, f32[1,24,2304]{2,1,0:T(8,128)}, u32[]{:S(2)}) copy-start(f32[1,24,2304]{2,1,0:T(8,128)} %param.33) | copy-start | bytes 663556
  1746.1 320.1 %copy-start.33 = (f32[1,24,2304]{2,1,0:T(8,128)S(1)}, f32[1,24,2304]{2,1,0:T(8,128)}, u32[]{:S(2)}) copy-start(f32[1,24,2304]{2,1,0:T(8,128)} %param.38) | copy-start | bytes 663556
  1941.4 125.6 %copy-start.8 = (f32[1,24,6144]{2,1,0:T(8,128)}, f32[1,24,6144]{2,1,0:T(8,128)S(1)}, u32[]{:S(2)}) copy-start(f32[1,24,6144]{2,1,0:T(8,128)S(1)} %get-tuple-element.515) | copy-start | bytes 1769476
  (110 other events, 2185.8 us)
Sparse Core Ops, SparseCore 0:
  11.5 62.7 all-gather.15
  109.2 13.2 all-gather.11
  124.0 15.6 all-gather.13
  143.0 55.2 all-gather.17
  201.7 81.0 all-gather.19
  286.1 62.2 all-gather.21
  628.3 4.2 reduce-scatter.19
  1458.3 18.9 reduce-scatter.11
  1484.0 100.2 reduce-scatter.13
  1590.6 134.5 reduce-scatter.17
  1733.3 205.8 reduce-scatter.15
  1946.3 118.1 reduce-scatter.21
where the time goes:
time: 2090 us; the launch traced here: 2070 us
  matrix products  899 us (43%)
  waiting for transfers between devices  528 us (25%)
  other arithmetic  402 us (19%)
  local copies, waits for them, and re-layouts  127 us (6%)
  blocking collectives  85.7 us (4%)
    dot_general x40, matrix products, inner_cols(): lax.dot_general(left_op, right_op, (((1,), (1,)), ((), ())), preferred_el...  459 us
    dot_general x29, matrix products, matmul(): return jnp.dot(left_op, right_op, preferred_element_type=jnp.float32)  257 us
    convert_element_type x12, other arithmetic, one_head(): grad_scores = (attn_probs * (grad_probs - row_dot)).astype(jnp.bfloat16)  219 us
    reduce_scatter x1, waiting for transfers between devices, body(): lax.psum_scatter(grad_exp, ('dp', 'dim'), scatter_dimension=0, tiled=True)  193 us
    dot_general x28, matrix products, inner_rows(): lax.dot_general(left_op, right_op, (((0,), (0,)), ((), ())), preferred_el...  171 us
    reduce_scatter x1, waiting for transfers between devices, body(): lax.psum_scatter(grad_con, ('dp', 'dim'), scatter_dimension=0, tiled=True)  139 us
    reduce_scatter x1, waiting for transfers between devices, body(): lax.psum_scatter(grad_mix, ('dp', 'dim'), scatter_dimension=0, tiled=True)  122 us
    reduce_sum x12, other arithmetic, one_head(): row_total = jnp.sum(exponent, axis=1, keepdims=True)  108 us
  transfers between devices with their start and end apart: 12, of which 6 were waited for; matrix products, arithmetic and copies ran while one was open for 26% of the time, Pallas kernels for 0%

commit v1 on v0

--- a/solution.py
+++ b/solution.py
@@ -3,6 +3,8 @@
 import jax
 import jax.numpy as jnp
 from jax import lax
+from jax.experimental import pallas as pl
+from jax.experimental.pallas import tpu as pltpu
 from jax.sharding import PartitionSpec as P
 
 HEAD = 64
@@ -135,7 +137,7 @@
     return (weight_next, moment_next, average_next, weight_next.astype(jnp.bfloat16))
 
 
-def body(
+def body_general(
     tokens,
     doc_lengths,
     pair_index,
@@ -399,6 +401,409 @@
     )
 
 
+NEG=-1e30
+BQ=256
+BK=512
+F32=jnp.float32
+BF=jnp.bfloat16
+
+def nt(a,b): return lax.dot_general(a,b,(((1,),(1,)),((),())),preferred_element_type=F32)
+def nn(a,b): return jnp.dot(a,b,preferred_element_type=F32)
+
+def fill_masks(e0,e1,kaug,q0,q1,rows,pad):
+    r=lax.broadcasted_iota(jnp.int32,(rows+pad,128),0)
+    l=lax.broadcasted_iota(jnp.int32,(rows+pad,128),1)
+    seg=(r>=e0).astype(jnp.int32)+(r>=e1).astype(jnp.int32)
+    kaug[:,128:256]=jnp.where((l<3)&(l!=seg),NEG,0.0).astype(BF)
+    qm=jnp.where(l==seg,1.0,0.0).astype(BF)[0:rows]
+    q0[:,128:256]=qm
+    q1[:,128:256]=qm
+
+def key_range(i,e0,e1):
+    first=i*BQ
+    last=jnp.minimum(first+BQ,e1)-1
+    lo=jnp.where(first>=e0,e0,0)
+    hi=jnp.where(last>=e0,e1,e0)
+    base=(lo//128)*128
+    return pl.multiple_of(base,128),(hi-base+BK-1)//BK
+
+def fwd_kernel(ctl,qo,ko,vo,qr,kr,vr,oo,ox,lse,kaug,q0,q1,vt):
+    rows=kaug.shape[0]-BK
+    half=rows//2
+    pos,e0,e1=ctl[0],ctl[1],ctl[2]
+    p=pl.program_id(0)
+    @pl.when(p==0)
+    def _():
+        fill_masks(e0,e1,kaug,q0,q1,rows,BK)
+        kaug[rows:,0:128]=jnp.zeros((BK,128),BF)
+        vt[:,:]=jnp.where(lax.broadcasted_iota(jnp.int32,vt.shape,0)%80>=64,1.0,0.0).astype(BF)
+    lane=lax.broadcasted_iota(jnp.int32,(half,128),1)
+    for own,(q,k,v) in ((True,(qo,ko,vo)),(False,(qr,kr,vr))):
+        at=pl.multiple_of((pos if own else 1-pos)*half,half)
+        scaled=q[...]*jnp.asarray(0.125,BF)
+        zero=jnp.zeros_like(scaled)
+        q0[pl.ds(at,half),0:128]=jnp.where(lane<64,scaled,zero)
+        q1[pl.ds(at,half),0:128]=jnp.where(lane<64,zero,scaled)
+        kaug[pl.ds(at,half),0:128]=k[...]
+        turned=v[...].T
+        vt[0:64,pl.ds(at,half)]=turned[0:64]
+        vt[80:144,pl.ds(at,half)]=turned[64:128]
+    def qblock(i,_):
+        r0=pl.multiple_of(i*BQ,BQ)
+        base,count=key_range(i,e0,e1)
+        qs=(q0[pl.ds(r0,BQ),:],q1[pl.ds(r0,BQ),:])
+        def step(j,carry):
+            k0=pl.multiple_of(base+j*BK,128)
+            kb=kaug[pl.ds(k0,BK),:]
+            out=[]
+            for h in range(2):
+                m,acc=carry[h]
+                st=nt(kb,qs[h])
+                mn=jnp.maximum(m,jnp.max(st,axis=0,keepdims=True))
+                pt=jnp.exp(st-mn).astype(BF)
+                acc=acc*jnp.exp(m-mn)+nn(vt[80*h:80*h+80,pl.ds(k0,BK)],pt)
+                out.append((mn,acc))
+            return tuple(out)
+        init=(jnp.full((1,BQ),-jnp.inf,F32),jnp.zeros((80,BQ),F32))
+        res=lax.fori_loop(0,count,step,(init,init))
+        outs=[]
+        for h in range(2):
+            m,acc=res[h]
+            l=acc[64:65]
+            outs.append(acc[0:64]/l)
+            lse[0,h:h+1,pl.ds(r0,BQ)]=m+jnp.log(l)
+        ob=jnp.concatenate(outs,axis=0).T.astype(BF)
+        put(i,ob)
+        return 0
+    def put(i,ob):
+        local=i*BQ-pos*half
+        @pl.when((local>=0)&(local<half))
+        def _(): oo[pl.ds(pl.multiple_of(local,BQ),BQ),:]=ob
+        @pl.when((local<0)|(local>=half))
+        def _(): ox[pl.ds(pl.multiple_of(i*BQ-(1-pos)*half,BQ),BQ),:]=ob
+    used=(e1+BQ-1)//BQ
+    lax.fori_loop(0,used,qblock,0)
+    def blank(i,_):
+        r0=pl.multiple_of(i*BQ,BQ)
+        lse[0,:,pl.ds(r0,BQ)]=jnp.zeros((8,BQ),F32)
+        put(i,jnp.zeros((BQ,128),BF))
+        return 0
+    lax.fori_loop(used,rows//BQ,blank,0)
+
+def attend_fwd(ctl,own,recv):
+    half,width=own.shape
+    pairs=width//384
+    rows=2*half
+    sp=[pl.BlockSpec((half,128),(lambda p,c,s=s:(0,s*pairs+p))) for s in range(3)]
+    outw=pairs*128
+    return pl.pallas_call(fwd_kernel,
+        grid_spec=pltpu.PrefetchScalarGridSpec(num_scalar_prefetch=1,grid=(pairs,),
+          in_specs=sp+sp,
+          out_specs=[pl.BlockSpec((half,128),lambda p,c:(0,p))]*2+[pl.BlockSpec((1,8,rows),lambda p,c:(p,0,0))],
+          scratch_shapes=[pltpu.VMEM((rows+BK,256),BF),pltpu.VMEM((rows,256),BF),pltpu.VMEM((rows,256),BF),pltpu.VMEM((160,rows+BK),BF)]),
+        out_shape=[jax.ShapeDtypeStruct((half,outw),BF)]*2+[jax.ShapeDtypeStruct((pairs,8,rows),F32)],
+        compiler_params=pltpu.CompilerParams(vmem_limit_bytes=56<<20,dimension_semantics=("arbitrary",)),
+        cost_estimate=pl.CostEstimate(flops=4*rows*rows*64*2*pairs//2,bytes_accessed=10*half*width,transcendentals=rows*rows*pairs),
+        name="attend_fwd",
+    )(ctl,own,own,own,recv,recv,recv)
+
+def bwd_kernel(ctl,qo,ko,vo,qr,kr,vr,do_o,do_r,oo,ox,lse,cos,sin,go,gx,kaug,q0,q1,vs,d0,d1,kt,delta,dk,dv):
+    rows=kaug.shape[0]-BK
+    half=rows//2
+    pos,e0,e1=ctl[0],ctl[1],ctl[2]
+    p=pl.program_id(0)
+    @pl.when(p==0)
+    def _():
+        fill_masks(e0,e1,kaug,q0,q1,rows,BK)
+        kaug[rows:,0:128]=jnp.zeros((BK,128),BF)
+        vs[rows:,:]=jnp.zeros((BK,128),BF)
+        kt[:,rows:]=jnp.zeros((128,BK),BF)
+    lane=lax.broadcasted_iota(jnp.int32,(half,128),1)
+    pick_r=lax.broadcasted_iota(jnp.int32,(16,128),0)
+    pick_l=lax.broadcasted_iota(jnp.int32,(16,128),1)
+    pick=jnp.where(pick_l//64==pick_r,1.0,0.0).astype(BF)
+    for own,(q,k,v,d,o) in ((True,(qo,ko,vo,do_o,oo)),(False,(qr,kr,vr,do_r,ox))):
+        at=pl.multiple_of((pos if own else 1-pos)*half,half)
+        scaled=q[...]*jnp.asarray(0.125,BF)
+        zero=jnp.zeros_like(scaled)
+        q0[pl.ds(at,half),0:128]=jnp.where(lane<64,scaled,zero)
+        q1[pl.ds(at,half),0:128]=jnp.where(lane<64,zero,scaled)
+        kb=k[...]
+        kaug[pl.ds(at,half),0:128]=kb
+        kt[:,pl.ds(at,half)]=kb.T
+        vs[pl.ds(at,half),:]=v[...]
+        db=d[...]
+        d0[pl.ds(at,half),:]=jnp.where(lane<64,db,zero)
+        d1[pl.ds(at,half),:]=jnp.where(lane<64,zero,db)
+        prod=db.astype(F32)*o[...].astype(F32)
+        hi=prod.astype(BF)
+        lo=(prod-hi.astype(F32)).astype(BF)
+        delta[:,pl.ds(at,half)]=nt(pick,hi)+nt(pick,lo)
+    dk[...]=jnp.zeros_like(dk)
+    dv[...]=jnp.zeros_like(dv)
+    def spread(i,col,val):
+        local=i*BQ-pos*half
+        @pl.when((local>=0)&(local<half))
+        def _(): go[pl.ds(pl.multiple_of(local,BQ),BQ),col*128:(col+1)*128] = val
+        @pl.when((local<0)|(local>=half))
+        def _(): gx[pl.ds(pl.multiple_of(i*BQ-(1-pos)*half,BQ),BQ),col*128:(col+1)*128] = val
+    def unturn(x,r0):
+        ln=lax.broadcasted_iota(jnp.int32,x.shape,1)
+        swapped=jnp.where((ln%64)<32,pltpu.roll(x,96,1),pltpu.roll(x,32,1))
+        return x*cos[pl.ds(r0,BQ),:]-swapped*sin[pl.ds(r0,BQ),:]
+    def qblock(i,_):
+        r0=pl.multiple_of(i*BQ,BQ)
+        base,count=key_range(i,e0,e1)
+        qs=(q0[pl.ds(r0,BQ),:],q1[pl.ds(r0,BQ),:])
+        ds_=(d0[pl.ds(r0,BQ),:],d1[pl.ds(r0,BQ),:])
+        ls=[lse[0,h:h+1,pl.ds(r0,BQ)] for h in range(2)]
+        de=[delta[h:h+1,pl.ds(r0,BQ)] for h in range(2)]
+        def step(j,carry):
+            k0=pl.multiple_of(base+j*BK,128)
+            kb=kaug[pl.ds(k0,BK),:]
+            vb=vs[pl.ds(k0,BK),:]
+            out=[]
+            dva=dv[pl.ds(k0,BK),:]
+            dka=dk[pl.ds(k0,BK),:]
+            for h in range(2):
+                st=nt(kb,qs[h])
+                pt=jnp.exp(st-ls[h])
+                dpt=nt(vb,ds_[h])
+                dst=(pt*(dpt-de[h])).astype(BF)
+                dva=dva+nn(pt.astype(BF),ds_[h])
+                dka=dka+nn(dst,qs[h][:,0:128])
+                out.append(carry[h]+nn(kt[64*h:64*h+64,pl.ds(k0,BK)],dst))
+            dv[pl.ds(k0,BK),:]=dva
+            dk[pl.ds(k0,BK),:]=dka
+            return tuple(out)
+        init=jnp.zeros((64,BQ),F32)
+        res=lax.fori_loop(0,count,step,(init,init))
+        dq=jnp.concatenate(res,axis=0).T*0.125
+        spread(i,0,unturn(dq,r0).astype(BF))
+        return 0
+    used=(e1+BQ-1)//BQ
+    lax.fori_loop(0,used,qblock,0)
+    def blank(i,_):
+        spread(i,0,jnp.zeros((BQ,128),BF))
+        return 0
+    lax.fori_loop(used,rows//BQ,blank,0)
+    def last(i,_):
+        r0=pl.multiple_of(i*BQ,BQ)
+        spread(i,1,unturn(dk[pl.ds(r0,BQ),:],r0).astype(BF))
+        spread(i,2,dv[pl.ds(r0,BQ),:].astype(BF))
+        return 0
+    lax.fori_loop(0,rows//BQ,last,0)
+
+def attend_bwd(ctl,own,recv,d_own,d_recv,o_own,o_oth,lse,cos,sin):
+    half,width=own.shape
+    pairs=width//384
+    rows=2*half
+    sp=[pl.BlockSpec((half,128),(lambda p,c,s=s:(0,s*pairs+p))) for s in range(3)]
+    one=pl.BlockSpec((half,128),lambda p,c:(0,p))
+    full=pl.BlockSpec((rows,128),lambda p,c:(0,0))
+    return pl.pallas_call(bwd_kernel,
+        grid_spec=pltpu.PrefetchScalarGridSpec(num_scalar_prefetch=1,grid=(pairs,),
+          in_specs=sp+sp+[one]*4+[pl.BlockSpec((1,8,rows),lambda p,c:(p,0,0)),full,full],
+          out_specs=[pl.BlockSpec((half,384),lambda p,c:(0,p))]*2,
+          scratch_shapes=[pltpu.VMEM((rows+BK,256),BF),pltpu.VMEM((rows,256),BF),pltpu.VMEM((rows,256),BF),
+             pltpu.VMEM((rows+BK,128),BF),pltpu.VMEM((rows,128),BF),pltpu.VMEM((rows,128),BF),
+             pltpu.VMEM((128,rows+BK),BF),pltpu.VMEM((16,rows),F32),pltpu.VMEM((rows+BK,128),F32),pltpu.VMEM((rows+BK,128),F32)]),
+        out_shape=[jax.ShapeDtypeStruct((half,width),BF)]*2,
+        compiler_params=pltpu.CompilerParams(vmem_limit_bytes=56<<20,dimension_semantics=("arbitrary",)),
+        cost_estimate=pl.CostEstimate(flops=10*rows*rows*64*2*pairs//2,bytes_accessed=20*half*width,transcendentals=rows*rows*pairs),
+        name="attend_bwd",
+    )(ctl,own,own,own,recv,recv,recv,d_own,d_recv,o_own,o_oth,lse,cos,sin)
+
+def mix_kernel(ctl,x,w,cos,sin,own,oth):
+    pos=ctl[0]
+    width=x.shape[1]
+    share=width//2
+    xb=x[...]
+    c=cos[...]
+    s=sin[...]
+    lane=lax.broadcasted_iota(jnp.int32,c.shape,1)
+    first=(lane%64)<32
+    for out,side in ((own,pos),(oth,1-pos)):
+        for part in range(3):
+            cols=pl.ds(pl.multiple_of(part*width+side*share,128),share)
+            y=nn(xb,w[:,cols])
+            for t in range(share//128):
+                z=y[:,t*128:(t+1)*128]
+                if part<2:
+                    swapped=jnp.where(first,pltpu.roll(z,96,1),pltpu.roll(z,32,1))
+                    z=z*c+swapped*s
+                out[:,part*share+t*128:part*share+(t+1)*128]=z.astype(BF)
+
+def mix(ctl,x,w,cos,sin):
+    rows,width=x.shape
+    cols=w.shape[1]
+    block=256
+    row=lambda n: pl.BlockSpec((block,n),lambda i,c:(i,0))
+    return pl.pallas_call(mix_kernel,
+        grid_spec=pltpu.PrefetchScalarGridSpec(num_scalar_prefetch=1,grid=(rows//block,),
+          in_specs=[row(width),pl.BlockSpec((width,cols),lambda i,c:(0,0)),row(128),row(128)],
+          out_specs=[row(cols//2)]*2),
+        out_shape=[jax.ShapeDtypeStruct((rows,cols//2),BF)]*2,
+        compiler_params=pltpu.CompilerParams(vmem_limit_bytes=40<<20,dimension_semantics=("arbitrary",)),
+        cost_estimate=pl.CostEstimate(flops=2*rows*width*cols,bytes_accessed=2*(rows*width+width*cols+rows*cols),transcendentals=0),
+        name="mix",
+    )(ctl,x,w,cos,sin)
+
+def fold_rows(x,per):
+    rows,cols=x.shape
+    return x.reshape(per,rows//per,cols).transpose(1,0,2).reshape(rows//per,per*cols)
+
+def unfold_rows(x,per,share):
+    count=x.shape[0]//share
+    cols=x.shape[1]//per
+    return x.reshape(count,share,per,cols).transpose(0,2,1,3).reshape(count*per*share,cols)
+
+def swap_cores(x):
+    return lax.ppermute(x,"dim",[(0,1),(1,0)])
+
+def join(pos,own,recv,axis=1):
+    return jnp.where(pos==0,jnp.concatenate([own,recv],axis),jnp.concatenate([recv,own],axis))
+
+def join_parts(pos,own,recv):
+    share=own.shape[1]//3
+    pieces=[]
+    for s in range(3):
+        pieces.append(own[:,s*share:(s+1)*share])
+        pieces.append(recv[:,s*share:(s+1)*share])
+    flip=[pieces[i^1] for i in range(6)]
+    return jnp.where(pos==0,jnp.concatenate(pieces,1),jnp.concatenate(flip,1))
+
+def body(tokens,doc_lengths,pair_index,target_bank,mixer_in,mixer_out,expand,contract,norm_params,*rest):
+    slices=lax.axis_size("dim")
+    if slices!=2 or doc_lengths.shape[1]!=2:
+        return body_general(tokens,doc_lengths,pair_index,target_bank,mixer_in,mixer_out,expand,contract,norm_params,*rest)
+    (mixer_in_moment,mixer_out_moment,expand_moment,contract_moment,norm_moment,
+     mixer_in_average,mixer_out_average,expand_average,contract_average,norm_average)=rest
+    local_rows,model_width=tokens.shape
+    group_rows=local_rows*slices
+    pos=lax.axis_index("dim")
+    doc_count=2
+    gather=lambda w,axis=0: lax.all_gather(w[0].astype(BF),("dp","dim"),axis=axis,tiled=True)
+    w_mix=gather(mixer_in)
+    share_rows=mixer_out.shape[1]
+    per=contract.shape[1]//share_rows
+    count=model_width//share_rows
+    con_cols=fold_rows(contract[0],per)
+    norm_cols=jnp.pad(norm_params[0],((0,share_rows-4),(0,128-share_rows)))
+    bundle=jnp.concatenate([mixer_out[0],expand[0],con_cols,norm_cols],1).astype(BF)
+    bundle=lax.all_gather(bundle,("dp","dim"),axis=0,tiled=True)
+    at1=model_width
+    at2=at1+expand.shape[2]
+    at3=at2+per*model_width
+    w_out=bundle[:,0:at1]
+    w_exp=bundle[:,at1:at2]
+    w_con=unfold_rows(bundle[:,at2:at3],per,share_rows)
+    w_norm=bundle[:,at3:].reshape(count,share_rows,128)[:,0:4,0:share_rows].transpose(1,0,2).reshape(4,model_width)
+    lengths=doc_lengths[0]
+    e0=lengths[0]
+    e1=lengths[0]+lengths[1]
+    ctl=jnp.stack([pos.astype(jnp.int32),e0,e1])
+    ids=jnp.arange(group_rows,dtype=jnp.int32)
+    seg=(ids>=e0).astype(jnp.int32)+(ids>=e1).astype(jnp.int32)
+    begin=jnp.where(seg==0,0,jnp.where(seg==1,e0,e1))
+    lane=jnp.arange(128,dtype=jnp.int32)
+    frequency=jnp.power(1000.0,-(2*(lane%32)).astype(F32)/HEAD)
+    angles=(ids-begin).astype(F32)[:,None]*frequency[None,:]
+    cos=jnp.cos(angles)
+    sin=jnp.sin(angles)*jnp.where((lane%64)<32,-1.0,1.0)[None,:]
+    cos_own=lax.dynamic_slice_in_dim(cos,pos*local_rows,local_rows,0)
+    sin_own=lax.dynamic_slice_in_dim(sin,pos*local_rows,local_rows,0)
+    seg_rows=lax.dynamic_slice_in_dim(seg,pos*local_rows,local_rows,0)
+    stream=tokens.astype(F32)
+    own,oth=mix(ctl,tokens,w_mix,cos_own,sin_own)
+    recv=swap_cores(oth)
+    o_own,o_oth,lse=attend_fwd(ctl,own,recv)
+    att_low=join(pos,o_own,swap_cores(o_oth))
+    norm_gains=w_norm.astype(F32)
+    first_sum=stream+matmul(att_low,w_out)
+    normed=normalize(first_sum,norm_gains[0],norm_gains[1])
+    y_low=normed.astype(BF)
+    gate_up=matmul(y_low,w_exp)
+    half=gate_up.shape[1]//2
+    hidden=(jax.nn.silu(gate_up[:,0:half])*gate_up[:,half:2*half]).astype(BF)
+    second_sum=normed+matmul(hidden,w_con)
+    final=normalize(second_sum,norm_gains[2],norm_gains[3])
+    member=(seg_rows[None,:]==jnp.arange(doc_count,dtype=jnp.int32)[:,None]).astype(F32)
+    partial_value=matmul_exact(member,final)
+    pooled=lax.psum_scatter(partial_value,"dim",scatter_dimension=1,tiled=True)
+    length_f=lengths.astype(F32)
+    embeddings=pooled/length_f[:,None]
+    share=embeddings.shape[1]
+    pick=(pair_index[:,None]==jnp.arange(target_bank.shape[0],dtype=jnp.int32)[None,:]).astype(BF)
+    targets=matmul(pick,target_bank)
+    feature_ids=pos*share+jnp.arange(share,dtype=jnp.int32)
+    cuts=jnp.array([model_width//12,model_width//6,model_width//3,2*model_width//3,model_width],dtype=jnp.int32)
+    masks=(feature_ids[None,:]<cuts[:,None]).astype(F32)
+    cross=matmul_exact(embeddings*targets,masks.T)
+    own_sq=matmul_exact(embeddings*embeddings,masks.T)
+    other=matmul_exact(targets*targets,masks.T)
+    cross,own_sq,other=lax.psum((cross,own_sq,other),"dim")
+    own_root=lax.rsqrt(own_sq+COSINE_EPSILON)
+    other_root=lax.rsqrt(other+COSINE_EPSILON)
+    cosine=cross*own_root*other_root
+    coef_target=-length_f[:,None]*own_root*other_root
+    coef_self=length_f[:,None]*cosine*own_root*own_root
+    grad_emb=matmul_exact(coef_target,masks)*targets+matmul_exact(coef_self,masks)*embeddings
+    grad_full=lax.all_gather(grad_emb,"dim",axis=1,tiled=True)
+    spread_rows=member/length_f[:,None]
+    grad_stream=lax.dot_general(spread_rows,grad_full,(((0,),(0,)),((),())),precision=PRECISE,preferred_element_type=F32)
+    grad_second,grad_gain2,grad_bias2=normalize_back(grad_stream,second_sum,norm_gains[2])
+    grad_m_low=grad_second.astype(BF)
+    grad_con=inner_rows(hidden,grad_m_low)
+    grad_hidden=inner_cols(grad_m_low,w_con)
+    gate_part=gate_up[:,0:half]
+    up_part=gate_up[:,half:2*half]
+    sigmoid_gate=jax.nn.sigmoid(gate_part)
+    activated=gate_part*sigmoid_gate
+    grad_gate=grad_hidden*up_part*sigmoid_gate*(1.0+gate_part*(1.0-sigmoid_gate))
+    grad_up=grad_hidden*activated
+    grad_both=jnp.concatenate([grad_gate,grad_up],axis=1).astype(BF)
+    grad_exp=inner_rows(y_low,grad_both)
+    grad_normed=grad_second+inner_cols(grad_both,w_exp)
+    grad_first,grad_gain1,grad_bias1=normalize_back(grad_normed,first_sum,norm_gains[0])
+    grad_a_low=grad_first.astype(BF)
+    grad_out=inner_rows(att_low,grad_a_low)
+    grad_attended=inner_cols(grad_a_low,w_out).astype(BF)
+    width=model_width//2
+    d_own=lax.dynamic_slice_in_dim(grad_attended,pos*width,width,1)
+    d_oth=lax.dynamic_slice_in_dim(grad_attended,(1-pos)*width,width,1)
+    d_recv=swap_cores(d_oth)
+    scatter=lambda g: lax.psum_scatter(g,("dp","dim"),scatter_dimension=0,tiled=True).astype(F32)
+    grad_norm=jnp.stack([grad_gain1,grad_bias1,grad_gain2,grad_bias2]).reshape(4,count,share_rows).transpose(1,0,2)
+    grad_norm=jnp.pad(grad_norm,((0,0),(0,share_rows-4),(0,128-share_rows))).reshape(model_width,128)
+    fold_con=grad_con.astype(BF).reshape(count,per,share_rows,model_width).transpose(0,2,1,3).reshape(model_width,per*model_width)
+    sums=scatter(jnp.concatenate([grad_out.astype(BF),grad_exp.astype(BF),fold_con,grad_norm.astype(BF)],1))
+    sum_out=sums[:,0:at1]
+    sum_exp=sums[:,at1:at2]
+    sum_con=unfold_rows(sums[:,at2:at3],per,share_rows)
+    sum_norm=sums[0:4,at3:at3+share_rows]
+    g_own,g_oth=attend_bwd(ctl,own,recv,d_own,d_recv,o_own,o_oth,lse,cos,sin)
+    grad_mixed=join_parts(pos,unpair(g_own),unpair(swap_cores(g_oth)))
+    grad_mix=inner_rows(tokens,grad_mixed)
+    token_grads=grad_first+inner_cols(grad_mixed,w_mix)
+    sum_mix=scatter(grad_mix.astype(BF))
+    total_rows=group_rows*lax.axis_size("dp")
+    matrix_rate=1.0/math.sqrt(total_rows)
+    norm_rate=0.3/math.sqrt(total_rows)
+    grads=[g[None] for g in (sum_mix,sum_out,sum_exp,sum_con,sum_norm)]
+    weights=(mixer_in,mixer_out,expand,contract,norm_params)
+    moments=(mixer_in_moment,mixer_out_moment,expand_moment,contract_moment,norm_moment)
+    averages=(mixer_in_average,mixer_out_average,expand_average,contract_average,norm_average)
+    rates=(matrix_rate,matrix_rate,matrix_rate,matrix_rate,norm_rate)
+    results=[advance(weights[k],moments[k],averages[k],grads[k],rates[k]) for k in range(5)]
+    return (embeddings,token_grads,*grads,*[results[k][f] for f in range(4) for k in range(5)])
+
+def unpair(g):
+    rows,width=g.shape
+    pairs=width//384
+    return jnp.concatenate([g[:,p*384+s*128:p*384+(s+1)*128] for s in range(3) for p in range(pairs)],1)
+
+
 def solution(mesh):
     placed = (
         P(("dp", "dim"), None),

time: 2090 us -> 926 us (0.44)
  matrix products: 899 us -> 179 us
  other arithmetic: 402 us -> 71.1 us
  Pallas kernels: 0 us -> 303 us
  waiting for transfers between devices: 528 us -> 269 us
  blocking collectives: 85.7 us -> 4.25 us
  local copies, waits for them, and re-layouts: 127 us -> 76.9 us
    reduce_scatter x5 -> x1, waiting for transfers between devices: 462 us -> 23.5 us  [body(): lax.psum_scatter(g, ('dp', 'dim'), scatter_dimension=0, tiled=True)]
    dot_general x40 -> x4, matrix products: 459 us -> 75.2 us  [inner_cols(): lax.dot_general(left_op, right_op, (((1,), (1,)), ((), ())), preferred_el...]
    pallas_call x0 -> x3, Pallas kernels: none -> 303 us  [the longest x1 150 us: attend_fwd(): pl.pallas_call(fwd_kernel, grid_spec=pltpu.PrefetchScalarGridSpec(num_sca...]
    convert_element_type x21 -> x6, other arithmetic: 241 us -> 20.9 us  [the longest x1 17.4 us: body(): (jax.nn.silu(gate_up[:, 0:half]) * gate_up[:, half:2 * half]).astype(BF)]
    dot_general x29 -> x4, matrix products: 257 us -> 44.1 us  [matmul(): return jnp.dot(left_op, right_op, preferred_element_type=jnp.float32)]
    unnamed x13 -> x7, waiting for transfers between devices: 4.54 us -> 182 us
    dot_general x28 -> x4, matrix products: 171 us -> 45.6 us  [inner_rows(): lax.dot_general(left_op, right_op, (((0,), (0,)), ((), ())), preferred_el...]
    reduce_sum x15 -> x0, other arithmetic: 108 us -> none  [the longest x12 108 us: one_head(): row_total = jnp.sum(exponent, axis=1, keepdims=True)]
  transfers between devices with their start and end apart: 12 -> 9, of which waited for: 6 -> 8; matrix products, arithmetic and copies ran while one was open for 26% -> 11% of each run, Pallas kernels for 0% -> 17%
where the time goes in v1:
time: 926 us; the launch traced here: 920 us
  Pallas kernels  303 us (33%)
  waiting for transfers between devices  269 us (29%)
  matrix products  179 us (19%)
  local copies, waits for them, and re-layouts  76.9 us (8%)
  other arithmetic  71.1 us (8%)
  between operations  16.2 us (2%)
    unnamed x7, waiting for transfers between devices  182 us
    pallas_call x1, Pallas kernels, attend_fwd(): pl.pallas_call(fwd_kernel, grid_spec=pltpu.PrefetchScalarGridSpec(num_sca...  150 us
    pallas_call x1, Pallas kernels, attend_bwd(): pl.pallas_call(bwd_kernel, grid_spec=pltpu.PrefetchScalarGridSpec(num_sca...  143 us
    dot_general x4, matrix products, inner_cols(): lax.dot_general(left_op, right_op, (((1,), (1,)), ((), ())), preferred_el...  75.2 us
    all_gather x1, waiting for transfers between devices, body(): lax.all_gather(w[0].astype(BF), ('dp', 'dim'), axis=axis, tiled=True)  48.5 us
    dot_general x4, matrix products, inner_rows(): lax.dot_general(left_op, right_op, (((0,), (0,)), ((), ())), preferred_el...  45.6 us
    dot_general x4, matrix products, matmul(): return jnp.dot(left_op, right_op, preferred_element_type=jnp.float32)  44.1 us
    unnamed x145, local copies, waits for them, and re-layouts  40.5 us
  transfers between devices with their start and end apart: 9, of which 8 were waited for; matrix products, arithmetic and copies ran while one was open for 11% of the time, Pallas kernels for 17%

profile of v1, /device:TPU:0, one launch (start us, length us, event | category | flops | bytes accessed | tf_op | source)
XLA Modules:
  0.0 919.9 jit_solution(11187128195746075666)
XLA Ops:
  17.7 5.5 fusion.20
  25.8 48.5 %all-gather.6.cloned.1.call-done = bf16[1,768,2304]{2,1,0:T(8,128)(2,1)} async-done(((bf16[1,24,2304]{2,1,0:T(8,128)(2,1)}), bf16[1,768,2304]{2,1,0:T(8,128)(2,1)}) %all-gather.6.cloned.1.call-update) | async-done | bytes 3538960 | tf_op jit(solution)/shard_map/all_gather | solution.py:686
  77.5 9.5 %mix.1 = (bf16[1536,1152]{1,0:T(8,128)(2,1)S(1)}, bf16[1536,1152]{1,0:T(8,128)(2,1)S(1)}) custom-call(s32[3]{0:T(128)S(1)} %pad_add_fusion.ctl, bf16[1536,768]{1,0:T(8,128)(2,1)S(1)} %copy-done.2, bf16[768,2304]{1,0:T(8,128)(2,1)S(1)} %bitcast.65, f32[1536,128]{1,0:T(8,128)S(1)} %copy-done.4, f32[1536,128]{1,0:T(8,128)S(1)} %constant_dynamic-slice_fusion.2.sin), custom_call_target="tpu_custom_call" | custom-call | flops 5435817984 | bytes 12976128 | tf_op jit(solution)/shard_map/mix/pallas_call | solution.py:642
  89.1 6.0 collective-permute-done.qr.kr.vr
  96.9 150.2 %attend_fwd.1 = (bf16[1536,384]{1,0:T(8,128)(2,1)}, bf16[1536,384]{1,0:T(8,128)(2,1)}, f32[3,8,3072]{2,1,0:T(8,128)}) custom-call(s32[3]{0:T(128)} %copy-done.5, bf16[1536,1152]{1,0:T(8,128)(2,1)} %copy-done.8, bf16[1536,1152]{1,0:T(8,128)(2,1)} %copy-done.8, bf16[1536,1152]{1,0:T(8,128)(2,1)} %copy-done.8, bf16[1536,1152]{1,0:T(8,128)(2,1)} %copy-done.49, ...), custom_call_target="tpu_custom_call" | custom-call | flops 7247757312 | bytes 17694720 | tf_op jit(solution)/shard_map/attend_fwd/pallas_call | solution.py:499
  250.3 5.9 fusion.96
  259.2 24.4 %fusion.5 = f32[1536,6144]{1,0:T(8,128)} fusion(bf16[768,10112]{1,0:T(8,128)(2,1)} %all-gather.4.cloned.1.call-done, f32[1536,768]{0,1:T(8,128)} %copy-done.10, f32[768]{0:T(1024)S(1)} %add.189, f32[768]{0:T(1024)S(1)} %mul.307, f32[1536]{0:T(1024)S(1)} %add_rsqrt_fusion.1, f32[1536]{0:T(1024)S(1)} %broadcast_multiply_fusion.5), kind=kOutput, calls=%fused_computation.11 | convolution fusion | flops 14501412864 | bytes 51922944 | tf_op jit(solution)/shard_map/dot_general | solution.py:22
  283.6 17.4 %multiply_convert_fusion.2 = bf16[1536,3072]{1,0:T(8,128)(2,1)} fusion(f32[1536,6144]{1,0:T(8,128)} %fusion.5), kind=kLoop, calls=%fused_computation.3 | loop fusion | flops 28311552 | bytes 47185920 | tf_op jit(solution)/shard_map/convert_element_type | solution.py:728
  301.0 4.8 slice.174
  305.8 9.8 %reshape.207 = bf16[32,24,4,768]{3,2,1,0:T(4,128)(2,1)} reshape(bf16[768,3072]{1,0:T(8,128)(2,1)} %slice.174) | data formatting | bytes 9437184 | tf_op jit(solution)/shard_map/reshape | solution.py:659
  319.2 13.7 %fusion.97 = (f32[1536]{0:T(1024)S(1)}, f32[1536,768]{0,1:T(8,128)}) fusion(bf16[1536,3072]{1,0:T(8,128)(2,1)} %multiply_convert_fusion.2, bf16[3072,768]{1,0:T(8,128)(2,1)S(1)} %bitcast.73, f32[768]{0:T(1024)S(1)} %add.189, f32[768]{0:T(1024)S(1)} %mul.307, f32[1536]{0:T(1024)S(1)} %add_rsqrt_fusion.1, f32[1536,768]{0,1:T(8,128)S(1)} %bitcast.69, ...), kind=kOutput, calls=%fused_computation.210 | convolution fusion | flops 7254833664 | bytes 23617536 | tf_op jit(solution)/shard_map/dot_general | solution.py:22
  335.9 5.9 fusion.21
  341.9 6.5 reduce-scatter.10.cloned.1.call-done
  354.5 6.8 fusion.98
  361.3 6.0 copy.131
  367.4 5.4 multiply_reduce_fusion
  372.7 5.6 subtract_multiply_fusion.1
  378.4 30.5 %multiply_convert_fusion.1 = (bf16[1536,3072]{1,0:T(8,128)(2,1)}, bf16[1536,3072]{1,0:T(8,128)(2,1)}) fusion(f32[1536,6144]{1,0:T(8,128)} %fusion.5, bf16[3072,768]{1,0:T(8,128)(2,1)} %bitcast.74, f32[1536,768]{0,1:T(8,128)} %subtract_multiply_fusion.1), kind=kOutput, calls=%fused_computation.2 | convolution fusion | flops 7310278656 | bytes 66060288 | tf_op jit(solution)/shard_map/dot_general | solution.py:36
  408.8 29.4 %multiply_reduce_fusion.1 = (bf16[768]{0:T(1024)(128)(2,1)}, f32[1536]{0:T(1024)S(1)}, f32[1536]{0:T(1024)S(1)}, bf16[768]{0:T(1024)(128)(2,1)}, f32[1536,768]{0,1:T(8,128)}) fusion(f32[1536,768]{0,1:T(8,128)} %copy-done.10, f32[1536]{0:T(1024)S(1)} %add_rsqrt_fusion.1, f32[1536]{0:T(1024)S(1)} %broadcast_multiply_fusion.5, f32[768]{0:T(1024)S(1)} %mul.307, ...), kind=kOutput, calls=%fused_computation.17 | convolution fusion | flops 14545054720 | bytes 42498048 | tf_op jit(solution)/shard_map/dot_general | solution.py:36
  438.2 5.0 subtract_multiply_fusion
  443.2 4.2 convolution_convert_fusion.2
  452.8 143.2 %attend_bwd.1 = (bf16[1536,1152]{1,0:T(8,128)(2,1)}, bf16[1536,1152]{1,0:T(8,128)(2,1)}) custom-call(s32[3]{0:T(128)} %copy-done.5, bf16[1536,1152]{1,0:T(8,128)(2,1)} %copy-done.8, bf16[1536,1152]{1,0:T(8,128)(2,1)} %copy-done.8, bf16[1536,1152]{1,0:T(8,128)(2,1)} %copy-done.8, bf16[1536,1152]{1,0:T(8,128)(2,1)} %copy-done.49, ...), custom_call_target="tpu_custom_call" | custom-call | flops 18119393280 | bytes 35389440 | tf_op jit(solution)/shard_map/attend_bwd/pallas_call | solution.py:604
  596.4 6.1 collective-permute-done.3
  612.6 6.4 fusion.10
  623.1 13.4 %convolution_convert_fusion = bf16[3072,768]{1,0:T(8,128)(2,1)} fusion(bf16[1536,3072]{1,0:T(8,128)(2,1)} %multiply_convert_fusion.2, f32[1536,768]{0,1:T(8,128)} %subtract_multiply_fusion.1), kind=kOutput, calls=%fused_computation.14 | convolution fusion | flops 7251296256 | bytes 18874368 | tf_op jit(solution)/shard_map/dot_general | solution.py:30
  637.0 4.9 copy.135
  650.6 22.0 %fusion.3 = bf16[768,6144]{1,0:T(8,128)(2,1)} fusion(bf16[1536,3072]{1,0:T(8,128)(2,1)} %get-tuple-element.206, bf16[1536,3072]{1,0:T(8,128)(2,1)} %get-tuple-element.205, f32[1536,768]{0,1:T(8,128)} %copy-done.10, f32[768]{0:T(1024)S(1)} %copy-done.42, f32[768]{0:T(1024)S(1)} %copy-done.36, f32[1536]{0:T(1024)S(1)} %add_rsqrt_fusion.1, ...), kind=kOutput, calls=%fused_computation.9 | convolution fusion | flops 14543880192 | bytes 33048576 | tf_op jit(solution)/shard_map/dot_general | solution.py:30
  672.6 11.0 %pad_maximum_fusion.1 = bf16[768,10112]{1,0:T(8,128)(2,1)} fusion(bf16[768,128]{1,0:T(8,128)(2,1)S(1)} %bitcast.81, bf16[768,3072]{1,0:T(8,128)(2,1)S(1)} %bitcast.72, bf16[768,6144]{1,0:T(8,128)(2,1)} %fusion.3, bf16[768,768]{1,0:T(8,128)(2,1)} %copy.138), kind=kLoop, calls=%fused_computation.6 | loop fusion | flops 62128128 | bytes 31064064 | tf_op jit(solution)/shard_map/concatenate | solution.py:780
  685.6 11.1 %convolution_add_fusion = f32[1536,768]{0,1:T(8,128)} fusion(f32[1536,768]{0,1:T(8,128)} %copy-done.12, bf16[1536,2304]{1,0:T(8,128)(2,1)} %copy-done.34, bf16[1536,2304]{1,0:T(8,128)(2,1)} %copy-done.33, pred[]{:T(512)S(6)} %eq.56, bf16[1,768,2304]{2,1,0:T(8,128)(2,1)S(1)} %copy-done.7), kind=kOutput, calls=%fused_computation.37 | convolution fusion | flops 5440536576 | bytes 27131904 | tf_op jit(solution)/shard_map/dot_general | solution.py:36
  696.7 6.1 copy.140
  702.9 23.5 %reduce-scatter.12.cloned.1.call-done = bf16[24,2304]{1,0:T(8,128)(2,1)} async-done(((bf16[768,2304]{1,0:T(8,128)(2,1)}), bf16[24,2304]{1,0:T(8,128)(2,1)}) %reduce-scatter.12.cloned.1.call-update) | async-done | bytes 110608 | tf_op jit(solution)/shard_map/reduce_scatter | solution.py:776
  728.9 175.4 %reduce-scatter.14.cloned.1.call-done = bf16[24,10112]{1,0:T(8,128)(2,1)} async-done(((bf16[768,10112]{1,0:T(8,128)(2,1)}), bf16[24,10112]{1,0:T(8,128)(2,1)}) %reduce-scatter.14.cloned.1.call-update) | async-done | bytes 485392
  (235 shorter events, 79.8 us)
Async XLA Ops:
  7.2 242.7 %copy-start = (bf16[256,384]{1,0:T(8,128)(2,1)S(1)}, bf16[256,384]{1,0:T(8,128)(2,1)}, u32[]{:S(2)}) copy-start(bf16[256,384]{1,0:T(8,128)(2,1)} %param.23) | copy-start | bytes 589828
  7.2 67.1 %all-gather.6.cloned.1.call-start = ((), (), s32[]{:S(2)}) async-start(), calls=%async_computation.4 | async-start | bytes 3649536 | tf_op jit(solution)/shard_map/all_gather | solution.py:686
  8.9 65.4 %copy-start.2 = (bf16[1536,768]{1,0:T(8,128)(2,1)S(1)}, bf16[1536,768]{1,0:T(8,128)(2,1)}, u32[]{:S(2)}) copy-start(bf16[1536,768]{1,0:T(8,128)(2,1)} %x.5) | copy-start | bytes 7077892
  8.9 241.4 %all-gather.4.cloned.1.call-start = ((), (), s32[]{:S(2)}) async-start(), calls=%async_computation.3 | async-start | bytes 16017408 | tf_op jit(solution)/shard_map/all_gather | solution.py:694
  13.6 334.7 %reduce-scatter.10.cloned.1.call-start = ((), (), s32[]{:S(2)}) async-start(), calls=%async_computation.5 | async-start | bytes 589824
  17.0 69.9 %copy-start.5 = (s32[3]{0:T(128)}, s32[3]{0:T(128)S(1)}, u32[]{:S(2)}) copy-start(s32[3]{0:T(128)S(1)} %pad_add_fusion.ctl) | copy-start | bytes 40
  88.9 6.2 collective-permute-start
  247.1 3.3 collective-permute-start.1
  259.1 179.1 %copy-start.35 = (f32[768]{0:T(1024)}, f32[768]{0:T(1024)S(1)}, u32[]{:S(2)}) copy-start(f32[768]{0:T(1024)S(1)} %mul.307) | copy-start | bytes 9220
  259.2 59.8 %copy-start.41 = (f32[768]{0:T(1024)}, f32[768]{0:T(1024)S(1)}, u32[]{:S(2)}) copy-start(f32[768]{0:T(1024)S(1)} %add.189) | copy-start | bytes 9220
  319.0 13.9 %copy-start.11 = (bf16[32,4,24,768]{3,2,1,0:T(8,128)(2,1)}, bf16[32,4,24,768]{3,2,1,0:T(8,128)(2,1)S(1)}, u32[]{:S(2)}) copy-start(bf16[32,4,24,768]{3,2,1,0:T(8,128)(2,1)S(1)} %copy.130) | copy-start | bytes 14155780
  341.8 384.5 %reduce-scatter.12.cloned.1.call-start = ((), (), s32[]{:S(2)}) async-start(), calls=%async_computation.6 | async-start | bytes 3649536 | tf_op jit(solution)/shard_map/reduce_scatter | solution.py:776
  448.9 2.8 collective-permute-start.2
  596.0 6.5 collective-permute-start.3
  623.1 13.7 %copy-start.38 = (bf16[768]{0:T(1024)(128)(2,1)S(1)}, bf16[768]{0:T(1024)(128)(2,1)}, u32[]{:S(2)}) copy-start(bf16[768]{0:T(1024)(128)(2,1)} %get-tuple-element.178) | copy-start | bytes 4612
  623.1 13.8 %copy-start.37 = (bf16[768]{0:T(1024)(128)(2,1)S(1)}, bf16[768]{0:T(1024)(128)(2,1)}, u32[]{:S(2)}) copy-start(bf16[768]{0:T(1024)(128)(2,1)} %get-tuple-element.252) | copy-start | bytes 4612
  623.1 281.1 %reduce-scatter.14.cloned.1.call-start = ((), (), s32[]{:S(2)}) async-start(), calls=%async_computation.7 | async-start | bytes 16017408
  649.0 23.5 %slice-start.2 = ((s8[4718592]{0:T(1024)(128)(4,1)}), s8[524288]{0:T(1024)(128)(4,1)S(1)}, s32[]{:S(2)}) async-start(s8[4718592]{0:T(1024)(128)(4,1)} %bitcast.70), calls=%async_computation.10 | async-start | bytes 1048576
  650.6 22.0 %slice-start.3 = ((s8[4718592]{0:T(1024)(128)(4,1)}), s8[4194304]{0:T(1024)(128)(4,1)S(1)}, s32[]{:S(2)}) async-start(s8[4718592]{0:T(1024)(128)(4,1)} %bitcast.70), calls=%async_computation.11 | async-start | bytes 8388608
  696.7 29.7 %copy-start.21 = (f32[1,24,2304]{2,1,0:T(8,128)S(1)}, f32[1,24,2304]{2,1,0:T(8,128)}, u32[]{:S(2)}) copy-start(f32[1,24,2304]{2,1,0:T(8,128)} %param.24) | copy-start | bytes 663556
  696.7 29.7 %copy-start.30 = (f32[1,24,2304]{2,1,0:T(8,128)S(1)}, f32[1,24,2304]{2,1,0:T(8,128)}, u32[]{:S(2)}) copy-start(f32[1,24,2304]{2,1,0:T(8,128)} %param.29) | copy-start | bytes 663556
  696.7 31.4 %copy-start.29 = (f32[1,24,2304]{2,1,0:T(8,128)S(1)}, f32[1,24,2304]{2,1,0:T(8,128)}, u32[]{:S(2)}) copy-start(f32[1,24,2304]{2,1,0:T(8,128)} %param.34) | copy-start | bytes 663556
  702.8 203.8 %copy-start.17 = (f32[1,24,6144]{2,1,0:T(8,128)S(1)}, f32[1,24,6144]{2,1,0:T(8,128)}, u32[]{:S(2)}) copy-start(f32[1,24,6144]{2,1,0:T(8,128)} %param.26) | copy-start | bytes 1769476
  702.8 203.8 %copy-start.24 = (f32[1,24,6144]{2,1,0:T(8,128)S(1)}, f32[1,24,6144]{2,1,0:T(8,128)}, u32[]{:S(2)}) copy-start(f32[1,24,6144]{2,1,0:T(8,128)} %param.31) | copy-start | bytes 1769476
  702.8 205.1 %copy-start.28 = (f32[1,24,768]{2,1,0:T(8,128)S(1)}, f32[1,24,768]{2,1,0:T(8,128)}, u32[]{:S(2)}) copy-start(f32[1,24,768]{2,1,0:T(8,128)} %param.25) | copy-start | bytes 221188
  702.8 205.1 %copy-start.32 = (f32[1,24,768]{2,1,0:T(8,128)S(1)}, f32[1,24,768]{2,1,0:T(8,128)}, u32[]{:S(2)}) copy-start(f32[1,24,768]{2,1,0:T(8,128)} %param.30) | copy-start | bytes 221188
  702.8 205.8 %copy-start.40 = (f32[1,4,24]{2,1,0:T(4,128)S(1)}, f32[1,4,24]{2,1,0:T(4,128)}, u32[]{:S(2)}) copy-start(f32[1,4,24]{2,1,0:T(4,128)} %param.28) | copy-start | bytes 1156
  702.8 205.8 %copy-start.48 = (f32[1,4,24]{2,1,0:T(4,128)S(1)}, f32[1,4,24]{2,1,0:T(4,128)}, u32[]{:S(2)}) copy-start(f32[1,4,24]{2,1,0:T(4,128)} %param.33) | copy-start | bytes 1156
  702.9 206.4 %copy-start.23 = (f32[1,24,6144]{2,1,0:T(8,128)S(1)}, f32[1,24,6144]{2,1,0:T(8,128)}, u32[]{:S(2)}) copy-start(f32[1,24,6144]{2,1,0:T(8,128)} %param.36) | copy-start | bytes 1769476
  728.1 182.1 %copy-start.22 = (f32[1,24,2304]{2,1,0:T(8,128)}, f32[1,24,2304]{2,1,0:T(8,128)S(1)}, u32[]{:S(2)}) copy-start(f32[1,24,2304]{2,1,0:T(8,128)S(1)} %get-tuple-element.202) | copy-start | bytes 663556
  728.9 181.4 %copy-start.19 = (f32[1,96,768]{2,1,0:T(8,128)S(1)}, f32[1,96,768]{2,1,0:T(8,128)}, u32[]{:S(2)}) copy-start(f32[1,96,768]{2,1,0:T(8,128)} %param.27) | copy-start | bytes 884740
  728.9 181.4 %copy-start.25 = (f32[1,96,768]{2,1,0:T(8,128)S(1)}, f32[1,96,768]{2,1,0:T(8,128)}, u32[]{:S(2)}) copy-start(f32[1,96,768]{2,1,0:T(8,128)} %param.32) | copy-start | bytes 884740
  (38 other events, 178.6 us)
Sparse Core Ops, SparseCore 0:
  11.5 62.7 all-gather.5
  77.8 108.1 all-gather.3
  341.9 6.3 reduce-scatter.9
  623.2 103.1 reduce-scatter.11
  733.4 170.7 reduce-scatter.13

commit v2 on v1

--- a/solution.py
+++ b/solution.py
@@ -402,7 +402,8 @@
 
 
 NEG=-1e30
-BQ=256
+BQ=512
+ROWS=256
 BK=512
 F32=jnp.float32
 BF=jnp.bfloat16
@@ -455,12 +456,12 @@
         def step(j,carry):
             k0=pl.multiple_of(base+j*BK,128)
             kb=kaug[pl.ds(k0,BK),:]
+            scores=[nt(kb,qs[h]) for h in range(2)]
             out=[]
             for h in range(2):
                 m,acc=carry[h]
-                st=nt(kb,qs[h])
-                mn=jnp.maximum(m,jnp.max(st,axis=0,keepdims=True))
-                pt=jnp.exp(st-mn).astype(BF)
+                mn=jnp.maximum(m,jnp.max(scores[h],axis=0,keepdims=True))
+                pt=jnp.exp(scores[h]-mn).astype(BF)
                 acc=acc*jnp.exp(m-mn)+nn(vt[80*h:80*h+80,pl.ds(k0,BK)],pt)
                 out.append((mn,acc))
             return tuple(out)
@@ -542,15 +543,15 @@
     dk[...]=jnp.zeros_like(dk)
     dv[...]=jnp.zeros_like(dv)
     def spread(i,col,val):
-        local=i*BQ-pos*half
+        local=i*ROWS-pos*half
         @pl.when((local>=0)&(local<half))
-        def _(): go[pl.ds(pl.multiple_of(local,BQ),BQ),col*128:(col+1)*128] = val
+        def _(): go[pl.ds(pl.multiple_of(local,ROWS),ROWS),col*128:(col+1)*128]=val
         @pl.when((local<0)|(local>=half))
-        def _(): gx[pl.ds(pl.multiple_of(i*BQ-(1-pos)*half,BQ),BQ),col*128:(col+1)*128] = val
+        def _(): gx[pl.ds(pl.multiple_of(i*ROWS-(1-pos)*half,ROWS),ROWS),col*128:(col+1)*128]=val
     def unturn(x,r0):
         ln=lax.broadcasted_iota(jnp.int32,x.shape,1)
         swapped=jnp.where((ln%64)<32,pltpu.roll(x,96,1),pltpu.roll(x,32,1))
-        return x*cos[pl.ds(r0,BQ),:]-swapped*sin[pl.ds(r0,BQ),:]
+        return x*cos[pl.ds(r0,ROWS),:]-swapped*sin[pl.ds(r0,ROWS),:]
     def qblock(i,_):
         r0=pl.multiple_of(i*BQ,BQ)
         base,count=key_range(i,e0,e1)
@@ -562,37 +563,35 @@
             k0=pl.multiple_of(base+j*BK,128)
             kb=kaug[pl.ds(k0,BK),:]
             vb=vs[pl.ds(k0,BK),:]
-            out=[]
-            dva=dv[pl.ds(k0,BK),:]
-            dka=dk[pl.ds(k0,BK),:]
-            for h in range(2):
-                st=nt(kb,qs[h])
-                pt=jnp.exp(st-ls[h])
-                dpt=nt(vb,ds_[h])
-                dst=(pt*(dpt-de[h])).astype(BF)
-                dva=dva+nn(pt.astype(BF),ds_[h])
-                dka=dka+nn(dst,qs[h][:,0:128])
-                out.append(carry[h]+nn(kt[64*h:64*h+64,pl.ds(k0,BK)],dst))
-            dv[pl.ds(k0,BK),:]=dva
-            dk[pl.ds(k0,BK),:]=dka
+            both=range(2)
+            st=[nt(kb,qs[h]) for h in both]
+            dpt=[nt(vb,ds_[h]) for h in both]
+            pt=[jnp.exp(st[h]-ls[h]) for h in both]
+            dst=[(pt[h]*(dpt[h]-de[h])).astype(BF) for h in both]
+            pb=[pt[h].astype(BF) for h in both]
+            dv[pl.ds(k0,BK),:]+=nn(pb[0],ds_[0])+nn(pb[1],ds_[1])
+            dk[pl.ds(k0,BK),:]+=nn(dst[0],qs[0][:,0:128])+nn(dst[1],qs[1][:,0:128])
+            out=[carry[h]+nn(kt[64*h:64*h+64,pl.ds(k0,BK)],dst[h]) for h in both]
             return tuple(out)
         init=jnp.zeros((64,BQ),F32)
         res=lax.fori_loop(0,count,step,(init,init))
         dq=jnp.concatenate(res,axis=0).T*0.125
-        spread(i,0,unturn(dq,r0).astype(BF))
+        for t in range(BQ//ROWS):
+            at=pl.multiple_of(r0+t*ROWS,ROWS)
+            spread(i*(BQ//ROWS)+t,0,unturn(dq[t*ROWS:(t+1)*ROWS],at).astype(BF))
         return 0
     used=(e1+BQ-1)//BQ
     lax.fori_loop(0,used,qblock,0)
     def blank(i,_):
-        spread(i,0,jnp.zeros((BQ,128),BF))
+        spread(i,0,jnp.zeros((ROWS,128),BF))
         return 0
-    lax.fori_loop(used,rows//BQ,blank,0)
+    lax.fori_loop(used*(BQ//ROWS),rows//ROWS,blank,0)
     def last(i,_):
-        r0=pl.multiple_of(i*BQ,BQ)
-        spread(i,1,unturn(dk[pl.ds(r0,BQ),:],r0).astype(BF))
-        spread(i,2,dv[pl.ds(r0,BQ),:].astype(BF))
+        r0=pl.multiple_of(i*ROWS,ROWS)
+        spread(i,1,unturn(dk[pl.ds(r0,ROWS),:],r0).astype(BF))
+        spread(i,2,dv[pl.ds(r0,ROWS),:].astype(BF))
         return 0
-    lax.fori_loop(0,rows//BQ,last,0)
+    lax.fori_loop(0,rows//ROWS,last,0)
 
 def attend_bwd(ctl,own,recv,d_own,d_recv,o_own,o_oth,lse,cos,sin):
     half,width=own.shape
@@ -649,6 +648,14 @@
         name="mix",
     )(ctl,x,w,cos,sin)
 
+def shuffle(x,count,per,share):
+    rows=x.shape[0]
+    return x.reshape(rows,2,count,per,share).transpose(0,1,3,2,4).reshape(x.shape)
+
+def unshuffle(x,count,per,share):
+    rows=x.shape[0]
+    return x.reshape(rows,2,per,count,share).transpose(0,1,3,2,4).reshape(x.shape)
+
 def fold_rows(x,per):
     rows,cols=x.shape
     return x.reshape(per,rows//per,cols).transpose(1,0,2).reshape(rows//per,per*cols)
@@ -688,16 +695,18 @@
     share_rows=mixer_out.shape[1]
     per=contract.shape[1]//share_rows
     count=model_width//share_rows
-    con_cols=fold_rows(contract[0],per)
-    norm_cols=jnp.pad(norm_params[0],((0,share_rows-4),(0,128-share_rows)))
-    bundle=jnp.concatenate([mixer_out[0],expand[0],con_cols,norm_cols],1).astype(BF)
+    hidden_width=contract.shape[1]*count
+    exp_cols=shuffle(expand[0].astype(BF),count,per,share_rows)
+    con_cols=fold_rows(contract[0].astype(BF),per)
+    norm_cols=jnp.pad(norm_params[0].astype(BF),((0,share_rows-4),(0,128-share_rows)))
+    bundle=jnp.concatenate([exp_cols,con_cols,mixer_out[0].astype(BF),norm_cols],1)
     bundle=lax.all_gather(bundle,("dp","dim"),axis=0,tiled=True)
-    at1=model_width
-    at2=at1+expand.shape[2]
-    at3=at2+per*model_width
-    w_out=bundle[:,0:at1]
-    w_exp=bundle[:,at1:at2]
-    w_con=unfold_rows(bundle[:,at2:at3],per,share_rows)
+    at1=2*hidden_width
+    at2=at1+per*model_width
+    at3=at2+model_width
+    w_exp=bundle[:,0:at1]
+    w_con=[bundle[:,at1+j*model_width:at1+(j+1)*model_width] for j in range(per)]
+    w_out=bundle[:,at2:at3]
     w_norm=bundle[:,at3:].reshape(count,share_rows,128)[:,0:4,0:share_rows].transpose(1,0,2).reshape(4,model_width)
     lengths=doc_lengths[0]
     e0=lengths[0]
@@ -726,6 +735,7 @@
     gate_up=matmul(y_low,w_exp)
     half=gate_up.shape[1]//2
     hidden=(jax.nn.silu(gate_up[:,0:half])*gate_up[:,half:2*half]).astype(BF)
+    w_con=jnp.concatenate(w_con,0)
     second_sum=normed+matmul(hidden,w_con)
     final=normalize(second_sum,norm_gains[2],norm_gains[3])
     member=(seg_rows[None,:]==jnp.arange(doc_count,dtype=jnp.int32)[:,None]).astype(F32)
@@ -776,17 +786,21 @@
     scatter=lambda g: lax.psum_scatter(g,("dp","dim"),scatter_dimension=0,tiled=True).astype(F32)
     grad_norm=jnp.stack([grad_gain1,grad_bias1,grad_gain2,grad_bias2]).reshape(4,count,share_rows).transpose(1,0,2)
     grad_norm=jnp.pad(grad_norm,((0,0),(0,share_rows-4),(0,128-share_rows))).reshape(model_width,128)
-    fold_con=grad_con.astype(BF).reshape(count,per,share_rows,model_width).transpose(0,2,1,3).reshape(model_width,per*model_width)
-    sums=scatter(jnp.concatenate([grad_out.astype(BF),grad_exp.astype(BF),fold_con,grad_norm.astype(BF)],1))
-    sum_out=sums[:,0:at1]
-    sum_exp=sums[:,at1:at2]
-    sum_con=unfold_rows(sums[:,at2:at3],per,share_rows)
-    sum_norm=sums[0:4,at3:at3+share_rows]
+    fold_con=[grad_con[j*model_width:(j+1)*model_width].astype(BF) for j in range(per)]
+    terms=jnp.concatenate([grad_exp.astype(BF),*fold_con,grad_out.astype(BF),grad_norm.astype(BF)],1)
+    terms,d_own,d_recv=lax.optimization_barrier((terms,d_own,d_recv))
+    sums=scatter(terms)
     g_own,g_oth=attend_bwd(ctl,own,recv,d_own,d_recv,o_own,o_oth,lse,cos,sin)
     grad_mixed=join_parts(pos,unpair(g_own),unpair(swap_cores(g_oth)))
     grad_mix=inner_rows(tokens,grad_mixed)
     token_grads=grad_first+inner_cols(grad_mixed,w_mix)
-    sum_mix=scatter(grad_mix.astype(BF))
+    grad_mix=grad_mix.astype(BF)
+    grad_mix,sums=lax.optimization_barrier((grad_mix,sums))
+    sum_mix=scatter(grad_mix)
+    sum_exp=unshuffle(sums[:,0:at1],count,per,share_rows)
+    sum_con=unfold_rows(sums[:,at1:at2],per,share_rows)
+    sum_out=sums[:,at2:at3]
+    sum_norm=sums[0:4,at3:at3+share_rows]
     total_rows=group_rows*lax.axis_size("dp")
     matrix_rate=1.0/math.sqrt(total_rows)
     norm_rate=0.3/math.sqrt(total_rows)

time: 926 us -> 722 us (0.78)
  waiting for transfers between devices: 269 us -> 140 us
  Pallas kernels: 303 us -> 221 us
    unnamed x7, waiting for transfers between devices: 182 us -> 21.5 us
    pallas_call x1, Pallas kernels: 150 us -> 79.1 us  [attend_fwd(): pl.pallas_call(fwd_kernel, grid_spec=pltpu.PrefetchScalarGridSpec(num_sca...]
    reduce_scatter x1, waiting for transfers between devices: 23.5 us -> 59.1 us  [body(): lax.psum_scatter(g, ('dp', 'dim'), scatter_dimension=0, tiled=True)]
    pallas_call x1, Pallas kernels: 143 us -> 132 us  [attend_bwd(): pl.pallas_call(bwd_kernel, grid_spec=pltpu.PrefetchScalarGridSpec(num_sca...]
    concatenate x2 -> x1, other arithmetic: 11.8 us -> 1.77 us  [body(): jnp.concatenate([exp_cols, con_cols, mixer_out[0].astype(BF), norm_cols], 1)]
    reshape x2 -> x1, local copies, waits for them, and re-layouts: 9.95 us -> 0.14 us  [unfold_rows(): x.reshape(count, share, per, cols).transpose(0, 2, 1, 3)]
    unnamed x145 -> x159, local copies, waits for them, and re-layouts: 40.5 us -> 48.4 us
  transfers between devices with their start and end apart: 9 -> 9, of which waited for: 8 -> 7; matrix products, arithmetic and copies ran while one was open for 11% -> 13% of each run, Pallas kernels for 17% -> 31%
where the time goes in v2:
time: 722 us; the launch traced here: 713 us
  Pallas kernels  221 us (31%)
  matrix products  180 us (25%)
  waiting for transfers between devices  140 us (19%)
  local copies, waits for them, and re-layouts  85 us (12%)
  other arithmetic  63.9 us (9%)
  between operations  16.5 us (2%)
    pallas_call x1, Pallas kernels, attend_bwd(): pl.pallas_call(bwd_kernel, grid_spec=pltpu.PrefetchScalarGridSpec(num_sca...  132 us
    pallas_call x1, Pallas kernels, attend_fwd(): pl.pallas_call(fwd_kernel, grid_spec=pltpu.PrefetchScalarGridSpec(num_sca...  79.1 us
    dot_general x4, matrix products, inner_cols(): lax.dot_general(left_op, right_op, (((1,), (1,)), ((), ())), preferred_el...  72 us
    reduce_scatter x1, waiting for transfers between devices, body(): lax.psum_scatter(g, ('dp', 'dim'), scatter_dimension=0, tiled=True)  59.1 us
    unnamed x159, local copies, waits for them, and re-layouts  48.4 us
    dot_general x4, matrix products, inner_rows(): lax.dot_general(left_op, right_op, (((0,), (0,)), ((), ())), preferred_el...  48.2 us
    dot_general x4, matrix products, matmul(): return jnp.dot(left_op, right_op, preferred_element_type=jnp.float32)  47 us
    all_gather x1, waiting for transfers between devices, body(): lax.all_gather(w[0].astype(BF), ('dp', 'dim'), axis=axis, tiled=True)  43 us
  transfers between devices with their start and end apart: 9, of which 7 were waited for; matrix products, arithmetic and copies ran while one was open for 13% of the time, Pallas kernels for 31%

profile of v2, /device:TPU:0, one launch (start us, length us, event | category | flops | bytes accessed | tf_op | source)
XLA Modules:
  0.0 712.7 jit_solution(1689162665471375278)
XLA Ops:
  23.1 5.5 fusion.21
  31.3 43.0 %all-gather.6.cloned.1.call-done = bf16[1,768,2304]{2,1,0:T(8,128)(2,1)} async-done(((bf16[1,24,2304]{2,1,0:T(8,128)(2,1)}), bf16[1,768,2304]{2,1,0:T(8,128)(2,1)}) %all-gather.6.cloned.1.call-update) | async-done | bytes 3538960 | tf_op jit(solution)/shard_map/all_gather | solution.py:693
  77.5 9.8 %mix.1 = (bf16[1536,1152]{1,0:T(8,128)(2,1)S(1)}, bf16[1536,1152]{1,0:T(8,128)(2,1)S(1)}) custom-call(s32[3]{0:T(128)S(1)} %pad_add_fusion.ctl, bf16[1536,768]{1,0:T(8,128)(2,1)S(1)} %copy-done.2, bf16[768,2304]{1,0:T(8,128)(2,1)S(1)} %bitcast.54, f32[1536,128]{1,0:T(8,128)S(1)} %copy-done.4, f32[1536,128]{1,0:T(8,128)S(1)} %constant_dynamic-slice_fusion.2.sin), custom_call_target="tpu_custom_call" | custom-call | flops 5435817984 | bytes 12976128 | tf_op jit(solution)/shard_map/mix/pallas_call | solution.py:641
  89.3 6.0 collective-permute-done.qr.kr.vr
  97.2 79.1 %attend_fwd.1 = (bf16[1536,384]{1,0:T(8,128)(2,1)}, bf16[1536,384]{1,0:T(8,128)(2,1)}, f32[3,8,3072]{2,1,0:T(8,128)}) custom-call(s32[3]{0:T(128)} %copy-done.5, bf16[1536,1152]{1,0:T(8,128)(2,1)} %copy-done.8, bf16[1536,1152]{1,0:T(8,128)(2,1)} %copy-done.8, bf16[1536,1152]{1,0:T(8,128)(2,1)} %copy-done.8, bf16[1536,1152]{1,0:T(8,128)(2,1)} %copy-done.54, ...), custom_call_target="tpu_custom_call" | custom-call | flops 7247757312 | bytes 17694720 | tf_op jit(solution)/shard_map/attend_fwd/pallas_call | solution.py:500
  181.2 4.7 all-gather.4.cloned.1.call-done
  185.9 5.8 fusion.101
  195.3 24.2 %fusion.6 = f32[1536,6144]{1,0:T(8,128)} fusion(bf16[768,10112]{1,0:T(8,128)(2,1)} %all-gather.4.cloned.1.call-done, f32[1536,768]{0,1:T(8,128)} %copy-done.10, f32[768]{0:T(1024)S(1)} %add.189, f32[768]{0:T(1024)S(1)} %mul.307, f32[1536]{0:T(1024)S(1)} %add_rsqrt_fusion.1, f32[1536]{0:T(1024)S(1)} %broadcast_multiply_fusion.5), kind=kOutput, calls=%fused_computation.11 | convolution fusion | flops 14501412864 | bytes 51922944 | tf_op jit(solution)/shard_map/dot_general | solution.py:22
  219.6 17.4 %multiply_convert_fusion.2 = bf16[1536,3072]{1,0:T(8,128)(2,1)} fusion(f32[1536,6144]{1,0:T(8,128)} %fusion.6), kind=kLoop, calls=%fused_computation.3 | loop fusion | flops 28311552 | bytes 47185920 | tf_op jit(solution)/shard_map/convert_element_type | solution.py:737
  240.7 16.8 %fusion.102 = (f32[1536]{0:T(1024)}, f32[1536,768]{0,1:T(8,128)}) fusion(bf16[1536,3072]{1,0:T(8,128)(2,1)} %multiply_convert_fusion.2, bf16[768,768]{1,0:T(8,128)(2,1)S(1)} %get-tuple-element.190, bf16[768,768]{1,0:T(8,128)(2,1)S(1)} %get-tuple-element.191, bf16[768,768]{1,0:T(8,128)(2,1)} %get-tuple-element.192, ...), kind=kOutput, calls=%fused_computation.218 | convolution fusion | flops 7273708032 | bytes 23617536 | tf_op jit(solution)/shard_map/dot_general | solution.py:22
  261.3 5.9 fusion.23
  267.3 6.0 reduce-scatter.10.cloned.1.call-done
  279.5 5.7 fusion.103
  285.2 6.1 copy.113
  291.3 5.2 multiply_reduce_fusion
  301.1 27.6 %multiply_convert_fusion.1 = (bf16[1536,3072]{1,0:T(8,128)(2,1)}, bf16[1536,3072]{1,0:T(8,128)(2,1)}) fusion(f32[1536,6144]{1,0:T(8,128)} %fusion.6, bf16[768,768]{1,0:T(8,128)(2,1)} %copy-done.21, bf16[768,768]{1,0:T(8,128)(2,1)} %copy-done.22, bf16[768,768]{1,0:T(8,128)(2,1)} %get-tuple-element.192, bf16[768,768]{1,0:T(8,128)(2,1)} %copy-done.20, ...), kind=kOutput, calls=%fused_computation.2 | convolution fusion | flops 7329153024 | bytes 66060288 | tf_op jit(solution)/shard_map/dot_general | solution.py:36
  328.7 13.4 %convolution_convert_fusion = bf16[3072,768]{1,0:T(8,128)(2,1)} fusion(bf16[1536,3072]{1,0:T(8,128)(2,1)} %multiply_convert_fusion.2, f32[1536,768]{0,1:T(8,128)} %subtract_multiply_fusion.1), kind=kOutput, calls=%fused_computation.14 | convolution fusion | flops 7251296256 | bytes 18874368 | tf_op jit(solution)/shard_map/dot_general | solution.py:30
  342.1 20.3 %fusion.4 = bf16[768,10112]{1,0:T(8,128)(2,1)} fusion(bf16[1536,3072]{1,0:T(8,128)(2,1)} %get-tuple-element.188, bf16[1536,3072]{1,0:T(8,128)(2,1)} %get-tuple-element.187, f32[1536,768]{0,1:T(8,128)S(1)} %bitcast.58, f32[768]{0:T(1024)S(1)} %copy-done.44, f32[768]{0:T(1024)S(1)} %copy-done.39, f32[1536]{0:T(1024)S(1)} %add_rsqrt_fusion.1, ...), kind=kOutput, calls=%fused_computation.9 | convolution fusion | flops 14543880192 | bytes 33048576 | tf_op jit(solution)/shard_map/dot_general | solution.py:30
  367.2 28.8 %multiply_reduce_fusion.1 = (bf16[768]{0:T(1024)(128)(2,1)S(1)}, f32[1536]{0:T(1024)S(1)}, f32[1536]{0:T(1024)S(1)}, bf16[768]{0:T(1024)(128)(2,1)S(1)}, f32[1536,768]{0,1:T(8,128)}) fusion(f32[1536,768]{0,1:T(8,128)} %copy-done.10, f32[1536]{0:T(1024)S(1)} %add_rsqrt_fusion.1, f32[1536]{0:T(1024)S(1)} %broadcast_multiply_fusion.5, f32[768]{0:T(1024)S(1)} %copy-done.39, ...), kind=kOutput, calls=%fused_computation.18 | convolution fusion | flops 14545054720 | bytes 42498048 | tf_op jit(solution)/shard_map/dot_general | solution.py:36
  396.0 5.0 subtract_multiply_fusion
  401.0 4.2 convolution_convert_fusion.2
  412.1 6.9 fusion.22
  420.9 132.2 %attend_bwd.1 = (bf16[1536,1152]{1,0:T(8,128)(2,1)}, bf16[1536,1152]{1,0:T(8,128)(2,1)}) custom-call(s32[3]{0:T(128)} %copy-done.5, bf16[1536,1152]{1,0:T(8,128)(2,1)} %copy-done.8, bf16[1536,1152]{1,0:T(8,128)(2,1)} %copy-done.8, bf16[1536,1152]{1,0:T(8,128)(2,1)} %copy-done.8, bf16[1536,1152]{1,0:T(8,128)(2,1)} %copy-done.54, ...), custom_call_target="tpu_custom_call" | custom-call | flops 18119393280 | bytes 35389440 | tf_op jit(solution)/shard_map/attend_bwd/pallas_call | solution.py:603
  553.5 6.1 collective-permute-done.3
  570.0 7.6 %fusion.11 = bf16[768,2304]{0,1:T(8,128)(2,1)} fusion(bf16[1536,768]{1,0:T(8,128)(2,1)S(1)} %copy-done.3, bf16[1536,2304]{1,0:T(8,128)(2,1)S(1)} %slice_dynamic-update-slice_fusion.5, bf16[1536,2304]{1,0:T(8,128)(2,1)S(1)} %get-tuple-element.193, pred[]{:T(512)S(6)} %eq.56), kind=kOutput, calls=%fused_computation.30 | convolution fusion | flops 5441126400 | bytes 20054016 | tf_op jit(solution)/shard_map/dot_general | solution.py:30
  577.6 15.4 %reduce-scatter.14.cloned.1.call-done = bf16[24,10112]{1,0:T(8,128)(2,1)} async-done(((bf16[768,10112]{1,0:T(8,128)(2,1)}), bf16[24,10112]{1,0:T(8,128)(2,1)}) %reduce-scatter.14.cloned.1.call-update) | async-done | bytes 485392
  595.0 5.9 copy.130
  601.0 11.3 %convolution_add_fusion = f32[1536,768]{0,1:T(8,128)} fusion(f32[1536,768]{0,1:T(8,128)} %copy-done.11, bf16[1536,2304]{1,0:T(8,128)(2,1)} %copy-done.37, bf16[1536,2304]{1,0:T(8,128)(2,1)} %copy-done.36, pred[]{:T(512)S(6)} %eq.56, bf16[1,768,2304]{2,1,0:T(8,128)(2,1)S(1)} %copy-done.7), kind=kOutput, calls=%fused_computation.38 | convolution fusion | flops 5440536576 | bytes 27131904 | tf_op jit(solution)/shard_map/dot_general | solution.py:36
  612.3 6.2 copy.123
  622.8 4.5 copy.121
  627.3 5.2 broadcast_in_dim_reshape.6
  643.9 59.1 %reduce-scatter.12.cloned.1.call-done = bf16[24,2304]{1,0:T(8,128)(2,1)} async-done(((bf16[768,2304]{1,0:T(8,128)(2,1)}), bf16[24,2304]{1,0:T(8,128)(2,1)}) %reduce-scatter.12.cloned.1.call-update) | async-done | bytes 110608 | tf_op jit(solution)/shard_map/reduce_scatter | solution.py:786
  (252 shorter events, 95.1 us)
Async XLA Ops:
  7.2 173.1 %copy-start = (bf16[256,384]{1,0:T(8,128)(2,1)S(1)}, bf16[256,384]{1,0:T(8,128)(2,1)}, u32[]{:S(2)}) copy-start(bf16[256,384]{1,0:T(8,128)(2,1)} %param.23) | copy-start | bytes 589828
  7.2 67.1 %all-gather.6.cloned.1.call-start = ((), (), s32[]{:S(2)}) async-start(), calls=%async_computation.4 | async-start | bytes 3649536 | tf_op jit(solution)/shard_map/all_gather | solution.py:693
  8.9 177.0 %all-gather.4.cloned.1.call-start = ((), (), s32[]{:S(2)}) async-start(), calls=%async_computation.3 | async-start | bytes 16017408 | tf_op jit(solution)/shard_map/all_gather | solution.py:703
  16.7 57.6 %copy-start.2 = (bf16[1536,768]{1,0:T(8,128)(2,1)S(1)}, bf16[1536,768]{1,0:T(8,128)(2,1)}, u32[]{:S(2)}) copy-start(bf16[1536,768]{1,0:T(8,128)(2,1)} %x.5) | copy-start | bytes 7077892
  19.8 253.5 %reduce-scatter.10.cloned.1.call-start = ((), (), s32[]{:S(2)}) async-start(), calls=%async_computation.5 | async-start | bytes 589824
  22.5 64.8 %copy-start.5 = (s32[3]{0:T(128)}, s32[3]{0:T(128)S(1)}, u32[]{:S(2)}) copy-start(s32[3]{0:T(128)S(1)} %pad_add_fusion.ctl) | copy-start | bytes 40
  89.1 6.2 collective-permute-start
  176.3 4.9 collective-permute-start.1
  195.2 24.3 %copy-start.38 = (f32[768]{0:T(1024)}, f32[768]{0:T(1024)S(1)}, u32[]{:S(2)}) copy-start(f32[768]{0:T(1024)S(1)} %mul.307) | copy-start | bytes 9220
  195.3 24.2 %copy-start.43 = (f32[768]{0:T(1024)}, f32[768]{0:T(1024)S(1)}, u32[]{:S(2)}) copy-start(f32[768]{0:T(1024)S(1)} %add.189) | copy-start | bytes 9220
  240.6 16.8 %copy-start.20 = (bf16[768,768]{1,0:T(8,128)(2,1)}, bf16[768,768]{1,0:T(8,128)(2,1)S(1)}, u32[]{:S(2)}) copy-start(bf16[768,768]{1,0:T(8,128)(2,1)S(1)} %get-tuple-element.189) | copy-start | bytes 3538948
  240.7 16.8 %copy-start.21 = (bf16[768,768]{1,0:T(8,128)(2,1)}, bf16[768,768]{1,0:T(8,128)(2,1)S(1)}, u32[]{:S(2)}) copy-start(bf16[768,768]{1,0:T(8,128)(2,1)S(1)} %get-tuple-element.190) | copy-start | bytes 3538948
  240.7 16.8 %copy-start.22 = (bf16[768,768]{1,0:T(8,128)(2,1)}, bf16[768,768]{1,0:T(8,128)(2,1)S(1)}, u32[]{:S(2)}) copy-start(bf16[768,768]{1,0:T(8,128)(2,1)S(1)} %get-tuple-element.191) | copy-start | bytes 3538948
  261.1 13.8 %copy-start.53 = (f32[2,5]{1,0:T(2,128)S(1)}, f32[2,5]{1,0:T(2,128)}, u32[]{:S(2)}) copy-start(f32[2,5]{1,0:T(2,128)} %fusion.40) | copy-start | bytes 124
  267.2 325.8 %reduce-scatter.14.cloned.1.call-start = ((), (), s32[]{:S(2)}) async-start(), calls=%async_computation.7 | async-start | bytes 16017408
  297.7 44.4 %slice-start.2 = ((s8[4718592]{0:T(1024)(128)(4,1)}), s8[524288]{0:T(1024)(128)(4,1)S(1)}, s32[]{:S(2)}) async-start(s8[4718592]{0:T(1024)(128)(4,1)} %bitcast.57), calls=%async_computation.10 | async-start | bytes 1048576
  301.1 41.1 %slice-start.3 = ((s8[4718592]{0:T(1024)(128)(4,1)}), s8[4194304]{0:T(1024)(128)(4,1)S(1)}, s32[]{:S(2)}) async-start(s8[4718592]{0:T(1024)(128)(4,1)} %bitcast.57), calls=%async_computation.11 | async-start | bytes 8388608
  328.7 13.5 %copy-start.39 = (f32[768]{0:T(1024)S(1)}, f32[768]{0:T(1024)}, u32[]{:S(2)}) copy-start(f32[768]{0:T(1024)} %copy-done.38) | copy-start | bytes 9220
  328.7 13.5 %copy-start.44 = (f32[768]{0:T(1024)S(1)}, f32[768]{0:T(1024)}, u32[]{:S(2)}) copy-start(f32[768]{0:T(1024)} %copy-done.43) | copy-start | bytes 9220
  406.7 13.1 %collective-permute-start.2 = (bf16[1536,384]{1,0:T(8,128)(2,1)S(1)}, bf16[1536,384]{1,0:T(8,128)(2,1)S(1)}, u32[]{:S(2)}, u32[]{:S(2)}) collective-permute-start(bf16[1536,384]{1,0:T(8,128)(2,1)S(1)} %get-tuple-element.223), channel_id=1, source_target_pairs={{0,1},{1,0},{2,3},{3,2},{4,5},{5,4},{6,7},{7,6},{8,9},{9,8},{10,11... | collective-permute-start | bytes 3538952 | tf_op jit(solution)/shard_map/ppermute | solution.py:669
  420.9 282.2 %reduce-scatter.12.cloned.1.call-start = ((), (), s32[]{:S(2)}) async-start(), calls=%async_computation.6 | async-start | bytes 3649536 | tf_op jit(solution)/shard_map/reduce_scatter | solution.py:786
  553.1 6.5 collective-permute-start.3
  627.3 13.5 %copy-start.19 = (f32[1,24,6144]{2,1,0:T(8,128)S(1)}, f32[1,24,6144]{2,1,0:T(8,128)}, u32[]{:S(2)}) copy-start(f32[1,24,6144]{2,1,0:T(8,128)} %param.26) | copy-start | bytes 1769476
  632.5 72.4 %copy-start.17 = (f32[1,24,6144]{2,1,0:T(8,128)}, f32[1,24,6144]{2,1,0:T(8,128)S(1)}, u32[]{:S(2)}) copy-start(f32[1,24,6144]{2,1,0:T(8,128)S(1)} %broadcast_in_dim_reshape.6) | copy-start | bytes 1769476
  632.7 70.4 %copy-start.26 = (f32[1,24,2304]{2,1,0:T(8,128)S(1)}, f32[1,24,2304]{2,1,0:T(8,128)}, u32[]{:S(2)}) copy-start(f32[1,24,2304]{2,1,0:T(8,128)} %param.24) | copy-start | bytes 663556
  632.8 72.1 %copy-start.25 = (f32[1,4,24,768]{3,2,1,0:T(8,128)}, f32[1,4,24,768]{3,2,1,0:T(8,128)S(1)}, u32[]{:S(2)}) copy-start(f32[1,4,24,768]{3,2,1,0:T(8,128)S(1)} %copy.122) | copy-start | bytes 884740
  633.4 71.5 %copy-start.40 = (f32[1,4,24]{2,1,0:T(4,128)}, f32[1,4,24]{2,1,0:T(4,128)S(1)}, u32[]{:S(2)}) copy-start(f32[1,4,24]{2,1,0:T(4,128)S(1)} %get-tuple-element.170) | copy-start | bytes 1156
  635.6 70.1 %copy-start.29 = (f32[1,24,768]{2,1,0:T(8,128)}, f32[1,24,768]{2,1,0:T(8,128)S(1)}, u32[]{:S(2)}) copy-start(f32[1,24,768]{2,1,0:T(8,128)S(1)} %get-tuple-element.180) | copy-start | bytes 221188
  635.6 69.4 %copy-start.32 = (f32[1,24,2304]{2,1,0:T(8,128)S(1)}, f32[1,24,2304]{2,1,0:T(8,128)}, u32[]{:S(2)}) copy-start(f32[1,24,2304]{2,1,0:T(8,128)} %param.34) | copy-start | bytes 663556
  635.6 70.1 %copy-start.1 = (bf16[256,384]{1,0:T(8,128)(2,1)S(1)}, bf16[256,384]{1,0:T(8,128)(2,1)}, u32[]{:S(2)}) copy-start(bf16[256,384]{1,0:T(8,128)(2,1)} %param.23) | copy-start | bytes 589828
  638.9 66.7 %copy-start.23 = (f32[1,96,768]{2,1,0:T(8,128)}, f32[1,96,768]{2,1,0:T(8,128)S(1)}, u32[]{:S(2)}) copy-start(f32[1,96,768]{2,1,0:T(8,128)S(1)} %get-tuple-element.174) | copy-start | bytes 884740
  642.9 62.8 %copy-start.18 = (f32[1,24,6144]{2,1,0:T(8,128)}, f32[1,24,6144]{2,1,0:T(8,128)S(1)}, u32[]{:S(2)}) copy-start(f32[1,24,6144]{2,1,0:T(8,128)S(1)} %get-tuple-element.177) | copy-start | bytes 1769476
  (44 other events, 284.6 us)
Sparse Core Ops, SparseCore 0:
  11.6 62.7 all-gather.5
  77.8 108.0 all-gather.3
  267.3 5.9 reduce-scatter.9
  419.9 173.0 reduce-scatter.13
  601.1 101.8 reduce-scatter.11

commit v3 on v2

--- a/solution.py
+++ b/solution.py
@@ -613,6 +613,154 @@
         name="attend_bwd",
     )(ctl,own,own,own,recv,recv,recv,d_own,d_recv,o_own,o_oth,lse,cos,sin)
 
+BLOCK=512
+
+def spread_mean(x):
+    return jnp.mean(x,axis=1,keepdims=True)
+
+def row_docs(ctl,block):
+    i=pl.program_id(0)
+    r=ctl[0]*(block*pl.num_programs(0))+i*block+lax.broadcasted_iota(jnp.int32,(block,1),0)
+    return (r>=ctl[1]).astype(jnp.int32)+(r>=ctl[2]).astype(jnp.int32)
+
+def ffn_fwd_kernel(ctl,ao,ax,tok,w_exp,w_con,w_out,norm,u1,u2,rs,yb,hb,pf,pooled):
+    block,width=tok.shape
+    hidden=hb.shape[1]
+    share=width//2
+    pos=ctl[0]
+    mine=pl.multiple_of(pos*share,share)
+    other=pl.multiple_of((1-pos)*share,share)
+    f=tok[...].astype(F32)+nn(ao[...],w_out[pl.ds(mine,share),:])+nn(ax[...],w_out[pl.ds(other,share),:])
+    cent=f-spread_mean(f)
+    scale=lax.rsqrt(spread_mean(cent*cent)+NORM_EPSILON)
+    unit=cent*scale
+    u1[...]=unit
+    rs[:,0:128]=jnp.broadcast_to(scale,(block,128))
+    y=unit*norm[0:1,:]+norm[1:2,:]
+    ylow=y.astype(BF)
+    yb[...]=ylow
+    acc=y
+    for c in range(hidden//width):
+        gc=slice(c*width,(c+1)*width)
+        uc=slice(hidden+c*width,hidden+(c+1)*width)
+        gate=nn(ylow,w_exp[:,gc])
+        up=nn(ylow,w_exp[:,uc])
+        sig=jax.nn.sigmoid(gate)
+        act=gate*sig
+        low=(act*up).astype(BF)
+        hb[:,gc]=low
+        pf[:,gc]=(up*sig*(1.0+gate*(1.0-sig))).astype(BF)
+        pf[:,uc]=act.astype(BF)
+        acc=acc+nn(low,w_con[:,gc])
+    cent=acc-spread_mean(acc)
+    scale=lax.rsqrt(spread_mean(cent*cent)+NORM_EPSILON)
+    unit=cent*scale
+    u2[...]=unit
+    rs[:,128:256]=jnp.broadcast_to(scale,(block,128))
+    out=unit*norm[2:3,:]+norm[3:4,:]
+    docs=row_docs(ctl,block)
+    @pl.when(pl.program_id(0)==0)
+    def _(): pooled[...]=jnp.zeros_like(pooled)
+    for d in range(2):
+        pooled[d:d+1,:]+=jnp.sum(jnp.where(docs==d,out,0.0),axis=0,keepdims=True)
+
+def ffn_fwd(ctl,ao,ax,tok,bundle,norm,hidden):
+    rows,width=tok.shape
+    row=lambda n: pl.BlockSpec((BLOCK,n),lambda i,c:(i,0))
+    held=lambda n,at: pl.BlockSpec((width,n),lambda i,c:(0,at//n),pipeline_mode=pl.Buffered(1))
+    flat=pl.BlockSpec((8,width),lambda i,c:(0,0))
+    return pl.pallas_call(ffn_fwd_kernel,
+        grid_spec=pltpu.PrefetchScalarGridSpec(num_scalar_prefetch=1,grid=(rows//BLOCK,),
+          in_specs=[row(width//2),row(width//2),row(width),held(2*hidden,0),held(hidden,2*hidden),held(width,3*hidden),flat],
+          out_specs=[row(width),row(width),row(256),row(width),row(hidden),row(2*hidden),flat]),
+        out_shape=[jax.ShapeDtypeStruct((rows,width),F32),jax.ShapeDtypeStruct((rows,width),F32),jax.ShapeDtypeStruct((rows,256),F32),
+          jax.ShapeDtypeStruct((rows,width),BF),jax.ShapeDtypeStruct((rows,hidden),BF),jax.ShapeDtypeStruct((rows,2*hidden),BF),
+          jax.ShapeDtypeStruct((8,width),F32)],
+        compiler_params=pltpu.CompilerParams(vmem_limit_bytes=60<<20,dimension_semantics=("arbitrary",)),
+        cost_estimate=pl.CostEstimate(flops=2*rows*width*(width+3*hidden),bytes_accessed=rows*(width*14+hidden*6)+2*width*(width+3*hidden),transcendentals=rows*hidden),
+        name="ffn_fwd",
+    )(ctl,ao,ax,tok,bundle,bundle,bundle,norm)
+
+def loss_grad(pool,targets,len0,len1):
+    width=pool.shape[1]
+    docs=lax.broadcasted_iota(jnp.int32,pool.shape,0)
+    length=jnp.where(docs==0,len0,len1)
+    emb=pool/length
+    lane=lax.broadcasted_iota(jnp.int32,pool.shape,1)
+    d_target=jnp.zeros_like(pool)
+    d_self=jnp.zeros_like(pool)
+    for cut in (width//12,width//6,width//3,2*width//3,width):
+        keep=lane<cut
+        total=lambda v: jnp.sum(jnp.where(keep,v,0.0),axis=1,keepdims=True)
+        own_root=lax.rsqrt(total(emb*emb)+COSINE_EPSILON)
+        other_root=lax.rsqrt(total(targets*targets)+COSINE_EPSILON)
+        cosine=total(emb*targets)*own_root*other_root
+        d_target=d_target+jnp.where(keep,own_root*other_root,0.0)
+        d_self=d_self+jnp.where(keep,cosine*own_root*own_root,0.0)
+    d_emb=length*(d_self*emb-d_target*targets)
+    return emb,d_emb/length
+
+def ffn_bwd_kernel(ctl,flen,pool_a,pool_b,targets,u1,u2,rs,pf,w_exp,w_con,w_out,norm,
+                   emb,mb,ub,df,ab,do,dx,gn,de):
+    block,width=u1.shape
+    hidden=pf.shape[1]//2
+    share=width//2
+    pos=ctl[0]
+    @pl.when(pl.program_id(0)==0)
+    def _():
+        e,d=loss_grad(pool_a[...]+pool_b[...],targets[...],flen[0],flen[1])
+        emb[...]=e
+        de[...]=d
+        gn[...]=jnp.zeros_like(gn)
+    docs=row_docs(ctl,block)
+    dout=jnp.where(docs==0,de[0:1,:],jnp.where(docs==1,de[1:2,:],0.0))
+    unit=u2[...]
+    gn[2:3,:]+=jnp.sum(dout*unit,axis=0,keepdims=True)
+    gn[3:4,:]+=jnp.sum(dout,axis=0,keepdims=True)
+    gu=dout*norm[2:3,:]
+    dg=rs[:,128:129]*(gu-spread_mean(gu)-unit*spread_mean(gu*unit))
+    mlow=dg.astype(BF)
+    mb[...]=mlow
+    acc=dg
+    for c in range(hidden//width):
+        gc=slice(c*width,(c+1)*width)
+        uc=slice(hidden+c*width,hidden+(c+1)*width)
+        dh=nt(mlow,w_con[:,gc])
+        dgate=(dh*pf[:,gc].astype(F32)).astype(BF)
+        dup=(dh*pf[:,uc].astype(F32)).astype(BF)
+        ub[:,gc]=dgate
+        ub[:,uc]=dup
+        acc=acc+nt(dgate,w_exp[:,gc])+nt(dup,w_exp[:,uc])
+    unit=u1[...]
+    gn[0:1,:]+=jnp.sum(acc*unit,axis=0,keepdims=True)
+    gn[1:2,:]+=jnp.sum(acc,axis=0,keepdims=True)
+    gu=acc*norm[0:1,:]
+    dfirst=rs[:,0:1]*(gu-spread_mean(gu)-unit*spread_mean(gu*unit))
+    df[...]=dfirst
+    alow=dfirst.astype(BF)
+    ab[...]=alow
+    do[...]=nt(alow,w_out[pl.ds(pl.multiple_of(pos*share,share),share),:]).astype(BF)
+    dx[...]=nt(alow,w_out[pl.ds(pl.multiple_of((1-pos)*share,share),share),:]).astype(BF)
+
+def ffn_bwd(ctl,flen,pool_a,pool_b,targets,u1,u2,rs,pf,bundle,norm):
+    rows,width=u1.shape
+    hidden=pf.shape[1]//2
+    row=lambda n: pl.BlockSpec((BLOCK,n),lambda i,c,l:(i,0))
+    held=lambda n,at: pl.BlockSpec((width,n),lambda i,c,l:(0,at//n),pipeline_mode=pl.Buffered(1))
+    flat=pl.BlockSpec((8,width),lambda i,c,l:(0,0))
+    sds=jax.ShapeDtypeStruct
+    return pl.pallas_call(ffn_bwd_kernel,
+        grid_spec=pltpu.PrefetchScalarGridSpec(num_scalar_prefetch=2,grid=(rows//BLOCK,),
+          in_specs=[flat,flat,flat,row(width),row(width),row(256),row(2*hidden),held(2*hidden,0),held(hidden,2*hidden),held(width,3*hidden),flat],
+          out_specs=[flat,row(width),row(2*hidden),row(width),row(width),row(width//2),row(width//2),flat],
+          scratch_shapes=[pltpu.VMEM((8,width),F32)]),
+        out_shape=[sds((8,width),F32),sds((rows,width),BF),sds((rows,2*hidden),BF),sds((rows,width),F32),sds((rows,width),BF),
+          sds((rows,width//2),BF),sds((rows,width//2),BF),sds((8,width),F32)],
+        compiler_params=pltpu.CompilerParams(vmem_limit_bytes=60<<20,dimension_semantics=("arbitrary",)),
+        cost_estimate=pl.CostEstimate(flops=2*rows*width*(width+3*hidden),bytes_accessed=rows*(width*18+hidden*8)+2*width*(width+3*hidden),transcendentals=0),
+        name="ffn_bwd",
+    )(ctl,flen,pool_a,pool_b,targets,u1,u2,rs,pf,bundle,bundle,bundle,norm)
+
 def mix_kernel(ctl,x,w,cos,sin,own,oth):
     pos=ctl[0]
     width=x.shape[1]
@@ -704,9 +852,6 @@
     at1=2*hidden_width
     at2=at1+per*model_width
     at3=at2+model_width
-    w_exp=bundle[:,0:at1]
-    w_con=[bundle[:,at1+j*model_width:at1+(j+1)*model_width] for j in range(per)]
-    w_out=bundle[:,at2:at3]
     w_norm=bundle[:,at3:].reshape(count,share_rows,128)[:,0:4,0:share_rows].transpose(1,0,2).reshape(4,model_width)
     lengths=doc_lengths[0]
     e0=lengths[0]
@@ -722,69 +867,25 @@
     sin=jnp.sin(angles)*jnp.where((lane%64)<32,-1.0,1.0)[None,:]
     cos_own=lax.dynamic_slice_in_dim(cos,pos*local_rows,local_rows,0)
     sin_own=lax.dynamic_slice_in_dim(sin,pos*local_rows,local_rows,0)
-    seg_rows=lax.dynamic_slice_in_dim(seg,pos*local_rows,local_rows,0)
-    stream=tokens.astype(F32)
     own,oth=mix(ctl,tokens,w_mix,cos_own,sin_own)
     recv=swap_cores(oth)
+    pick=(pair_index[:,None]==jnp.arange(target_bank.shape[0],dtype=jnp.int32)[None,:]).astype(BF)
+    some=matmul(pick,target_bank)
+    targets=jnp.pad(join(pos,some,swap_cores(some)),((0,6),(0,0)))
     o_own,o_oth,lse=attend_fwd(ctl,own,recv)
-    att_low=join(pos,o_own,swap_cores(o_oth))
-    norm_gains=w_norm.astype(F32)
-    first_sum=stream+matmul(att_low,w_out)
-    normed=normalize(first_sum,norm_gains[0],norm_gains[1])
-    y_low=normed.astype(BF)
-    gate_up=matmul(y_low,w_exp)
-    half=gate_up.shape[1]//2
-    hidden=(jax.nn.silu(gate_up[:,0:half])*gate_up[:,half:2*half]).astype(BF)
-    w_con=jnp.concatenate(w_con,0)
-    second_sum=normed+matmul(hidden,w_con)
-    final=normalize(second_sum,norm_gains[2],norm_gains[3])
-    member=(seg_rows[None,:]==jnp.arange(doc_count,dtype=jnp.int32)[:,None]).astype(F32)
-    partial_value=matmul_exact(member,final)
-    pooled=lax.psum_scatter(partial_value,"dim",scatter_dimension=1,tiled=True)
-    length_f=lengths.astype(F32)
-    embeddings=pooled/length_f[:,None]
-    share=embeddings.shape[1]
-    pick=(pair_index[:,None]==jnp.arange(target_bank.shape[0],dtype=jnp.int32)[None,:]).astype(BF)
-    targets=matmul(pick,target_bank)
-    feature_ids=pos*share+jnp.arange(share,dtype=jnp.int32)
-    cuts=jnp.array([model_width//12,model_width//6,model_width//3,2*model_width//3,model_width],dtype=jnp.int32)
-    masks=(feature_ids[None,:]<cuts[:,None]).astype(F32)
-    cross=matmul_exact(embeddings*targets,masks.T)
-    own_sq=matmul_exact(embeddings*embeddings,masks.T)
-    other=matmul_exact(targets*targets,masks.T)
-    cross,own_sq,other=lax.psum((cross,own_sq,other),"dim")
-    own_root=lax.rsqrt(own_sq+COSINE_EPSILON)
-    other_root=lax.rsqrt(other+COSINE_EPSILON)
-    cosine=cross*own_root*other_root
-    coef_target=-length_f[:,None]*own_root*other_root
-    coef_self=length_f[:,None]*cosine*own_root*own_root
-    grad_emb=matmul_exact(coef_target,masks)*targets+matmul_exact(coef_self,masks)*embeddings
-    grad_full=lax.all_gather(grad_emb,"dim",axis=1,tiled=True)
-    spread_rows=member/length_f[:,None]
-    grad_stream=lax.dot_general(spread_rows,grad_full,(((0,),(0,)),((),())),precision=PRECISE,preferred_element_type=F32)
-    grad_second,grad_gain2,grad_bias2=normalize_back(grad_stream,second_sum,norm_gains[2])
-    grad_m_low=grad_second.astype(BF)
+    o_recv=swap_cores(o_oth)
+    norm_gains=jnp.pad(w_norm.astype(F32),((0,4),(0,0)))
+    u1,u2,rs,y_low,hidden,factors,pooled=ffn_fwd(ctl,o_own,o_recv,tokens,bundle,norm_gains,hidden_width)
+    embeds,grad_m_low,grad_both,grad_first,grad_a_low,d_own,d_oth,grad_norm=ffn_bwd(
+        ctl,lengths.astype(F32),pooled,swap_cores(pooled),targets,u1,u2,rs,factors,bundle,norm_gains)
+    share=model_width//2
+    embeddings=lax.dynamic_slice(embeds,(0,pos*share),(doc_count,share))
+    d_recv=swap_cores(d_oth)
+    grad_exp=inner_rows(y_low,grad_both)
     grad_con=inner_rows(hidden,grad_m_low)
-    grad_hidden=inner_cols(grad_m_low,w_con)
-    gate_part=gate_up[:,0:half]
-    up_part=gate_up[:,half:2*half]
-    sigmoid_gate=jax.nn.sigmoid(gate_part)
-    activated=gate_part*sigmoid_gate
-    grad_gate=grad_hidden*up_part*sigmoid_gate*(1.0+gate_part*(1.0-sigmoid_gate))
-    grad_up=grad_hidden*activated
-    grad_both=jnp.concatenate([grad_gate,grad_up],axis=1).astype(BF)
-    grad_exp=inner_rows(y_low,grad_both)
-    grad_normed=grad_second+inner_cols(grad_both,w_exp)
-    grad_first,grad_gain1,grad_bias1=normalize_back(grad_normed,first_sum,norm_gains[0])
-    grad_a_low=grad_first.astype(BF)
-    grad_out=inner_rows(att_low,grad_a_low)
-    grad_attended=inner_cols(grad_a_low,w_out).astype(BF)
-    width=model_width//2
-    d_own=lax.dynamic_slice_in_dim(grad_attended,pos*width,width,1)
-    d_oth=lax.dynamic_slice_in_dim(grad_attended,(1-pos)*width,width,1)
-    d_recv=swap_cores(d_oth)
+    grad_out=join(pos,inner_rows(o_own,grad_a_low),inner_rows(o_recv,grad_a_low),0)
     scatter=lambda g: lax.psum_scatter(g,("dp","dim"),scatter_dimension=0,tiled=True).astype(F32)
-    grad_norm=jnp.stack([grad_gain1,grad_bias1,grad_gain2,grad_bias2]).reshape(4,count,share_rows).transpose(1,0,2)
+    grad_norm=grad_norm[0:4].reshape(4,count,share_rows).transpose(1,0,2)
     grad_norm=jnp.pad(grad_norm,((0,0),(0,share_rows-4),(0,128-share_rows))).reshape(model_width,128)
     fold_con=[grad_con[j*model_width:(j+1)*model_width].astype(BF) for j in range(per)]
     terms=jnp.concatenate([grad_exp.astype(BF),*fold_con,grad_out.astype(BF),grad_norm.astype(BF)],1)

time: 722 us -> 615 us (0.85)
  matrix products: 180 us -> 46.7 us
  Pallas kernels: 221 us -> 310 us
  other arithmetic: 63.9 us -> 37.1 us
  local copies, waits for them, and re-layouts: 85 us -> 59 us
    pallas_call x0 -> x2, Pallas kernels: none -> 88.8 us  [the longest x1 44.9 us: ffn_bwd(): pl.pallas_call(ffn_bwd_kernel, grid_spec=pltpu.PrefetchScalarGridSpec(num...]
    dot_general x4 -> x1, matrix products: 72 us -> 8.34 us  [inner_cols(): lax.dot_general(left_op, right_op, (((1,), (1,)), ((), ())), preferred_el...]
    dot_general x4 -> x1, matrix products: 47 us -> 0.18 us  [matmul(): return jnp.dot(left_op, right_op, preferred_element_type=jnp.float32)]
    convert_element_type x3 -> x1, other arithmetic: 17.9 us -> 0.51 us  [body(): lengths.astype(F32)]
    unnamed x159 -> x107, local copies, waits for them, and re-layouts: 48.4 us -> 32.6 us
    unnamed x7 -> x5, waiting for transfers between devices: 21.5 us -> 11.3 us
    dot_general x4 -> x5, matrix products: 48.2 us -> 38.2 us  [inner_rows(): lax.dot_general(left_op, right_op, (((0,), (0,)), ((), ())), preferred_el...]
    reduce_sum x3 -> x0, other arithmetic: 8.57 us -> none  [the longest x1 5.16 us: normalize_back(): return (grad_sum, jnp.sum(grad_in * unit, axis=0), jnp.sum(grad_in, axis=0))]
  transfers between devices with their start and end apart: 9 -> 10, of which waited for: 7 -> 7; matrix products, arithmetic and copies ran while one was open for 13% -> 19% of each run, Pallas kernels for 31% -> 44%
where the time goes in v3:
time: 615 us; the launch traced here: 609 us
  Pallas kernels  310 us (50%)
  waiting for transfers between devices  138 us (22%)
  local copies, waits for them, and re-layouts  59 us (10%)
  matrix products  46.7 us (8%)
  other arithmetic  37.1 us (6%)
  between operations  16.2 us (3%)
    pallas_call x1, Pallas kernels, attend_bwd(): pl.pallas_call(bwd_kernel, grid_spec=pltpu.PrefetchScalarGridSpec(num_sca...  133 us
    pallas_call x1, Pallas kernels, attend_fwd(): pl.pallas_call(fwd_kernel, grid_spec=pltpu.PrefetchScalarGridSpec(num_sca...  79.2 us
    reduce_scatter x1, waiting for transfers between devices, body(): lax.psum_scatter(g, ('dp', 'dim'), scatter_dimension=0, tiled=True)  62.3 us
    all_gather x1, waiting for transfers between devices, body(): lax.all_gather(w[0].astype(BF), ('dp', 'dim'), axis=axis, tiled=True)  45.2 us
    pallas_call x1, Pallas kernels, ffn_bwd(): pl.pallas_call(ffn_bwd_kernel, grid_spec=pltpu.PrefetchScalarGridSpec(num...  44.9 us
    pallas_call x1, Pallas kernels, ffn_fwd(): pl.pallas_call(ffn_fwd_kernel, grid_spec=pltpu.PrefetchScalarGridSpec(num...  44 us
    dot_general x5, matrix products, inner_rows(): lax.dot_general(left_op, right_op, (((0,), (0,)), ((), ())), preferred_el...  38.2 us
    unnamed x107, local copies, waits for them, and re-layouts  32.6 us
  transfers between devices with their start and end apart: 10, of which 7 were waited for; matrix products, arithmetic and copies ran while one was open for 19% of the time, Pallas kernels for 44%

profile of v3, /device:TPU:0, one launch (start us, length us, event | category | flops | bytes accessed | tf_op | source)
XLA Modules:
  0.0 609.1 jit_solution(8199238954172266480)
XLA Ops:
  11.2 2.5 convert_element_type.129
  14.1 3.0 reshape.134
  22.4 5.5 fusion.4
  29.2 45.2 %all-gather.6.cloned.1.call-done = bf16[1,768,2304]{2,1,0:T(8,128)(2,1)} async-done(((bf16[1,24,2304]{2,1,0:T(8,128)(2,1)}), bf16[1,768,2304]{2,1,0:T(8,128)(2,1)}) %all-gather.6.cloned.1.call-update) | async-done | bytes 3538960 | tf_op jit(solution)/shard_map/all_gather | solution.py:841
  74.3 2.0 copy-done.3
  78.0 9.3 %mix.1 = (bf16[1536,1152]{1,0:T(8,128)(2,1)S(1)}, bf16[1536,1152]{1,0:T(8,128)(2,1)S(1)}) custom-call(s32[3]{0:T(128)S(1)} %pad_add_fusion.ctl, bf16[1536,768]{1,0:T(8,128)(2,1)S(1)} %copy-done.5, bf16[768,2304]{1,0:T(8,128)(2,1)S(1)} %bitcast.54, f32[1536,128]{1,0:T(8,128)S(1)} %constant_dynamic-slice_fusion.2.cos, ...), custom_call_target="tpu_custom_call" | custom-call | flops 5435817984 | bytes 12976128 | tf_op jit(solution)/shard_map/mix/pallas_call | solution.py:789
  87.3 1.9 copy-done.7
  89.4 6.0 collective-permute-done.qr.kr.vr
  97.2 79.2 %attend_fwd.1 = (bf16[1536,384]{1,0:T(8,128)(2,1)}, bf16[1536,384]{1,0:T(8,128)(2,1)}, f32[3,8,3072]{2,1,0:T(8,128)}) custom-call(s32[3]{0:T(128)} %copy-done.2, bf16[1536,1152]{1,0:T(8,128)(2,1)} %copy-done.7, bf16[1536,1152]{1,0:T(8,128)(2,1)} %copy-done.7, bf16[1536,1152]{1,0:T(8,128)(2,1)} %copy-done.7, bf16[1536,1152]{1,0:T(8,128)(2,1)} %copy-done.30, ...), custom_call_target="tpu_custom_call" | custom-call | flops 7247757312 | bytes 17694720 | tf_op jit(solution)/shard_map/attend_fwd/pallas_call | solution.py:500
  177.7 8.2 %all-gather.4.cloned.1.call-done.w_exp.w_con.w_out = bf16[768,10112]{1,0:T(8,128)(2,1)} async-done(((bf16[24,10112]{1,0:T(8,128)(2,1)}), bf16[768,10112]{1,0:T(8,128)(2,1)}) %all-gather.4.cloned.1.call-update) | async-done | bytes 15532048 | tf_op jit(solution)/shard_map/all_gather | solution.py:851
  188.6 44.0 %ffn_fwd.1 = (f32[1536,768]{1,0:T(8,128)}, f32[1536,768]{1,0:T(8,128)}, f32[1536,256]{1,0:T(8,128)}, bf16[1536,768]{1,0:T(8,128)(2,1)}, bf16[1536,3072]{1,0:T(8,...) custom-call(s32[3]{0:T(128)} %copy-done.2, bf16[1536,384]{1,0:T(8,128)(2,1)} %get-tuple-element.56.ao.oo, ...), custom_call_target="tpu_custom_call" | custom-call | flops 23555211264 | bytes 60162048 | tf_op jit(solution)/shard_map/ffn_fwd/pallas_call | solution.py:672
  234.6 44.9 %ffn_bwd.1 = (f32[8,768]{1,0:T(8,128)}, bf16[1536,768]{1,0:T(8,128)(2,1)}, bf16[1536,6144]{1,0:T(8,128)(2,1)}, f32[1536,768]{1,0:T(8,128)}, bf16[1536,768]{1,0:T...) custom-call(s32[3]{0:T(128)} %copy-done.2, f32[2]{0:T(128)} %convert_bitcast_fusion.2.flen, ...), custom_call_target="tpu_custom_call" | custom-call | flops 23555211264 | bytes 74317824 | tf_op jit(solution)/shard_map/ffn_bwd/pallas_call | solution.py:752
  280.7 11.2 %convolution_convert_fusion.1 = bf16[3072,768]{1,0:T(8,128)(2,1)S(1)} fusion(bf16[1536,3072]{1,0:T(8,128)(2,1)} %get-tuple-element.67, bf16[1536,768]{1,0:T(8,128)(2,1)} %get-tuple-element.68), kind=kOutput, calls=%fused_computation.3 | convolution fusion | flops 7250116608 | bytes 16515072 | tf_op jit(solution)/shard_map/dot_general | solution.py:30
  292.0 17.1 %fusion = bf16[768,10112]{1,0:T(8,128)(2,1)} fusion(bf16[1536,768]{1,0:T(8,128)(2,1)S(1)} %copy-done.39, bf16[1536,6144]{1,0:T(8,128)(2,1)S(1)} %copy-done.38), kind=kOutput, calls=%fused_computation.1 | convolution fusion | flops 14500233216 | bytes 30670848 | tf_op jit(solution)/shard_map/dot_general | solution.py:30
  319.3 132.6 %attend_bwd.1 = (bf16[1536,1152]{1,0:T(8,128)(2,1)}, bf16[1536,1152]{1,0:T(8,128)(2,1)}) custom-call(s32[3]{0:T(128)} %copy-done.2, bf16[1536,1152]{1,0:T(8,128)(2,1)} %copy-done.7, bf16[1536,1152]{1,0:T(8,128)(2,1)} %copy-done.7, bf16[1536,1152]{1,0:T(8,128)(2,1)} %copy-done.7, bf16[1536,1152]{1,0:T(8,128)(2,1)} %copy-done.30, ...), custom_call_target="tpu_custom_call" | custom-call | flops 18119393280 | bytes 35389440 | tf_op jit(solution)/shard_map/attend_bwd/pallas_call | solution.py:603
  453.6 4.8 collective-permute-done.5
  465.0 2.6 copy-done.22
  467.6 2.1 copy-done.23
  469.7 7.6 %fusion.1 = bf16[768,2304]{0,1:T(8,128)(2,1)} fusion(bf16[1536,768]{1,0:T(8,128)(2,1)S(1)} %copy-done.6, bf16[1536,2304]{1,0:T(8,128)(2,1)S(1)} %slice_dynamic-update-slice_fusion.5, bf16[1536,2304]{1,0:T(8,128)(2,1)S(1)} %get-tuple-element.180, pred[]{:T(512)S(6)} %eq.45), kind=kOutput, calls=%fused_computation.5 | convolution fusion | flops 5441126400 | bytes 20054016 | tf_op jit(solution)/shard_map/dot_general | solution.py:30
  477.3 11.3 %reduce-scatter.9.cloned.1.call-done = bf16[24,10112]{1,0:T(8,128)(2,1)} async-done(((bf16[768,10112]{1,0:T(8,128)(2,1)}), bf16[24,10112]{1,0:T(8,128)(2,1)}) %reduce-scatter.9.cloned.1.call-update) | async-done | bytes 485392
  488.6 2.1 convert_element_type.143
  490.7 5.8 copy.100
  496.5 8.3 %fusion.2 = f32[1536,768]{1,0:T(8,128)S(1)} fusion(bf16[1536,2304]{1,0:T(8,128)(2,1)} %copy-done.23, bf16[1536,2304]{1,0:T(8,128)(2,1)} %copy-done.22, pred[]{:T(512)S(6)} %eq.45, bf16[1,768,2304]{2,1,0:T(8,128)(2,1)S(1)} %copy-done.4), kind=kOutput, calls=%fused_computation.6 | convolution fusion | flops 5439356928 | bytes 22413312 | tf_op jit(solution)/shard_map/dot_general | solution.py:36
  504.9 5.3 add.106
  512.0 3.3 reshape.138
  515.4 4.5 copy.97
  519.9 5.2 broadcast_in_dim_reshape.6
  529.2 2.0 fusion.21
  531.2 1.8 add_multiply_fusion.1
  534.1 2.2 add_multiply_fusion
  536.3 62.3 %reduce-scatter.7.cloned.1.call-done = bf16[24,2304]{1,0:T(8,128)(2,1)} async-done(((bf16[768,2304]{1,0:T(8,128)(2,1)}), bf16[24,2304]{1,0:T(8,128)(2,1)}) %reduce-scatter.7.cloned.1.call-update) | async-done | bytes 110608 | tf_op jit(solution)/shard_map/reduce_scatter | solution.py:887
  598.5 1.8 fusion.24
  (163 shorter events, 47.4 us)
Async XLA Ops:
  7.2 169.5 %copy-start = (bf16[256,384]{1,0:T(8,128)(2,1)S(1)}, bf16[256,384]{1,0:T(8,128)(2,1)}, u32[]{:S(2)}) copy-start(bf16[256,384]{1,0:T(8,128)(2,1)} %param.22) | copy-start | bytes 589828
  7.2 11.8 %copy-start.28 = (s32[1,2]{1,0:T(1,128)S(1)}, s32[1,2]{1,0:T(1,128)}, u32[]{:S(2)}) copy-start(s32[1,2]{1,0:T(1,128)} %param.20) | copy-start | bytes 28
  7.2 67.1 %all-gather.6.cloned.1.call-start = ((), (), s32[]{:S(2)}) async-start(), calls=%async_computation.3 | async-start | bytes 3649536 | tf_op jit(solution)/shard_map/all_gather | solution.py:841
  8.9 176.9 %all-gather.4.cloned.1.call-start = ((), (), s32[]{:S(2)}) async-start(), calls=%async_computation.2 | async-start | bytes 16017408 | tf_op jit(solution)/shard_map/all_gather | solution.py:851
  18.8 469.8 %reduce-scatter.9.cloned.1.call-start = ((), (), s32[]{:S(2)}) async-start(), calls=%async_computation.5 | async-start | bytes 16017408
  21.7 65.6 %copy-start.2 = (s32[3]{0:T(128)}, s32[3]{0:T(128)S(1)}, u32[]{:S(2)}) copy-start(s32[3]{0:T(128)S(1)} %pad_add_fusion.ctl) | copy-start | bytes 40
  27.9 59.4 %copy-start.9 = (f32[3072,128]{1,0:T(8,128)}, f32[3072,128]{1,0:T(8,128)S(1)}, u32[]{:S(2)}) copy-start(f32[3072,128]{1,0:T(8,128)S(1)} %get-tuple-element.210.sin) | copy-start | bytes 4718596
  89.2 6.2 %collective-permute-start = (bf16[1536,1152]{1,0:T(8,128)(2,1)S(1)}, bf16[1536,1152]{1,0:T(8,128)(2,1)S(1)}, u32[]{:S(2)}, u32[]{:S(2)}) collective-permute-start(bf16[1536,1152]{1,0:T(8,128)(2,1)S(1)} %get-tuple-element.55), channel_id=1, source_target_pairs={{0,1},{1,0},{2,3},{3,2},{4,5},{5,4},{6,7},{7,6},{8,9},{9,8},{10,11... | collective-permute-start | bytes 10616840 | tf_op jit(solution)/shard_map/ppermute | solution.py:817
  97.2 79.5 %copy-start.35 = (s32[2]{0:T(128)S(1)}, s32[2]{0:T(128)}, u32[]{:S(2)}) copy-start(s32[2]{0:T(128)} %param.21) | copy-start | bytes 28
  176.4 11.1 %collective-permute-start.1 = (bf16[1536,384]{1,0:T(8,128)(2,1)}, bf16[1536,384]{1,0:T(8,128)(2,1)S(1)}, u32[]{:S(2)}, u32[]{:S(2)}) collective-permute-start(bf16[1536,384]{1,0:T(8,128)(2,1)} %get-tuple-element.57.ox), channel_id=1, source_target_pairs={{0,1},{1,0},{2,3},{3,2},{4,5},{5,4},{6,7},{7,6},{8,9},{9,8},{10,11... | collective-permute-start | bytes 3538952 | tf_op jit(solution)/shard_map/ppermute | solution.py:817
  176.8 56.0 %collective-permute-start.3 = (f32[2,384]{1,0:T(2,128)S(1)}, f32[2,384]{1,0:T(2,128)S(1)}, u32[]{:S(2)}, u32[]{:S(2)}) collective-permute-start(f32[2,384]{1,0:T(2,128)S(1)} %fusion.10), channel_id=1, source_target_pairs={{0,1},{1,0},{2,3},{3,2},{4,5},{5,4},{6,7},{7,6},{8,9},{9,8},{10,11... | collective-permute-start | bytes 9224 | tf_op jit(solution)/shard_map/ppermute | solution.py:817
  232.5 1.5 collective-permute-start.2
  280.4 37.8 %collective-permute-start.4 = (bf16[1536,384]{1,0:T(8,128)(2,1)}, bf16[1536,384]{1,0:T(8,128)(2,1)S(1)}, u32[]{:S(2)}, u32[]{:S(2)}) collective-permute-start(bf16[1536,384]{1,0:T(8,128)(2,1)} %get-tuple-element.72), channel_id=1, source_target_pairs={{0,1},{1,0},{2,3},{3,2},{4,5},{5,4},{6,7},{7,6},{8,9},{9,8},{10,11... | collective-permute-start | bytes 3538952 | tf_op jit(solution)/shard_map/ppermute | solution.py:817
  280.7 11.2 %copy-start.38 = (bf16[1536,6144]{1,0:T(8,128)(2,1)S(1)}, bf16[1536,6144]{1,0:T(8,128)(2,1)}, u32[]{:S(2)}) copy-start(bf16[1536,6144]{1,0:T(8,128)(2,1)} %get-tuple-element.66) | copy-start | bytes 56623108
  280.7 11.2 %copy-start.39 = (bf16[1536,768]{1,0:T(8,128)(2,1)S(1)}, bf16[1536,768]{1,0:T(8,128)(2,1)}, u32[]{:S(2)}) copy-start(bf16[1536,768]{1,0:T(8,128)(2,1)} %get-tuple-element.65) | copy-start | bytes 7077892
  319.3 279.3 %reduce-scatter.7.cloned.1.call-start = ((), (), s32[]{:S(2)}) async-start(), calls=%async_computation.4 | async-start | bytes 3649536 | tf_op jit(solution)/shard_map/reduce_scatter | solution.py:887
  451.9 6.5 %collective-permute-start.5 = (bf16[1536,1152]{1,0:T(8,128)(2,1)}, bf16[1536,1152]{1,0:T(8,128)(2,1)S(1)}, u32[]{:S(2)}, u32[]{:S(2)}) collective-permute-start(bf16[1536,1152]{1,0:T(8,128)(2,1)} %get-tuple-element.77), channel_id=1, source_target_pairs={{0,1},{1,0},{2,3},{3,2},{4,5},{5,4},{6,7},{7,6},{8,9},{9,8},{10,11... | collective-permute-start | bytes 10616840 | tf_op jit(solution)/shard_map/ppermute | solution.py:817
  477.3 19.2 %copy-start.4 = (bf16[1,768,2304]{2,1,0:T(8,128)(2,1)S(1)}, bf16[1,768,2304]{2,1,0:T(8,128)(2,1)}, u32[]{:S(2)}) copy-start(bf16[1,768,2304]{2,1,0:T(8,128)(2,1)} %all-gather.6.cloned.1.call-done) | copy-start | bytes 10616836
  511.2 13.9 %copy-start.26 = (f32[1,4,24]{2,1,0:T(4,128)S(1)}, f32[1,4,24]{2,1,0:T(4,128)}, u32[]{:S(2)}) copy-start(f32[1,4,24]{2,1,0:T(4,128)} %param.27) | copy-start | bytes 1156
  511.2 13.9 %copy-start.29 = (f32[1,4,24]{2,1,0:T(4,128)S(1)}, f32[1,4,24]{2,1,0:T(4,128)}, u32[]{:S(2)}) copy-start(f32[1,4,24]{2,1,0:T(4,128)} %param.32) | copy-start | bytes 1156
  511.2 15.2 %copy-start.27 = (f32[1,4,24]{2,1,0:T(4,128)S(1)}, f32[1,4,24]{2,1,0:T(4,128)}, u32[]{:S(2)}) copy-start(f32[1,4,24]{2,1,0:T(4,128)} %param.37) | copy-start | bytes 1156
  511.2 15.7 %copy-start.20 = (f32[1,24,768]{2,1,0:T(8,128)S(1)}, f32[1,24,768]{2,1,0:T(8,128)}, u32[]{:S(2)}) copy-start(f32[1,24,768]{2,1,0:T(8,128)} %param.24) | copy-start | bytes 221188
  512.0 16.6 %copy-start.21 = (f32[1,24,768]{2,1,0:T(8,128)S(1)}, f32[1,24,768]{2,1,0:T(8,128)}, u32[]{:S(2)}) copy-start(f32[1,24,768]{2,1,0:T(8,128)} %param.34) | copy-start | bytes 221188
  515.4 86.8 %copy-start.1 = (bf16[256,384]{1,0:T(8,128)(2,1)S(1)}, bf16[256,384]{1,0:T(8,128)(2,1)}, u32[]{:S(2)}) copy-start(bf16[256,384]{1,0:T(8,128)(2,1)} %param.22) | copy-start | bytes 589828
  519.9 13.1 %copy-start.14 = (f32[1,24,6144]{2,1,0:T(8,128)S(1)}, f32[1,24,6144]{2,1,0:T(8,128)}, u32[]{:S(2)}) copy-start(f32[1,24,6144]{2,1,0:T(8,128)} %param.25) | copy-start | bytes 1769476
  519.9 13.1 %copy-start.18 = (f32[1,24,6144]{2,1,0:T(8,128)S(1)}, f32[1,24,6144]{2,1,0:T(8,128)}, u32[]{:S(2)}) copy-start(f32[1,24,6144]{2,1,0:T(8,128)} %param.30) | copy-start | bytes 1769476
  519.9 78.6 %copy-start.16 = (f32[1,24,2304]{2,1,0:T(8,128)S(1)}, f32[1,24,2304]{2,1,0:T(8,128)}, u32[]{:S(2)}) copy-start(f32[1,24,2304]{2,1,0:T(8,128)} %param.23) | copy-start | bytes 663556
  525.1 77.0 %copy-start.12 = (f32[1,24,6144]{2,1,0:T(8,128)}, f32[1,24,6144]{2,1,0:T(8,128)S(1)}, u32[]{:S(2)}) copy-start(f32[1,24,6144]{2,1,0:T(8,128)S(1)} %broadcast_in_dim_reshape.6) | copy-start | bytes 1769476
  526.4 75.7 %copy-start.24 = (f32[1,4,24]{2,1,0:T(4,128)}, f32[1,4,24]{2,1,0:T(4,128)S(1)}, u32[]{:S(2)}) copy-start(f32[1,4,24]{2,1,0:T(4,128)S(1)} %get-tuple-element.163) | copy-start | bytes 1156
  528.6 73.5 %copy-start.19 = (f32[1,24,768]{2,1,0:T(8,128)}, f32[1,24,768]{2,1,0:T(8,128)S(1)}, u32[]{:S(2)}) copy-start(f32[1,24,768]{2,1,0:T(8,128)S(1)} %get-tuple-element.173) | copy-start | bytes 221188
  531.2 70.9 %copy-start.15 = (f32[1,96,768]{2,1,0:T(8,128)}, f32[1,96,768]{2,1,0:T(8,128)S(1)}, u32[]{:S(2)}) copy-start(f32[1,96,768]{2,1,0:T(8,128)S(1)} %get-tuple-element.167) | copy-start | bytes 884740
  534.1 68.0 %copy-start.13 = (f32[1,24,6144]{2,1,0:T(8,128)}, f32[1,24,6144]{2,1,0:T(8,128)S(1)}, u32[]{:S(2)}) copy-start(f32[1,24,6144]{2,1,0:T(8,128)S(1)} %get-tuple-element.170) | copy-start | bytes 1769476
  (19 other events, 73.5 us)
Sparse Core Ops, SparseCore 0:
  11.5 62.7 all-gather.5
  77.8 107.9 all-gather.3
  318.3 170.1 reduce-scatter.8
  496.6 101.8 reduce-scatter.6

commit v4 on v3

--- a/solution.py
+++ b/solution.py
@@ -503,7 +503,7 @@
           out_specs=[pl.BlockSpec((half,128),lambda p,c:(0,p))]*2+[pl.BlockSpec((1,8,rows),lambda p,c:(p,0,0))],
           scratch_shapes=[pltpu.VMEM((rows+BK,256),BF),pltpu.VMEM((rows,256),BF),pltpu.VMEM((rows,256),BF),pltpu.VMEM((160,rows+BK),BF)]),
         out_shape=[jax.ShapeDtypeStruct((half,outw),BF)]*2+[jax.ShapeDtypeStruct((pairs,8,rows),F32)],
-        compiler_params=pltpu.CompilerParams(vmem_limit_bytes=56<<20,dimension_semantics=("arbitrary",)),
+        compiler_params=pltpu.CompilerParams(vmem_limit_bytes=60<<20,dimension_semantics=("arbitrary",)),
         cost_estimate=pl.CostEstimate(flops=4*rows*rows*64*2*pairs//2,bytes_accessed=10*half*width,transcendentals=rows*rows*pairs),
         name="attend_fwd",
     )(ctl,own,own,own,recv,recv,recv)
@@ -608,7 +608,7 @@
              pltpu.VMEM((rows+BK,128),BF),pltpu.VMEM((rows,128),BF),pltpu.VMEM((rows,128),BF),
              pltpu.VMEM((128,rows+BK),BF),pltpu.VMEM((16,rows),F32),pltpu.VMEM((rows+BK,128),F32),pltpu.VMEM((rows+BK,128),F32)]),
         out_shape=[jax.ShapeDtypeStruct((half,width),BF)]*2,
-        compiler_params=pltpu.CompilerParams(vmem_limit_bytes=56<<20,dimension_semantics=("arbitrary",)),
+        compiler_params=pltpu.CompilerParams(vmem_limit_bytes=60<<20,dimension_semantics=("arbitrary",)),
         cost_estimate=pl.CostEstimate(flops=10*rows*rows*64*2*pairs//2,bytes_accessed=20*half*width,transcendentals=rows*rows*pairs),
         name="attend_bwd",
     )(ctl,own,own,own,recv,recv,recv,d_own,d_recv,o_own,o_oth,lse,cos,sin)
@@ -761,6 +761,168 @@
         name="ffn_bwd",
     )(ctl,flen,pool_a,pool_b,targets,u1,u2,rs,pf,bundle,bundle,bundle,norm)
 
+MESH=pl.DeviceIdType.MESH
+
+def place():
+    dp=lax.axis_index("dp")
+    core=lax.axis_index("dim")
+    return dp//4,(dp//2)%2,dp%2,core
+
+def meet(z,y,x,core):
+    chip=lambda a,b,c: a*4+b*2+c
+    peers=[(chip(z,y,x),1-core),(chip(z,y,1-x),core),(chip(z,1-y,x),core)]
+    peers+=[(chip(lax.rem(z+k,4),y,x),core) for k in (1,2,3)]
+    barrier=pltpu.get_barrier_semaphore()
+    for peer in peers:
+        pl.semaphore_signal(barrier,inc=1,device_id=peer,device_id_type=MESH)
+    pl.semaphore_wait(barrier,len(peers))
+    return peers
+
+def lanes_of(cols):
+    tiles=cols//128
+    widths=[tiles-tiles//4*3]+[tiles//4]*3
+    widths=[widths[0],widths[2],widths[1],widths[3]]
+    widths=[5,5,4,4] if tiles==18 else widths
+    out=[]
+    at=0
+    for n,w in enumerate(widths):
+        out.append((at*128,w*128,n%2==0))
+        at+=w
+    return out
+
+def send(src,dst,sems,n,k,peer):
+    copy=pltpu.make_async_remote_copy(src_ref=src,dst_ref=dst,send_sem=sems[0].at[n,k],recv_sem=sems[1].at[n,k],device_id=peer,device_id_type=MESH)
+    copy.start()
+    return copy
+
+def gather_kernel(w,out,low,local,s_sem,r_sem):
+    z,y,x,core=place()
+    low[...]=w[...].astype(BF)
+    keep=pltpu.make_async_copy(low,out.at[z,y,x,core],local)
+    keep.start()
+    pair,xn,yn,z1,z2,z3=meet(z,y,x,core)
+    sems=(s_sem,r_sem)
+    lanes=lanes_of(w.shape[1])
+    every=[]
+    def go(n,k,peer,*index,src=None):
+        at,width,_=lanes[n]
+        dst=out.at[(*index,slice(None),pl.ds(at,width))]
+        if src is None: src=dst
+        copy=send(src,dst,sems,n,k,peer)
+        every.append(copy)
+        return copy
+    whole=slice(None)
+    first=[]
+    for n,(at,width,_) in enumerate(lanes):
+        piece=low.at[:,pl.ds(at,width)]
+        first.append([go(n,k,peer,z,y,x,core,src=piece) for k,peer in enumerate((z1,z2,z3))])
+    keep.wait()
+    second=[]
+    for n,(_,_,flip) in enumerate(lanes):
+        for copy in first[n]: copy.wait_recv()
+        second.append(go(n,3,yn if flip else xn,whole,y,x,core))
+        go(n,5,pair,whole,y,x,core)
+    third=[]
+    for n,(_,_,flip) in enumerate(lanes):
+        second[n].wait_recv()
+        if flip:
+            third.append(go(n,4,xn,whole,whole,x,core))
+            go(n,6,pair,whole,1-y,x,core)
+        else:
+            third.append(go(n,4,yn,whole,y,whole,core))
+            go(n,6,pair,whole,y,1-x,core)
+    for n,(_,_,flip) in enumerate(lanes):
+        third[n].wait_recv()
+        if flip: go(n,7,pair,whole,whole,1-x,core)
+        else: go(n,7,pair,whole,1-y,whole,core)
+    done=set(id(c) for c in second+third+[c for f in first for c in f])
+    for copy in every:
+        copy.wait_send()
+        if id(copy) not in done: copy.wait_recv()
+
+def ring_gather(w):
+    share,cols=w.shape
+    out=pl.pallas_call(gather_kernel,
+        in_specs=[pl.BlockSpec(memory_space=pltpu.VMEM)],
+        out_specs=pl.BlockSpec(memory_space=pl.ANY),
+        scratch_shapes=[pltpu.VMEM((share,cols),BF),pltpu.SemaphoreType.DMA,pltpu.SemaphoreType.DMA((4,8)),pltpu.SemaphoreType.DMA((4,8))],
+        out_shape=jax.ShapeDtypeStruct((4,2,2,2,share,cols),BF),
+        compiler_params=pltpu.CompilerParams(collective_id=1,has_side_effects=True,vmem_limit_bytes=16<<20),
+        cost_estimate=pl.CostEstimate(flops=0,bytes_accessed=64*share*cols*20,transcendentals=0),
+        name="comm_gather",
+    )(w)
+    return out.reshape(32*share,cols)
+
+def scatter_kernel(g,out,r0,b1,k1,r1,b2,k2,r2,b3,k3,r3,s_sem,r_sem):
+    z,y,x,core=place()
+    pair,xn,yn,z1,z2,z3=meet(z,y,x,core)
+    sems=(s_sem,r_sem)
+    lanes=lanes_of(out.shape[1])
+    span=[pl.ds(at,width) for at,width,_ in lanes]
+    every=[]
+    def go(n,k,peer,src,dst):
+        copy=send(src,dst,sems,n,k,peer)
+        every.append(copy)
+        return copy
+    n_lanes=range(len(lanes))
+    zero=[go(n,0,pair,g.at[:,1-core,:,span[n]],r0.at[:,:,span[n]]) for n in n_lanes]
+    def split1(n,iz,j,side):
+        row=iz*4+(j*2+side if lanes[n][2] else side*2+j)
+        c=span[n]
+        return g[row,core,:,c].astype(F32)+r0[row,:,c].astype(F32)
+    one=[]
+    for n in n_lanes:
+        flip=lanes[n][2]
+        side=x if flip else y
+        zero[n].wait_recv()
+        for iz in range(4):
+            for j in range(2):
+                b1[iz,j,:,span[n]]=split1(n,iz,j,1-side).astype(BF)
+        one.append(go(n,1,xn if flip else yn,b1.at[:,:,:,span[n]],r1.at[:,:,:,span[n]]))
+        for iz in range(4):
+            for j in range(2):
+                k1[iz,j,:,span[n]]=split1(n,iz,j,side)
+    two=[]
+    for n in n_lanes:
+        flip=lanes[n][2]
+        side=y if flip else x
+        c=span[n]
+        one[n].wait_recv()
+        for iz in range(4):
+            b2[iz,:,c]=(k1[iz,1-side,:,c]+r1[iz,1-side,:,c].astype(F32)).astype(BF)
+        two.append(go(n,2,yn if flip else xn,b2.at[:,:,c],r2.at[:,:,c]))
+        for iz in range(4):
+            k2[iz,:,c]=k1[iz,side,:,c]+r1[iz,side,:,c].astype(F32)
+    three=[]
+    for n in n_lanes:
+        c=span[n]
+        two[n].wait_recv()
+        for k in (1,2,3):
+            to=lax.rem(z+k,4)
+            b3[k-1,:,c]=(k2[to,:,c]+r2[to,:,c].astype(F32)).astype(BF)
+        three.append([go(n,2+k,(z1,z2,z3)[k-1],b3.at[k-1,:,c],r3.at[k-1,:,c]) for k in (1,2,3)])
+        k3[:,c]=k2[z,:,c]+r2[z,:,c].astype(F32)
+    for n in n_lanes:
+        c=span[n]
+        for copy in three[n]: copy.wait_recv()
+        out[:,c]=k3[:,c]+r3[0,:,c].astype(F32)+r3[1,:,c].astype(F32)+r3[2,:,c].astype(F32)
+    for copy in every: copy.wait_send()
+
+def ring_scatter(g):
+    rows,cols=g.shape
+    share=rows//32
+    v=lambda *s: pltpu.VMEM((*s,share,cols),BF)
+    f=lambda *s: pltpu.VMEM((*s,share,cols),F32)
+    return pl.pallas_call(scatter_kernel,
+        in_specs=[pl.BlockSpec(memory_space=pltpu.VMEM)],
+        out_specs=pl.BlockSpec(memory_space=pltpu.VMEM),
+        scratch_shapes=[v(16),v(4,2),f(4,2),v(4,2),v(4),f(4),v(4),v(3),f(),v(3),pltpu.SemaphoreType.DMA((4,6)),pltpu.SemaphoreType.DMA((4,6))],
+        out_shape=jax.ShapeDtypeStruct((share,cols),F32),
+        compiler_params=pltpu.CompilerParams(collective_id=2,has_side_effects=True,vmem_limit_bytes=40<<20),
+        cost_estimate=pl.CostEstimate(flops=0,bytes_accessed=64*share*cols*20,transcendentals=0),
+        name="comm_scatter",
+    )(g.reshape(16,2,share,cols))
+
 def mix_kernel(ctl,x,w,cos,sin,own,oth):
     pos=ctl[0]
     width=x.shape[1]
@@ -791,7 +953,7 @@
           in_specs=[row(width),pl.BlockSpec((width,cols),lambda i,c:(0,0)),row(128),row(128)],
           out_specs=[row(cols//2)]*2),
         out_shape=[jax.ShapeDtypeStruct((rows,cols//2),BF)]*2,
-        compiler_params=pltpu.CompilerParams(vmem_limit_bytes=40<<20,dimension_semantics=("arbitrary",)),
+        compiler_params=pltpu.CompilerParams(vmem_limit_bytes=60<<20,dimension_semantics=("arbitrary",)),
         cost_estimate=pl.CostEstimate(flops=2*rows*width*cols,bytes_accessed=2*(rows*width+width*cols+rows*cols),transcendentals=0),
         name="mix",
     )(ctl,x,w,cos,sin)
@@ -830,7 +992,7 @@
 
 def body(tokens,doc_lengths,pair_index,target_bank,mixer_in,mixer_out,expand,contract,norm_params,*rest):
     slices=lax.axis_size("dim")
-    if slices!=2 or doc_lengths.shape[1]!=2:
+    if slices!=2 or lax.axis_size("dp")!=16 or doc_lengths.shape[1]!=2:
         return body_general(tokens,doc_lengths,pair_index,target_bank,mixer_in,mixer_out,expand,contract,norm_params,*rest)
     (mixer_in_moment,mixer_out_moment,expand_moment,contract_moment,norm_moment,
      mixer_in_average,mixer_out_average,expand_average,contract_average,norm_average)=rest
@@ -838,8 +1000,7 @@
     group_rows=local_rows*slices
     pos=lax.axis_index("dim")
     doc_count=2
-    gather=lambda w,axis=0: lax.all_gather(w[0].astype(BF),("dp","dim"),axis=axis,tiled=True)
-    w_mix=gather(mixer_in)
+    w_mix=ring_gather(mixer_in[0])
     share_rows=mixer_out.shape[1]
     per=contract.shape[1]//share_rows
     count=model_width//share_rows
@@ -897,7 +1058,7 @@
     token_grads=grad_first+inner_cols(grad_mixed,w_mix)
     grad_mix=grad_mix.astype(BF)
     grad_mix,sums=lax.optimization_barrier((grad_mix,sums))
-    sum_mix=scatter(grad_mix)
+    sum_mix=ring_scatter(grad_mix)
     sum_exp=unshuffle(sums[:,0:at1],count,per,share_rows)
     sum_con=unfold_rows(sums[:,at1:at2],per,share_rows)
     sum_out=sums[:,at2:at3]

time: 615 us -> 551 us (0.90)
  waiting for transfers between devices: 138 us -> 12.5 us
  Pallas kernels: 310 us -> 373 us
    reduce_scatter x1 -> x0, waiting for transfers between devices: 62.3 us -> none  [body(): lax.psum_scatter(g, ('dp', 'dim'), scatter_dimension=0, tiled=True)]
    pallas_call x0 -> x2, Pallas kernels: none -> 59.7 us  [the longest x1 32.2 us: ring_gather(): pl.pallas_call(gather_kernel, in_specs=[pl.BlockSpec(memory_space=pltpu.V...]
    all_gather x1 -> x0, waiting for transfers between devices: 45.2 us -> none  [body(): lax.all_gather(w[0].astype(BF), ('dp', 'dim'), axis=axis, tiled=True)]
    unnamed x5 -> x3, waiting for transfers between devices: 11.3 us -> 0.6 us
    unnamed x107 -> x101, local copies, waits for them, and re-layouts: 32.6 us -> 22.5 us
    all_gather x1, waiting for transfers between devices: 8.17 us -> 0.01 us  [body(): bundle = lax.all_gather(bundle, ('dp', 'dim'), axis=0, tiled=True)]
  transfers between devices with their start and end apart: 10 -> 8, of which waited for: 7 -> 5; matrix products, arithmetic and copies ran while one was open for 19% -> 14% of each run, Pallas kernels for 44% -> 55%
where the time goes in v4:
time: 551 us; the launch traced here: 545 us
  Pallas kernels  373 us (68%)
  local copies, waits for them, and re-layouts  60.7 us (11%)
  matrix products  47 us (9%)
  other arithmetic  33.5 us (6%)
  between operations  16.5 us (3%)
  waiting for transfers between devices  12.5 us (2%)
    pallas_call x1, Pallas kernels, attend_bwd(): pl.pallas_call(bwd_kernel, grid_spec=pltpu.PrefetchScalarGridSpec(num_sca...  132 us
    pallas_call x1, Pallas kernels, attend_fwd(): pl.pallas_call(fwd_kernel, grid_spec=pltpu.PrefetchScalarGridSpec(num_sca...  79.2 us
    pallas_call x1, Pallas kernels, ffn_bwd(): pl.pallas_call(ffn_bwd_kernel, grid_spec=pltpu.PrefetchScalarGridSpec(num...  44.8 us
    pallas_call x1, Pallas kernels, ffn_fwd(): pl.pallas_call(ffn_fwd_kernel, grid_spec=pltpu.PrefetchScalarGridSpec(num...  43.9 us
    dot_general x5, matrix products, inner_rows(): lax.dot_general(left_op, right_op, (((0,), (0,)), ((), ())), preferred_el...  38.6 us
    pallas_call x1, Pallas kernels, ring_gather(): pl.pallas_call(gather_kernel, in_specs=[pl.BlockSpec(memory_space=pltpu.V...  32.2 us
    pallas_call x1, Pallas kernels, ring_scatter(): pl.pallas_call(scatter_kernel, in_specs=[pl.BlockSpec(memory_space=pltpu....  27.6 us
    unnamed x101, local copies, waits for them, and re-layouts  22.5 us
  transfers between devices with their start and end apart: 8, of which 5 were waited for; matrix products, arithmetic and copies ran while one was open for 14% of the time, Pallas kernels for 55%

profile of v4, /device:TPU:0, one launch (start us, length us, event | category | flops | bytes accessed | tf_op | source)
XLA Modules:
  0.0 545.1 jit_solution(8068337613842318664)
XLA Ops:
  11.1 2.5 convert_element_type.120
  15.2 3.3 reshape.140
  19.6 32.2 %comm_gather.1 = bf16[4,2,2,2,24,2304]{5,4,3,2,1,0:T(8,128)(2,1)S(1)} custom-call(f32[24,2304]{1,0:T(8,128)S(1)} %bitcast.56), custom_call_target="tpu_custom_call" | custom-call | bytes 70778880 | tf_op jit(solution)/shard_map/comm_gather/pallas_call | solution.py:845
  51.8 1.8 copy-done.2
  57.4 5.5 %fusion.4 = (f32[3072,128]{1,0:T(8,128)S(1)}, f32[3072,128]{1,0:T(8,128)S(1)}) fusion(f32[128]{0:T(128)S(1)} %get-tuple-element.132, f32[128]{0:T(128)S(1)} %get-tuple-element.133, f32[3072]{0:T(1024)S(1)} %subtract_convert_fusion), kind=kLoop, calls=%fused_computation.11 | loop fusion | flops 786432 | bytes 3159040 | tf_op jit(solution)/shard_map/mul | solution.py:1028
  65.1 12.8 %mix.1 = (bf16[1536,1152]{1,0:T(8,128)(2,1)}, bf16[1536,1152]{1,0:T(8,128)(2,1)}) custom-call(s32[3]{0:T(128)} %pad_add_fusion.ctl, bf16[1536,768]{1,0:T(8,128)(2,1)} %tok.1, bf16[768,2304]{1,0:T(8,128)(2,1)} %bitcast.53, f32[1536,128]{1,0:T(8,128)} %constant_dynamic-slice_fusion.2.cos, f32[1536,128]{1,0:T(8,128)} %constant_dynamic-slice_fusion.1.sin), custom_call_target="tpu_custom_call" | custom-call | flops 5435817984 | bytes 12976128 | tf_op jit(solution)/shard_map/mix/pallas_call | solution.py:951
  78.2 6.3 %collective-permute-done.qr.kr.vr = bf16[1536,1152]{1,0:T(8,128)(2,1)} collective-permute-done((bf16[1536,1152]{1,0:T(8,128)(2,1)}, bf16[1536,1152]{1,0:T(8,128)(2,1)}, u32[]{:S(2)}, u32[]{:S(2)}) %collective-permute-start) | collective-permute-done | bytes 3538976 | tf_op jit(solution)/shard_map/ppermute | solution.py:979
  84.5 79.2 %attend_fwd.1 = (bf16[1536,384]{1,0:T(8,128)(2,1)}, bf16[1536,384]{1,0:T(8,128)(2,1)}, f32[3,8,3072]{2,1,0:T(8,128)}) custom-call(s32[3]{0:T(128)} %pad_add_fusion.ctl, bf16[1536,1152]{1,0:T(8,128)(2,1)} %get-tuple-element.54.qo.ko.vo, bf16[1536,1152]{1,0:T(8,128)(2,1)} %get-tuple-element.54.qo.ko.vo, bf16[1536,1152]{1,0:T(8,128)(2,1)} %get-tuple-element.54.qo.ko.vo, ...), custom_call_target="tpu_custom_call" | custom-call | flops 7247757312 | bytes 17694720 | tf_op jit(solution)/shard_map/attend_fwd/pallas_call | solution.py:500
  167.8 43.9 %ffn_fwd.1 = (f32[1536,768]{1,0:T(8,128)}, f32[1536,768]{1,0:T(8,128)}, f32[1536,256]{1,0:T(8,128)}, bf16[1536,768]{1,0:T(8,128)(2,1)}, bf16[1536,3072]{1,0:T(8,...) custom-call(s32[3]{0:T(128)} %pad_add_fusion.ctl, bf16[1536,384]{1,0:T(8,128)(2,1)} %get-tuple-element.56.ao.oo, ...), custom_call_target="tpu_custom_call" | custom-call | flops 23555211264 | bytes 60162048 | tf_op jit(solution)/shard_map/ffn_fwd/pallas_call | solution.py:672
  213.8 44.8 %ffn_bwd.1 = (f32[8,768]{1,0:T(8,128)}, bf16[1536,768]{1,0:T(8,128)(2,1)}, bf16[1536,6144]{1,0:T(8,128)(2,1)}, f32[1536,768]{1,0:T(8,128)}, bf16[1536,768]{1,0:T...) custom-call(s32[3]{0:T(128)} %pad_add_fusion.ctl, ...), custom_call_target="tpu_custom_call" | custom-call | flops 23555211264 | bytes 74317824 | tf_op jit(solution)/shard_map/ffn_bwd/pallas_call | solution.py:752
  259.9 11.2 %convolution_convert_fusion.1 = bf16[3072,768]{1,0:T(8,128)(2,1)S(1)} fusion(bf16[1536,3072]{1,0:T(8,128)(2,1)} %get-tuple-element.67, bf16[1536,768]{1,0:T(8,128)(2,1)} %get-tuple-element.68), kind=kOutput, calls=%fused_computation.3 | convolution fusion | flops 7250116608 | bytes 16515072 | tf_op jit(solution)/shard_map/dot_general | solution.py:30
  271.2 17.2 %fusion = bf16[768,10112]{1,0:T(8,128)(2,1)} fusion(bf16[1536,768]{1,0:T(8,128)(2,1)S(1)} %copy-done.34, bf16[1536,6144]{1,0:T(8,128)(2,1)S(1)} %copy-done.33), kind=kOutput, calls=%fused_computation.1 | convolution fusion | flops 14500233216 | bytes 30670848 | tf_op jit(solution)/shard_map/dot_general | solution.py:30
  298.9 132.4 %attend_bwd.1 = (bf16[1536,1152]{1,0:T(8,128)(2,1)}, bf16[1536,1152]{1,0:T(8,128)(2,1)}) custom-call(s32[3]{0:T(128)} %pad_add_fusion.ctl, bf16[1536,1152]{1,0:T(8,128)(2,1)} %get-tuple-element.54.qo.ko.vo, bf16[1536,1152]{1,0:T(8,128)(2,1)} %get-tuple-element.54.qo.ko.vo, bf16[1536,1152]{1,0:T(8,128)(2,1)} %get-tuple-element.54.qo.ko.vo, ...), custom_call_target="tpu_custom_call" | custom-call | flops 18119393280 | bytes 35389440 | tf_op jit(solution)/shard_map/attend_bwd/pallas_call | solution.py:603
  432.8 5.0 collective-permute-done.5
  444.4 3.2 copy-done.18
  447.5 8.2 %fusion.2 = f32[1536,768]{1,0:T(8,128)S(1)} fusion(bf16[768,2304]{1,0:T(8,128)(2,1)S(1)} %bitcast.54, bf16[1536,2304]{1,0:T(8,128)(2,1)} %copy-done.18, bf16[1536,2304]{1,0:T(8,128)(2,1)S(1)} %get-tuple-element.98, pred[]{:T(512)S(6)} %eq.45), kind=kOutput, calls=%fused_computation.6 | convolution fusion | flops 5439356928 | bytes 22413312 | tf_op jit(solution)/shard_map/dot_general | solution.py:36
  455.8 3.0 add.104
  458.8 1.7 copy-done.19
  461.2 8.0 %fusion.1 = bf16[768,2304]{0,1:T(8,128)(2,1)} fusion(bf16[1536,768]{1,0:T(8,128)(2,1)S(1)} %copy-done.25, bf16[1536,2304]{1,0:T(8,128)(2,1)S(1)} %copy-done.19, bf16[1536,2304]{1,0:T(8,128)(2,1)S(1)} %get-tuple-element.98, pred[]{:T(512)S(6)} %eq.45), kind=kOutput, calls=%fused_computation.5 | convolution fusion | flops 5441126400 | bytes 20054016 | tf_op jit(solution)/shard_map/dot_general | solution.py:30
  469.7 2.1 convert_element_type.134
  471.8 1.7 slice.145
  473.5 1.9 slice.144
  475.4 4.3 copy.67
  479.7 27.6 %comm_scatter.1 = f32[24,2304]{1,0:T(8,128)S(1)} custom-call(bf16[16,2,24,2304]{3,2,1,0:T(8,128)(2,1)S(1)} %bitcast.52), custom_call_target="tpu_custom_call" | custom-call | bytes 70778880 | tf_op jit(solution)/shard_map/comm_scatter/pallas_call | solution.py:916
  509.2 1.6 fusion.22
  512.8 2.0 fusion.23
  514.8 3.3 reshape.145
  518.1 4.5 copy.68
  522.6 5.5 %broadcast_in_dim_reshape.6 = f32[1,24,6144]{2,1,0:T(8,128)S(1)} reshape(f32[24,2,32,4,24]{4,3,2,1,0:T(4,128)} %copy.68) | data formatting | bytes 1179648 | tf_op jit(solution)/shard_map/broadcast_in_dim;reshape | solution.py:1069
  529.5 1.8 add_multiply_fusion.2
  531.2 2.0 fusion.20
  533.2 1.8 add_multiply_fusion.1
  (153 shorter events, 46.4 us)
Async XLA Ops:
  7.2 156.9 %copy-start = (bf16[256,384]{1,0:T(8,128)(2,1)S(1)}, bf16[256,384]{1,0:T(8,128)(2,1)}, u32[]{:S(2)}) copy-start(bf16[256,384]{1,0:T(8,128)(2,1)} %param.22) | copy-start | bytes 589828
  7.2 12.4 %copy-start.6 = (f32[1,24,2304]{2,1,0:T(8,128)S(1)}, f32[1,24,2304]{2,1,0:T(8,128)}, u32[]{:S(2)}) copy-start(f32[1,24,2304]{2,1,0:T(8,128)} %param.23) | copy-start | bytes 663556
  7.2 46.4 %copy-start.23 = (s32[1,2]{1,0:T(1,128)S(1)}, s32[1,2]{1,0:T(1,128)}, u32[]{:S(2)}) copy-start(s32[1,2]{1,0:T(1,128)} %param.20) | copy-start | bytes 28
  7.2 157.7 %all-gather.2.cloned.1.call-start = ((), (), s32[]{:S(2)}) async-start(), calls=%async_computation.1 | async-start | bytes 16017408 | tf_op jit(solution)/shard_map/all_gather | solution.py:1012
  19.3 450.4 %reduce-scatter.4.cloned.1.call-start = ((), (), s32[]{:S(2)}) async-start(), calls=%async_computation.2 | async-start | bytes 16017408
  62.9 14.9 %copy-start.7 = (f32[3072,128]{1,0:T(8,128)}, f32[3072,128]{1,0:T(8,128)S(1)}, u32[]{:S(2)}) copy-start(f32[3072,128]{1,0:T(8,128)S(1)} %get-tuple-element.128.sin) | copy-start | bytes 4718596
  63.0 14.9 %copy-start.8 = (f32[3072,128]{1,0:T(8,128)}, f32[3072,128]{1,0:T(8,128)S(1)}, u32[]{:S(2)}) copy-start(f32[3072,128]{1,0:T(8,128)S(1)} %get-tuple-element.129.cos) | copy-start | bytes 4718596
  77.8 6.6 %collective-permute-start = (bf16[1536,1152]{1,0:T(8,128)(2,1)}, bf16[1536,1152]{1,0:T(8,128)(2,1)}, u32[]{:S(2)}, u32[]{:S(2)}) collective-permute-start(bf16[1536,1152]{1,0:T(8,128)(2,1)} %get-tuple-element.55), channel_id=1, source_target_pairs={{0,1},{1,0},{2,3},{3,2},{4,5},{5,4},{6,7},{7,6},{8,9},{9,8},{10,11... | collective-permute-start | bytes 10616840 | tf_op jit(solution)/shard_map/ppermute | solution.py:979
  84.5 79.6 %copy-start.30 = (s32[2]{0:T(128)S(1)}, s32[2]{0:T(128)}, u32[]{:S(2)}) copy-start(s32[2]{0:T(128)} %param.21) | copy-start | bytes 28
  163.7 3.1 collective-permute-start.1
  164.2 47.9 %collective-permute-start.3 = (f32[2,384]{1,0:T(2,128)S(1)}, f32[2,384]{1,0:T(2,128)S(1)}, u32[]{:S(2)}, u32[]{:S(2)}) collective-permute-start(f32[2,384]{1,0:T(2,128)S(1)} %fusion.10), channel_id=1, source_target_pairs={{0,1},{1,0},{2,3},{3,2},{4,5},{5,4},{6,7},{7,6},{8,9},{9,8},{10,11... | collective-permute-start | bytes 9224 | tf_op jit(solution)/shard_map/ppermute | solution.py:979
  211.8 1.5 collective-permute-start.2
  259.6 38.2 %collective-permute-start.4 = (bf16[1536,384]{1,0:T(8,128)(2,1)}, bf16[1536,384]{1,0:T(8,128)(2,1)S(1)}, u32[]{:S(2)}, u32[]{:S(2)}) collective-permute-start(bf16[1536,384]{1,0:T(8,128)(2,1)} %get-tuple-element.72), channel_id=1, source_target_pairs={{0,1},{1,0},{2,3},{3,2},{4,5},{5,4},{6,7},{7,6},{8,9},{9,8},{10,11... | collective-permute-start | bytes 3538952 | tf_op jit(solution)/shard_map/ppermute | solution.py:979
  259.9 11.2 %copy-start.33 = (bf16[1536,6144]{1,0:T(8,128)(2,1)S(1)}, bf16[1536,6144]{1,0:T(8,128)(2,1)}, u32[]{:S(2)}) copy-start(bf16[1536,6144]{1,0:T(8,128)(2,1)} %get-tuple-element.66) | copy-start | bytes 56623108
  259.9 11.2 %copy-start.34 = (bf16[1536,768]{1,0:T(8,128)(2,1)S(1)}, bf16[1536,768]{1,0:T(8,128)(2,1)}, u32[]{:S(2)}) copy-start(bf16[1536,768]{1,0:T(8,128)(2,1)} %get-tuple-element.65) | copy-start | bytes 7077892
  431.3 6.5 %collective-permute-start.5 = (bf16[1536,1152]{1,0:T(8,128)(2,1)}, bf16[1536,1152]{1,0:T(8,128)(2,1)S(1)}, u32[]{:S(2)}, u32[]{:S(2)}) collective-permute-start(bf16[1536,1152]{1,0:T(8,128)(2,1)} %get-tuple-element.77), channel_id=1, source_target_pairs={{0,1},{1,0},{2,3},{3,2},{4,5},{5,4},{6,7},{7,6},{8,9},{9,8},{10,11... | collective-permute-start | bytes 10616840 | tf_op jit(solution)/shard_map/ppermute | solution.py:979
  431.4 10.9 %copy-start.9 = (bf16[1536,1152]{1,0:T(8,128)(2,1)S(1)}, bf16[1536,1152]{1,0:T(8,128)(2,1)}, u32[]{:S(2)}) copy-start(bf16[1536,1152]{1,0:T(8,128)(2,1)} %get-tuple-element.76) | copy-start | bytes 10616836
  443.8 11.9 %slice-start = ((s8[4718592]{0:T(1024)(128)(4,1)}), s8[4194304]{0:T(1024)(128)(4,1)S(1)}, s32[]{:S(2)}) async-start(s8[4718592]{0:T(1024)(128)(4,1)} %bitcast.59), calls=%async_computation.3 | async-start | bytes 8388608
  447.5 8.2 %slice-start.1 = ((s8[4718592]{0:T(1024)(128)(4,1)}), s8[524288]{0:T(1024)(128)(4,1)S(1)}, s32[]{:S(2)}) async-start(s8[4718592]{0:T(1024)(128)(4,1)} %bitcast.59), calls=%async_computation.4 | async-start | bytes 1048576
  455.8 5.4 copy-start.25
  469.1 38.8 %copy-start.21 = (f32[1,4,24]{2,1,0:T(4,128)S(1)}, f32[1,4,24]{2,1,0:T(4,128)}, u32[]{:S(2)}) copy-start(f32[1,4,24]{2,1,0:T(4,128)} %param.27) | copy-start | bytes 1156
  469.1 38.8 %copy-start.24 = (f32[1,4,24]{2,1,0:T(4,128)S(1)}, f32[1,4,24]{2,1,0:T(4,128)}, u32[]{:S(2)}) copy-start(f32[1,4,24]{2,1,0:T(4,128)} %param.32) | copy-start | bytes 1156
  509.2 18.9 %copy-start.20 = (f32[1,4,24]{2,1,0:T(4,128)}, f32[1,4,24]{2,1,0:T(4,128)S(1)}, u32[]{:S(2)}) copy-start(f32[1,4,24]{2,1,0:T(4,128)S(1)} %get-tuple-element.172) | copy-start | bytes 1156
  510.9 17.9 %copy-start.16 = (f32[1,24,768]{2,1,0:T(8,128)}, f32[1,24,768]{2,1,0:T(8,128)S(1)}, u32[]{:S(2)}) copy-start(f32[1,24,768]{2,1,0:T(8,128)S(1)} %get-tuple-element.169) | copy-start | bytes 221188
  514.8 13.4 %copy-start.22 = (f32[1,4,24]{2,1,0:T(4,128)S(1)}, f32[1,4,24]{2,1,0:T(4,128)}, u32[]{:S(2)}) copy-start(f32[1,4,24]{2,1,0:T(4,128)} %param.37) | copy-start | bytes 1156
  514.8 14.0 %copy-start.17 = (f32[1,24,768]{2,1,0:T(8,128)S(1)}, f32[1,24,768]{2,1,0:T(8,128)}, u32[]{:S(2)}) copy-start(f32[1,24,768]{2,1,0:T(8,128)} %param.34) | copy-start | bytes 221188
  518.1 19.6 %copy-start.1 = (bf16[256,384]{1,0:T(8,128)(2,1)S(1)}, bf16[256,384]{1,0:T(8,128)(2,1)}, u32[]{:S(2)}) copy-start(bf16[256,384]{1,0:T(8,128)(2,1)} %param.22) | copy-start | bytes 589828
  522.6 12.4 %copy-start.12 = (f32[1,24,6144]{2,1,0:T(8,128)S(1)}, f32[1,24,6144]{2,1,0:T(8,128)}, u32[]{:S(2)}) copy-start(f32[1,24,6144]{2,1,0:T(8,128)} %param.25) | copy-start | bytes 1769476
  522.6 12.4 %copy-start.14 = (f32[1,24,6144]{2,1,0:T(8,128)S(1)}, f32[1,24,6144]{2,1,0:T(8,128)}, u32[]{:S(2)}) copy-start(f32[1,24,6144]{2,1,0:T(8,128)} %param.30) | copy-start | bytes 1769476
  522.6 13.4 %copy-start.15 = (f32[1,24,6144]{2,1,0:T(8,128)S(1)}, f32[1,24,6144]{2,1,0:T(8,128)}, u32[]{:S(2)}) copy-start(f32[1,24,6144]{2,1,0:T(8,128)} %param.35) | copy-start | bytes 1769476
  522.6 14.4 %copy-start.5 = (f32[24,2304]{1,0:T(8,128)S(1)}, f32[24,2304]{1,0:T(8,128)}, u32[]{:S(2)}) copy-start(f32[24,2304]{1,0:T(8,128)} %copy-done.4) | copy-start | bytes 663556
  528.1 9.6 %copy-start.10 = (f32[1,24,6144]{2,1,0:T(8,128)}, f32[1,24,6144]{2,1,0:T(8,128)S(1)}, u32[]{:S(2)}) copy-start(f32[1,24,6144]{2,1,0:T(8,128)S(1)} %broadcast_in_dim_reshape.6) | copy-start | bytes 1769476
  (13 other events, 39.2 us)
Sparse Core Ops, SparseCore 0:
  19.5 113.3 all-gather.1
  297.9 171.7 reduce-scatter.3

commit v5 on v4

--- a/solution.py
+++ b/solution.py
@@ -508,7 +508,7 @@
         name="attend_fwd",
     )(ctl,own,own,own,recv,recv,recv)
 
-def bwd_kernel(ctl,qo,ko,vo,qr,kr,vr,do_o,do_r,oo,ox,lse,cos,sin,go,gx,kaug,q0,q1,vs,d0,d1,kt,delta,dk,dv):
+def bwd_kernel(ctl,qo,ko,vo,qr,kr,vr,do_o,do_r,oo,ox,lse,cos,sin,g0,g1,g2,x0,x1,x2,kaug,q0,q1,vs,d0,d1,kt,delta,dk,dv):
     rows=kaug.shape[0]-BK
     half=rows//2
     pos,e0,e1=ctl[0],ctl[1],ctl[2]
@@ -545,9 +545,9 @@
     def spread(i,col,val):
         local=i*ROWS-pos*half
         @pl.when((local>=0)&(local<half))
-        def _(): go[pl.ds(pl.multiple_of(local,ROWS),ROWS),col*128:(col+1)*128]=val
+        def _(): (g0,g1,g2)[col][pl.ds(pl.multiple_of(local,ROWS),ROWS),:]=val
         @pl.when((local<0)|(local>=half))
-        def _(): gx[pl.ds(pl.multiple_of(i*ROWS-(1-pos)*half,ROWS),ROWS),col*128:(col+1)*128]=val
+        def _(): (x0,x1,x2)[col][pl.ds(pl.multiple_of(i*ROWS-(1-pos)*half,ROWS),ROWS),:]=val
     def unturn(x,r0):
         ln=lax.broadcasted_iota(jnp.int32,x.shape,1)
         swapped=jnp.where((ln%64)<32,pltpu.roll(x,96,1),pltpu.roll(x,32,1))
@@ -603,11 +603,11 @@
     return pl.pallas_call(bwd_kernel,
         grid_spec=pltpu.PrefetchScalarGridSpec(num_scalar_prefetch=1,grid=(pairs,),
           in_specs=sp+sp+[one]*4+[pl.BlockSpec((1,8,rows),lambda p,c:(p,0,0)),full,full],
-          out_specs=[pl.BlockSpec((half,384),lambda p,c:(0,p))]*2,
+          out_specs=[one]*6,
           scratch_shapes=[pltpu.VMEM((rows+BK,256),BF),pltpu.VMEM((rows,256),BF),pltpu.VMEM((rows,256),BF),
              pltpu.VMEM((rows+BK,128),BF),pltpu.VMEM((rows,128),BF),pltpu.VMEM((rows,128),BF),
              pltpu.VMEM((128,rows+BK),BF),pltpu.VMEM((16,rows),F32),pltpu.VMEM((rows+BK,128),F32),pltpu.VMEM((rows+BK,128),F32)]),
-        out_shape=[jax.ShapeDtypeStruct((half,width),BF)]*2,
+        out_shape=[jax.ShapeDtypeStruct((half,width//3),BF)]*6,
         compiler_params=pltpu.CompilerParams(vmem_limit_bytes=60<<20,dimension_semantics=("arbitrary",)),
         cost_estimate=pl.CostEstimate(flops=10*rows*rows*64*2*pairs//2,bytes_accessed=20*half*width,transcendentals=rows*rows*pairs),
         name="attend_bwd",
@@ -853,8 +853,10 @@
     )(w)
     return out.reshape(32*share,cols)
 
-def scatter_kernel(g,out,r0,b1,k1,r1,b2,k2,r2,b3,k3,r3,s_sem,r_sem):
+def scatter_kernel(g,out,gl,r0,b1,k1,r1,b2,k2,r2,b3,k3,r3,local,s_sem,r_sem):
     z,y,x,core=place()
+    keep=pltpu.make_async_copy(g.at[:,core],gl,local)
+    keep.start()
     pair,xn,yn,z1,z2,z3=meet(z,y,x,core)
     sems=(s_sem,r_sem)
     lanes=lanes_of(out.shape[1])
@@ -869,8 +871,9 @@
     def split1(n,iz,j,side):
         row=iz*4+(j*2+side if lanes[n][2] else side*2+j)
         c=span[n]
-        return g[row,core,:,c].astype(F32)+r0[row,:,c].astype(F32)
+        return gl[row,:,c].astype(F32)+r0[row,:,c].astype(F32)
     one=[]
+    keep.wait()
     for n in n_lanes:
         flip=lanes[n][2]
         side=x if flip else y
@@ -914,14 +917,131 @@
     v=lambda *s: pltpu.VMEM((*s,share,cols),BF)
     f=lambda *s: pltpu.VMEM((*s,share,cols),F32)
     return pl.pallas_call(scatter_kernel,
-        in_specs=[pl.BlockSpec(memory_space=pltpu.VMEM)],
+        in_specs=[pl.BlockSpec(memory_space=pl.ANY)],
         out_specs=pl.BlockSpec(memory_space=pltpu.VMEM),
-        scratch_shapes=[v(16),v(4,2),f(4,2),v(4,2),v(4),f(4),v(4),v(3),f(),v(3),pltpu.SemaphoreType.DMA((4,6)),pltpu.SemaphoreType.DMA((4,6))],
+        scratch_shapes=[v(16),v(16),v(4,2),f(4,2),v(4,2),v(4),f(4),v(4),v(3),f(),v(3),pltpu.SemaphoreType.DMA,pltpu.SemaphoreType.DMA((4,6)),pltpu.SemaphoreType.DMA((4,6))],
         out_shape=jax.ShapeDtypeStruct((share,cols),F32),
         compiler_params=pltpu.CompilerParams(collective_id=2,has_side_effects=True,vmem_limit_bytes=40<<20),
         cost_estimate=pl.CostEstimate(flops=0,bytes_accessed=64*share*cols*20,transcendentals=0),
         name="comm_scatter",
     )(g.reshape(16,2,share,cols))
+
+def selector(forward):
+    r=lax.broadcasted_iota(jnp.int32,(512,512),0)
+    c=lax.broadcasted_iota(jnp.int32,(512,512),1)
+    a,b=(r,c) if forward else (c,r)
+    return jnp.where(a==4*(b%128)+b//128,1.0,0.0).astype(BF)
+
+def bundle_kernel(exp,con,out,norm,bundle,tiles):
+    share,width=out.shape
+    hidden=exp.shape[1]//2
+    pick=selector(True)
+    for b in range(exp.shape[1]//512):
+        half,at=divmod(b*512,hidden)
+        y=nn(exp[:,b*512:(b+1)*512].astype(BF),pick).astype(BF)
+        for j in range(4):
+            to=half*hidden+j*width+at//4
+            bundle[:,to:to+128]=y[:,j*128:(j+1)*128]
+    for t in range(width//128):
+        tiles[t]=con[:,t*128:(t+1)*128]
+        for j in range(4):
+            to=2*hidden+j*width+t*128
+            bundle[:,to:to+128]=tiles[t,pl.ds(j,share,stride=4),:].astype(BF)
+    bundle[:,3*hidden:3*hidden+width]=out[...].astype(BF)
+    flat=jnp.concatenate([norm[...],jnp.zeros((4,128-share),F32)],1)
+    bundle[:,3*hidden+width:]=jnp.concatenate([flat,jnp.zeros((share-4,128),F32)],0).astype(BF)
+
+def make_bundle(exp,con,out,norm):
+    share,width=out.shape
+    total=exp.shape[1]+4*width+width+128
+    return pl.pallas_call(bundle_kernel,
+        out_shape=jax.ShapeDtypeStruct((share,total),BF),
+        scratch_shapes=[pltpu.VMEM((width//128,4*share,128),F32)],
+        compiler_params=pltpu.CompilerParams(vmem_limit_bytes=24<<20),
+        cost_estimate=pl.CostEstimate(flops=2*share*512*exp.shape[1],bytes_accessed=6*share*total,transcendentals=0),
+        name="make_bundle",
+    )(exp,con,out,norm)
+
+def update_kernel(rates,sums,*refs):
+    ins,outs,tiles=refs[:12],refs[12:32],refs[32]
+    exp_w,con_w,out_w,norm_w=(ins[3*k:3*k+3] for k in range(4))
+    share,width=out_w[0].shape
+    hidden=exp_w[0].shape[1]//2
+    def step(kind,index,g,rate):
+        w,m,a=(ref[index] for ref in ins[3*kind:3*kind+3])
+        grad,nxt,mom,avg,low=outs[5*kind:5*kind+5]
+        mn=MOMENTUM*m+g
+        wn=w-rate*(g+MOMENTUM*mn)
+        grad[index]=g
+        nxt[index]=wn
+        mom[index]=mn
+        avg[index]=AVERAGE_DECAY*a+(1.0-AVERAGE_DECAY)*wn
+        low[index]=wn.astype(BF)
+    pick=selector(False)
+    for b in range(2*hidden//512):
+        half,at=divmod(b*512,hidden)
+        z=jnp.concatenate([sums[:,half*hidden+j*width+at//4:half*hidden+j*width+at//4+128] for j in range(4)],1)
+        step(0,(slice(None),slice(b*512,(b+1)*512)),nn(z,pick),rates[0])
+    for t in range(width//128):
+        for j in range(4):
+            at=2*hidden+j*width+t*128
+            tiles[t,pl.ds(j,share,stride=4),:]=sums[:,at:at+128].astype(F32)
+        step(1,(slice(None),slice(t*128,(t+1)*128)),tiles[t],rates[0])
+    step(2,(slice(None),slice(None)),sums[:,3*hidden:3*hidden+width].astype(F32),rates[0])
+    step(3,(slice(None),slice(None)),sums[0:8,3*hidden+width:].astype(F32)[0:4,0:share],rates[1])
+
+def update(sums,rates,params):
+    sds=jax.ShapeDtypeStruct
+    shapes=[]
+    for w,_,_ in params:
+        shapes+=[sds(w.shape,F32)]*4+[sds(w.shape,BF)]
+    flat=[x for p in params for x in p]
+    import_vmem=pl.BlockSpec(memory_space=pltpu.VMEM)
+    outs=pl.pallas_call(lambda *refs: update_kernel(rates,*refs),
+        in_specs=[import_vmem]*13,
+        out_specs=[import_vmem]*20,
+        out_shape=shapes,
+        scratch_shapes=[pltpu.VMEM((params[2][0].shape[1]//128,params[1][0].shape[0],128),F32)],
+        compiler_params=pltpu.CompilerParams(vmem_limit_bytes=40<<20),
+        cost_estimate=pl.CostEstimate(flops=2*24*512*6144,bytes_accessed=12<<20,transcendentals=0),
+        name="update",
+    )(sums,*flat)
+    return [outs[5*k:5*k+5] for k in range(4)]
+
+def tail_kernel(ctl,x,qo,ko,vo,qr,kr,vr,w,df,tok,gm,acc):
+    pos=ctl[0]
+    i=pl.program_id(0)
+    width=x.shape[1]
+    share=width//2
+    turned=x[...].T
+    total=df[...]
+    @pl.when(i==0)
+    def _(): acc[...]=jnp.zeros_like(acc)
+    for side,parts in ((pos,(qo,ko,vo)),(1-pos,(qr,kr,vr))):
+        for s,d in enumerate(parts):
+            cols=pl.ds(pl.multiple_of(s*width+side*share,128),share)
+            grad=d[...]
+            total=total+nt(grad,w[:,cols])
+            acc[:,cols]+=nn(turned,grad)
+    tok[...]=total
+    @pl.when(i==pl.num_programs(0)-1)
+    def _(): gm[...]=acc[...].astype(BF)
+
+def tail(ctl,x,own,recv,w,df):
+    rows,width=x.shape
+    cols=w.shape[1]
+    row=lambda n: pl.BlockSpec((BLOCK,n),lambda i,c:(i,0))
+    held=pl.BlockSpec((width,cols),lambda i,c:(0,0),pipeline_mode=pl.Buffered(1))
+    return pl.pallas_call(tail_kernel,
+        grid_spec=pltpu.PrefetchScalarGridSpec(num_scalar_prefetch=1,grid=(rows//BLOCK,),
+          in_specs=[row(width)]+[row(width//2)]*6+[held,row(width)],
+          out_specs=[row(width),pl.BlockSpec((width,cols),lambda i,c:(0,0))],
+          scratch_shapes=[pltpu.VMEM((width,cols),F32)]),
+        out_shape=[jax.ShapeDtypeStruct((rows,width),F32),jax.ShapeDtypeStruct((width,cols),BF)],
+        compiler_params=pltpu.CompilerParams(vmem_limit_bytes=60<<20,dimension_semantics=("arbitrary",)),
+        cost_estimate=pl.CostEstimate(flops=4*rows*width*cols,bytes_accessed=rows*width*16+8*width*cols,transcendentals=0),
+        name="tail",
+    )(ctl,x,*own,*recv,w,df)
 
 def mix_kernel(ctl,x,w,cos,sin,own,oth):
     pos=ctl[0]
@@ -958,37 +1078,11 @@
         name="mix",
     )(ctl,x,w,cos,sin)
 
-def shuffle(x,count,per,share):
-    rows=x.shape[0]
-    return x.reshape(rows,2,count,per,share).transpose(0,1,3,2,4).reshape(x.shape)
-
-def unshuffle(x,count,per,share):
-    rows=x.shape[0]
-    return x.reshape(rows,2,per,count,share).transpose(0,1,3,2,4).reshape(x.shape)
-
-def fold_rows(x,per):
-    rows,cols=x.shape
-    return x.reshape(per,rows//per,cols).transpose(1,0,2).reshape(rows//per,per*cols)
-
-def unfold_rows(x,per,share):
-    count=x.shape[0]//share
-    cols=x.shape[1]//per
-    return x.reshape(count,share,per,cols).transpose(0,2,1,3).reshape(count*per*share,cols)
-
 def swap_cores(x):
     return lax.ppermute(x,"dim",[(0,1),(1,0)])
 
 def join(pos,own,recv,axis=1):
     return jnp.where(pos==0,jnp.concatenate([own,recv],axis),jnp.concatenate([recv,own],axis))
-
-def join_parts(pos,own,recv):
-    share=own.shape[1]//3
-    pieces=[]
-    for s in range(3):
-        pieces.append(own[:,s*share:(s+1)*share])
-        pieces.append(recv[:,s*share:(s+1)*share])
-    flip=[pieces[i^1] for i in range(6)]
-    return jnp.where(pos==0,jnp.concatenate(pieces,1),jnp.concatenate(flip,1))
 
 def body(tokens,doc_lengths,pair_index,target_bank,mixer_in,mixer_out,expand,contract,norm_params,*rest):
     slices=lax.axis_size("dim")
@@ -1005,10 +1099,7 @@
     per=contract.shape[1]//share_rows
     count=model_width//share_rows
     hidden_width=contract.shape[1]*count
-    exp_cols=shuffle(expand[0].astype(BF),count,per,share_rows)
-    con_cols=fold_rows(contract[0].astype(BF),per)
-    norm_cols=jnp.pad(norm_params[0].astype(BF),((0,share_rows-4),(0,128-share_rows)))
-    bundle=jnp.concatenate([exp_cols,con_cols,mixer_out[0].astype(BF),norm_cols],1)
+    bundle=make_bundle(expand[0],contract[0],mixer_out[0],norm_params[0])
     bundle=lax.all_gather(bundle,("dp","dim"),axis=0,tiled=True)
     at1=2*hidden_width
     at2=at1+per*model_width
@@ -1045,40 +1136,25 @@
     grad_exp=inner_rows(y_low,grad_both)
     grad_con=inner_rows(hidden,grad_m_low)
     grad_out=join(pos,inner_rows(o_own,grad_a_low),inner_rows(o_recv,grad_a_low),0)
-    scatter=lambda g: lax.psum_scatter(g,("dp","dim"),scatter_dimension=0,tiled=True).astype(F32)
     grad_norm=grad_norm[0:4].reshape(4,count,share_rows).transpose(1,0,2)
     grad_norm=jnp.pad(grad_norm,((0,0),(0,share_rows-4),(0,128-share_rows))).reshape(model_width,128)
     fold_con=[grad_con[j*model_width:(j+1)*model_width].astype(BF) for j in range(per)]
     terms=jnp.concatenate([grad_exp.astype(BF),*fold_con,grad_out.astype(BF),grad_norm.astype(BF)],1)
     terms,d_own,d_recv=lax.optimization_barrier((terms,d_own,d_recv))
-    sums=scatter(terms)
-    g_own,g_oth=attend_bwd(ctl,own,recv,d_own,d_recv,o_own,o_oth,lse,cos,sin)
-    grad_mixed=join_parts(pos,unpair(g_own),unpair(swap_cores(g_oth)))
-    grad_mix=inner_rows(tokens,grad_mixed)
-    token_grads=grad_first+inner_cols(grad_mixed,w_mix)
-    grad_mix=grad_mix.astype(BF)
+    sums=lax.psum_scatter(terms,("dp","dim"),scatter_dimension=0,tiled=True)
+    backs=attend_bwd(ctl,own,recv,d_own,d_recv,o_own,o_oth,lse,cos,sin)
+    token_grads,grad_mix=tail(ctl,tokens,backs[0:3],[swap_cores(g) for g in backs[3:6]],w_mix,grad_first)
     grad_mix,sums=lax.optimization_barrier((grad_mix,sums))
-    sum_mix=ring_scatter(grad_mix)
-    sum_exp=unshuffle(sums[:,0:at1],count,per,share_rows)
-    sum_con=unfold_rows(sums[:,at1:at2],per,share_rows)
-    sum_out=sums[:,at2:at3]
-    sum_norm=sums[0:4,at3:at3+share_rows]
     total_rows=group_rows*lax.axis_size("dp")
     matrix_rate=1.0/math.sqrt(total_rows)
     norm_rate=0.3/math.sqrt(total_rows)
-    grads=[g[None] for g in (sum_mix,sum_out,sum_exp,sum_con,sum_norm)]
-    weights=(mixer_in,mixer_out,expand,contract,norm_params)
-    moments=(mixer_in_moment,mixer_out_moment,expand_moment,contract_moment,norm_moment)
-    averages=(mixer_in_average,mixer_out_average,expand_average,contract_average,norm_average)
-    rates=(matrix_rate,matrix_rate,matrix_rate,matrix_rate,norm_rate)
-    results=[advance(weights[k],moments[k],averages[k],grads[k],rates[k]) for k in range(5)]
-    return (embeddings,token_grads,*grads,*[results[k][f] for f in range(4) for k in range(5)])
-
-def unpair(g):
-    rows,width=g.shape
-    pairs=width//384
-    return jnp.concatenate([g[:,p*384+s*128:p*384+(s+1)*128] for s in range(3) for p in range(pairs)],1)
-
+    new_exp,new_con,new_out,new_norm=update(sums,(matrix_rate,norm_rate),[
+        (expand[0],expand_moment[0],expand_average[0]),(contract[0],contract_moment[0],contract_average[0]),
+        (mixer_out[0],mixer_out_moment[0],mixer_out_average[0]),(norm_params[0],norm_moment[0],norm_average[0])])
+    sum_mix=ring_scatter(grad_mix)
+    nxt,mom,avg,low=advance(mixer_in[0],mixer_in_moment[0],mixer_in_average[0],sum_mix,matrix_rate)
+    results=[[sum_mix,nxt,mom,avg,low],new_out,new_exp,new_con,new_norm]
+    return (embeddings,token_grads,*[results[k][f][None] for f in range(5) for k in range(5)])
 
 def solution(mesh):
     placed = (

time: 551 us -> 519 us (0.942)
  local copies, waits for them, and re-layouts: 60.7 us -> 25.3 us
  Pallas kernels: 373 us -> 403 us
  other arithmetic: 33.5 us -> 11.6 us
  matrix products: 47 us -> 32 us
  waiting for transfers between devices: 12.5 us -> 19.3 us
    pallas_call x1 -> x4, Pallas kernels: 27.6 us -> 58.8 us  [the longest x1 29 us: ring_scatter(): pl.pallas_call(scatter_kernel, in_specs=[pl.BlockSpec(memory_space=pl.ANY...]
    convert_element_type x10 -> x0, other arithmetic: 13.7 us -> none  [the longest x5 7.87 us: advance(): weight_next.astype(jnp.bfloat16)]
    add x6 -> x0, other arithmetic: 8.88 us -> none  [the longest x5 5.87 us: advance(): average_next = AVERAGE_DECAY * average + (1.0 - AVERAGE_DECAY) * weight_next]
    dot_general x1 -> x0, matrix products: 8.21 us -> none  [inner_cols(): lax.dot_general(left_op, right_op, (((1,), (1,)), ((), ())), preferred_el...]
    optimization_barrier x0 -> x1, waiting for transfers between devices: none -> 7.77 us  [body(): grad_mix, sums = lax.optimization_barrier((grad_mix, sums))]
    reshape x3 -> x0, local copies, waits for them, and re-layouts: 7.75 us -> none  [the longest x1 3.34 us: unshuffle(): x.reshape(rows, 2, per, count, share).transpose(0, 1, 3, 2, 4)]
    transpose x3 -> x0, local copies, waits for them, and re-layouts: 6.81 us -> none  [the longest x1 4.5 us: unshuffle(): x.reshape(rows, 2, per, count, share).transpose(0, 1, 3, 2, 4)]
    dot_general x5 -> x4, matrix products: 38.6 us -> 31.9 us  [inner_rows(): lax.dot_general(left_op, right_op, (((0,), (0,)), ((), ())), preferred_el...]
  transfers between devices with their start and end apart: 8 -> 10, of which waited for: 5 -> 7; matrix products, arithmetic and copies ran while one was open for 14% -> 10% of each run, Pallas kernels for 55% -> 64%
where the time goes in v5:
time: 519 us; the launch traced here: 510 us
  Pallas kernels  403 us (78%)
  matrix products  32 us (6%)
  local copies, waits for them, and re-layouts  25.3 us (5%)
  waiting for transfers between devices  19.3 us (4%)
  between operations  16.2 us (3%)
  other arithmetic  11.6 us (2%)
    pallas_call x1, Pallas kernels, attend_bwd(): pl.pallas_call(bwd_kernel, grid_spec=pltpu.PrefetchScalarGridSpec(num_sca...  132 us
    pallas_call x1, Pallas kernels, attend_fwd(): pl.pallas_call(fwd_kernel, grid_spec=pltpu.PrefetchScalarGridSpec(num_sca...  79.2 us
    pallas_call x1, Pallas kernels, ffn_bwd(): pl.pallas_call(ffn_bwd_kernel, grid_spec=pltpu.PrefetchScalarGridSpec(num...  44.8 us
    pallas_call x1, Pallas kernels, ffn_fwd(): pl.pallas_call(ffn_fwd_kernel, grid_spec=pltpu.PrefetchScalarGridSpec(num...  44 us
    dot_general x4, matrix products, inner_rows(): lax.dot_general(left_op, right_op, (((0,), (0,)), ((), ())), preferred_el...  31.9 us
    pallas_call x1, Pallas kernels, ring_gather(): pl.pallas_call(gather_kernel, in_specs=[pl.BlockSpec(memory_space=pltpu.V...  31.4 us
    pallas_call x1, Pallas kernels, ring_scatter(): pl.pallas_call(scatter_kernel, in_specs=[pl.BlockSpec(memory_space=pl.ANY...  29 us
    pallas_call x1, Pallas kernels, tail(): pl.pallas_call(tail_kernel, grid_spec=pltpu.PrefetchScalarGridSpec(num_sc...  24.5 us
  transfers between devices with their start and end apart: 10, of which 7 were waited for; matrix products, arithmetic and copies ran while one was open for 10% of the time, Pallas kernels for 64%

profile of v5, /device:TPU:0, one launch (start us, length us, event | category | flops | bytes accessed | tf_op | source)
XLA Modules:
  0.0 509.7 jit_solution(6439695454090272013)
XLA Ops:
  7.3 1.1 copy-done.4
  10.9 2.0 make_bundle.1
  13.9 31.4 %comm_gather.1 = bf16[4,2,2,2,24,2304]{5,4,3,2,1,0:T(8,128)(2,1)S(1)} custom-call(f32[24,2304]{1,0:T(8,128)S(1)} %bitcast.88), custom_call_target="tpu_custom_call" | custom-call | bytes 70778880 | tf_op jit(solution)/shard_map/comm_gather/pallas_call | solution.py:845
  45.4 1.8 copy-done.2
  49.1 1.2 pad_add_fusion.ctl
  51.0 5.5 %fusion.2 = (f32[3072,128]{1,0:T(8,128)S(1)}, f32[3072,128]{1,0:T(8,128)S(1)}) fusion(f32[128]{0:T(128)S(1)} %get-tuple-element.140, f32[128]{0:T(128)S(1)} %get-tuple-element.141, f32[3072]{0:T(1024)S(1)} %subtract_convert_fusion), kind=kLoop, calls=%fused_computation.7 | loop fusion | flops 786432 | bytes 3159040 | tf_op jit(solution)/shard_map/mul | solution.py:1119
  56.5 1.1 constant_dynamic-slice_fusion.1.sin
  57.6 1.1 constant_dynamic-slice_fusion.2.cos
  58.7 12.8 %mix.1 = (bf16[1536,1152]{1,0:T(8,128)(2,1)}, bf16[1536,1152]{1,0:T(8,128)(2,1)}) custom-call(s32[3]{0:T(128)} %pad_add_fusion.ctl, bf16[1536,768]{1,0:T(8,128)(2,1)} %x.9, bf16[768,2304]{1,0:T(8,128)(2,1)} %bitcast.80, f32[1536,128]{1,0:T(8,128)} %constant_dynamic-slice_fusion.2.cos, f32[1536,128]{1,0:T(8,128)} %constant_dynamic-slice_fusion.1.sin), custom_call_target="tpu_custom_call" | custom-call | flops 5435817984 | bytes 12976128 | tf_op jit(solution)/shard_map/mix/pallas_call | solution.py:1071
  71.8 6.3 %collective-permute-done.qr.kr.vr = bf16[1536,1152]{1,0:T(8,128)(2,1)} collective-permute-done((bf16[1536,1152]{1,0:T(8,128)(2,1)}, bf16[1536,1152]{1,0:T(8,128)(2,1)}, u32[]{:S(2)}, u32[]{:S(2)}) %collective-permute-start) | collective-permute-done | bytes 3538976 | tf_op jit(solution)/shard_map/ppermute | solution.py:1082
  78.1 79.2 %attend_fwd.1 = (bf16[1536,384]{1,0:T(8,128)(2,1)}, bf16[1536,384]{1,0:T(8,128)(2,1)}, f32[3,8,3072]{2,1,0:T(8,128)}) custom-call(s32[3]{0:T(128)} %pad_add_fusion.ctl, bf16[1536,1152]{1,0:T(8,128)(2,1)} %get-tuple-element.80.qo.ko.vo, bf16[1536,1152]{1,0:T(8,128)(2,1)} %get-tuple-element.80.qo.ko.vo, bf16[1536,1152]{1,0:T(8,128)(2,1)} %get-tuple-element.80.qo.ko.vo, ...), custom_call_target="tpu_custom_call" | custom-call | flops 7247757312 | bytes 17694720 | tf_op jit(solution)/shard_map/attend_fwd/pallas_call | solution.py:500
  160.4 1.0 copy-done.29
  161.4 44.0 %ffn_fwd.1 = (f32[1536,768]{1,0:T(8,128)}, f32[1536,768]{1,0:T(8,128)}, f32[1536,256]{1,0:T(8,128)}, bf16[1536,768]{1,0:T(8,128)(2,1)}, bf16[1536,3072]{1,0:T(8,...) custom-call(s32[3]{0:T(128)} %pad_add_fusion.ctl, bf16[1536,384]{1,0:T(8,128)(2,1)} %get-tuple-element.82.ao.oo, ...), custom_call_target="tpu_custom_call" | custom-call | flops 23555211264 | bytes 60162048 | tf_op jit(solution)/shard_map/ffn_fwd/pallas_call | solution.py:672
  207.5 44.8 %ffn_bwd.1 = (f32[8,768]{1,0:T(8,128)}, bf16[1536,768]{1,0:T(8,128)(2,1)}, bf16[1536,6144]{1,0:T(8,128)(2,1)}, f32[1536,768]{1,0:T(8,128)}, bf16[1536,768]{1,0:T...) custom-call(s32[3]{0:T(128)} %pad_add_fusion.ctl, ...), custom_call_target="tpu_custom_call" | custom-call | flops 23555211264 | bytes 74317824 | tf_op jit(solution)/shard_map/ffn_bwd/pallas_call | solution.py:752
  253.5 11.2 %convolution_convert_fusion.1 = bf16[3072,768]{1,0:T(8,128)(2,1)S(1)} fusion(bf16[1536,3072]{1,0:T(8,128)(2,1)} %get-tuple-element.92, bf16[1536,768]{1,0:T(8,128)(2,1)} %get-tuple-element.93), kind=kOutput, calls=%fused_computation.2 | convolution fusion | flops 7250116608 | bytes 16515072 | tf_op jit(solution)/shard_map/dot_general | solution.py:30
  264.7 18.4 %fusion = bf16[768,10112]{1,0:T(8,128)(2,1)} fusion(bf16[1536,768]{1,0:T(8,128)(2,1)} %get-tuple-element.90, bf16[1536,6144]{1,0:T(8,128)(2,1)S(1)} %copy-done.38), kind=kOutput, calls=%fused_computation.1 | convolution fusion | flops 14500233216 | bytes 30670848 | tf_op jit(solution)/shard_map/dot_general | solution.py:30
  283.1 1.2 slice_dynamic-update-slice_fusion.3
  284.3 1.1 slice_dynamic-update-slice_fusion.2
  285.4 1.2 slice_dynamic-update-slice_fusion.1
  286.6 1.2 slice_dynamic-update-slice_fusion
  288.3 1.1 fusion.19
  289.5 1.1 fusion.20
  290.6 1.5 fusion.3
  293.9 131.8 %attend_bwd.1 = (bf16[1536,384]{1,0:T(8,128)(2,1)}, bf16[1536,384]{1,0:T(8,128)(2,1)}, bf16[1536,384]{1,0:T(8,128)(2,1)}, bf16[1536,384]{1,0:T(8,128)(2,1)}, bf1...) custom-call(s32[3]{0:T(128)} %pad_add_fusion.ctl, bf16[1536,1152]{1,0:T(8,128)(2,1)} %get-tuple-element.80.qo.ko.vo, ...), custom_call_target="tpu_custom_call" | custom-call | flops 18119393280 | bytes 35389440 | tf_op jit(solution)/shard_map/attend_bwd/pallas_call | solution.py:603
  426.5 1.3 constant_dynamic-slice_fusion
  427.8 1.1 collective-permute-done.5.qr
  428.8 3.4 collective-permute-done.6.kr
  433.3 24.5 %tail.1 = (f32[1536,768]{1,0:T(8,128)}, bf16[768,2304]{1,0:T(8,128)(2,1)}) custom-call(s32[3]{0:T(128)} %pad_add_fusion.ctl, bf16[1536,768]{1,0:T(8,128)(2,1)} %x.9, bf16[1536,384]{1,0:T(8,128)(2,1)} %get-tuple-element.101.qo, bf16[1536,384]{1,0:T(8,128)(2,1)} %get-tuple-element.102.ko, bf16[1536,384]{1,0:T(8,128)(2,1)} %get-tuple-element.103.vo, ...), custom_call_target="tpu_custom_call" | custom-call | flops 10871635968 | bytes 33030144 | tf_op jit(solution)/shard_map/tail/pallas_call | solution.py:1035
  457.8 7.8 %reduce-scatter.4.cloned.1.call-done.refs_0_ = bf16[24,10112]{1,0:T(8,128)(2,1)} async-done(((bf16[768,10112]{1,0:T(8,128)(2,1)}), bf16[24,10112]{1,0:T(8,128)(2,1)}) %reduce-scatter.4.cloned.1.call-update) | async-done | bytes 485392 | tf_op jit(solution)/shard_map/optimization_barrier | solution.py:1147
  465.6 2.0 copy-done.3
  467.7 29.0 %comm_scatter.1 = f32[24,2304]{1,0:T(8,128)S(1)} custom-call(bf16[16,2,24,2304]{3,2,1,0:T(8,128)(2,1)S(1)} %bitcast.82), custom_call_target="tpu_custom_call" | custom-call | bytes 70778880 | tf_op jit(solution)/shard_map/comm_scatter/pallas_call | solution.py:919
  498.4 3.3 update.1
  (112 shorter events, 18.1 us)
Async XLA Ops:
  7.2 150.4 %copy-start = (bf16[256,384]{1,0:T(8,128)(2,1)S(1)}, bf16[256,384]{1,0:T(8,128)(2,1)}, u32[]{:S(2)}) copy-start(bf16[256,384]{1,0:T(8,128)(2,1)} %param.22) | copy-start | bytes 589828
  7.2 151.4 %all-gather.2.cloned.1.call-start = ((), (), s32[]{:S(2)}) async-start(), calls=%async_computation.1 | async-start | bytes 16017408 | tf_op jit(solution)/shard_map/all_gather | solution.py:1103
  12.9 34.3 %copy-start.28 = (s32[1,2]{1,0:T(1,128)S(1)}, s32[1,2]{1,0:T(1,128)}, u32[]{:S(2)}) copy-start(s32[1,2]{1,0:T(1,128)} %param.20) | copy-start | bytes 28
  12.9 452.7 %reduce-scatter.4.cloned.1.call-start = ((), (), s32[]{:S(2)}) async-start(), calls=%async_computation.2 | async-start | bytes 16017408
  56.5 14.9 %copy-start.23 = (f32[3072,128]{1,0:T(8,128)}, f32[3072,128]{1,0:T(8,128)S(1)}, u32[]{:S(2)}) copy-start(f32[3072,128]{1,0:T(8,128)S(1)} %get-tuple-element.136.sin) | copy-start | bytes 4718596
  56.5 14.9 %copy-start.24 = (f32[3072,128]{1,0:T(8,128)}, f32[3072,128]{1,0:T(8,128)S(1)}, u32[]{:S(2)}) copy-start(f32[3072,128]{1,0:T(8,128)S(1)} %get-tuple-element.137.cos) | copy-start | bytes 4718596
  71.5 6.6 %collective-permute-start = (bf16[1536,1152]{1,0:T(8,128)(2,1)}, bf16[1536,1152]{1,0:T(8,128)(2,1)}, u32[]{:S(2)}, u32[]{:S(2)}) collective-permute-start(bf16[1536,1152]{1,0:T(8,128)(2,1)} %get-tuple-element.81), channel_id=1, source_target_pairs={{0,1},{1,0},{2,3},{3,2},{4,5},{5,4},{6,7},{7,6},{8,9},{9,8},{10,11... | collective-permute-start | bytes 10616840 | tf_op jit(solution)/shard_map/ppermute | solution.py:1082
  78.1 79.5 %copy-start.35 = (s32[2]{0:T(128)S(1)}, s32[2]{0:T(128)}, u32[]{:S(2)}) copy-start(s32[2]{0:T(128)} %param.21) | copy-start | bytes 28
  157.3 3.1 collective-permute-start.1
  157.8 47.9 %collective-permute-start.3 = (f32[2,384]{1,0:T(2,128)S(1)}, f32[2,384]{1,0:T(2,128)S(1)}, u32[]{:S(2)}, u32[]{:S(2)}) collective-permute-start(f32[2,384]{1,0:T(2,128)S(1)} %fusion.9), channel_id=1, source_target_pairs={{0,1},{1,0},{2,3},{3,2},{4,5},{5,4},{6,7},{7,6},{8,9},{9,8},{10,11... | collective-permute-start | bytes 9224 | tf_op jit(solution)/shard_map/ppermute | solution.py:1082
  205.4 1.5 collective-permute-start.2
  253.1 39.7 %collective-permute-start.4 = (bf16[1536,384]{1,0:T(8,128)(2,1)}, bf16[1536,384]{1,0:T(8,128)(2,1)S(1)}, u32[]{:S(2)}, u32[]{:S(2)}) collective-permute-start(bf16[1536,384]{1,0:T(8,128)(2,1)} %get-tuple-element.97), channel_id=1, source_target_pairs={{0,1},{1,0},{2,3},{3,2},{4,5},{5,4},{6,7},{7,6},{8,9},{9,8},{10,11... | collective-permute-start | bytes 3538952 | tf_op jit(solution)/shard_map/ppermute | solution.py:1082
  253.4 11.2 %copy-start.38 = (bf16[1536,6144]{1,0:T(8,128)(2,1)S(1)}, bf16[1536,6144]{1,0:T(8,128)(2,1)}, u32[]{:S(2)}) copy-start(bf16[1536,6144]{1,0:T(8,128)(2,1)} %get-tuple-element.91) | copy-start | bytes 56623108
  425.7 3.1 collective-permute-start.5
  426.0 6.2 %collective-permute-start.6 = (bf16[1536,384]{1,0:T(8,128)(2,1)}, bf16[1536,384]{1,0:T(8,128)(2,1)S(1)}, u32[]{:S(2)}, u32[]{:S(2)}) collective-permute-start(bf16[1536,384]{1,0:T(8,128)(2,1)} %get-tuple-element.105), channel_id=1, source_target_pairs={{0,1},{1,0},{2,3},{3,2},{4,5},{5,4},{6,7},{7,6},{8,9},{9,8},{10,11... | collective-permute-start | bytes 3538952 | tf_op jit(solution)/shard_map/ppermute | solution.py:1082
  426.3 6.1 %collective-permute-start.7 = (bf16[1536,384]{1,0:T(8,128)(2,1)}, bf16[1536,384]{1,0:T(8,128)(2,1)}, u32[]{:S(2)}, u32[]{:S(2)}) collective-permute-start(bf16[1536,384]{1,0:T(8,128)(2,1)} %get-tuple-element.106), channel_id=1, source_target_pairs={{0,1},{1,0},{2,3},{3,2},{4,5},{5,4},{6,7},{7,6},{8,9},{9,8},{10,11... | collective-permute-start | bytes 3538952 | tf_op jit(solution)/shard_map/ppermute | solution.py:1082
  433.3 63.4 %copy-start.9 = (f32[1,24,2304]{2,1,0:T(8,128)S(1)}, f32[1,24,2304]{2,1,0:T(8,128)}, u32[]{:S(2)}) copy-start(f32[1,24,2304]{2,1,0:T(8,128)} %param.23) | copy-start | bytes 663556
  433.3 63.4 %copy-start.26 = (f32[1,24,2304]{2,1,0:T(8,128)S(1)}, f32[1,24,2304]{2,1,0:T(8,128)}, u32[]{:S(2)}) copy-start(f32[1,24,2304]{2,1,0:T(8,128)} %param.28) | copy-start | bytes 663556
  467.6 29.9 %copy-start.27 = (f32[1,24,2304]{2,1,0:T(8,128)S(1)}, f32[1,24,2304]{2,1,0:T(8,128)}, u32[]{:S(2)}) copy-start(f32[1,24,2304]{2,1,0:T(8,128)} %param.33) | copy-start | bytes 663556
  467.6 30.7 %copy-start.5 = (f32[1,24,6144]{2,1,0:T(8,128)S(1)}, f32[1,24,6144]{2,1,0:T(8,128)}, u32[]{:S(2)}) copy-start(f32[1,24,6144]{2,1,0:T(8,128)} %param.25) | copy-start | bytes 1769476
  467.6 30.7 %copy-start.7 = (f32[1,96,768]{2,1,0:T(8,128)S(1)}, f32[1,96,768]{2,1,0:T(8,128)}, u32[]{:S(2)}) copy-start(f32[1,96,768]{2,1,0:T(8,128)} %param.26) | copy-start | bytes 884740
  467.6 30.7 %copy-start.10 = (f32[1,24,6144]{2,1,0:T(8,128)S(1)}, f32[1,24,6144]{2,1,0:T(8,128)}, u32[]{:S(2)}) copy-start(f32[1,24,6144]{2,1,0:T(8,128)} %param.30) | copy-start | bytes 1769476
  467.6 30.7 %copy-start.11 = (f32[1,24,6144]{2,1,0:T(8,128)S(1)}, f32[1,24,6144]{2,1,0:T(8,128)}, u32[]{:S(2)}) copy-start(f32[1,24,6144]{2,1,0:T(8,128)} %param.35) | copy-start | bytes 1769476
  467.6 30.7 %copy-start.12 = (bf16[24,10112]{1,0:T(8,128)(2,1)S(1)}, bf16[24,10112]{1,0:T(8,128)(2,1)}, u32[]{:S(2)}) copy-start(bf16[24,10112]{1,0:T(8,128)(2,1)} %reduce-scatter.4.cloned.1.call-done.refs_0_) | copy-start | bytes 1456132
  467.6 30.7 %copy-start.13 = (f32[1,96,768]{2,1,0:T(8,128)S(1)}, f32[1,96,768]{2,1,0:T(8,128)}, u32[]{:S(2)}) copy-start(f32[1,96,768]{2,1,0:T(8,128)} %param.31) | copy-start | bytes 884740
  467.6 30.7 %copy-start.14 = (f32[1,96,768]{2,1,0:T(8,128)S(1)}, f32[1,96,768]{2,1,0:T(8,128)}, u32[]{:S(2)}) copy-start(f32[1,96,768]{2,1,0:T(8,128)} %param.36) | copy-start | bytes 884740
  467.6 30.7 %copy-start.16 = (f32[1,24,768]{2,1,0:T(8,128)S(1)}, f32[1,24,768]{2,1,0:T(8,128)}, u32[]{:S(2)}) copy-start(f32[1,24,768]{2,1,0:T(8,128)} %param.24) | copy-start | bytes 221188
  467.6 30.7 %copy-start.17 = (f32[1,24,768]{2,1,0:T(8,128)S(1)}, f32[1,24,768]{2,1,0:T(8,128)}, u32[]{:S(2)}) copy-start(f32[1,24,768]{2,1,0:T(8,128)} %param.29) | copy-start | bytes 221188
  467.7 30.7 %copy-start.18 = (f32[1,24,768]{2,1,0:T(8,128)S(1)}, f32[1,24,768]{2,1,0:T(8,128)}, u32[]{:S(2)}) copy-start(f32[1,24,768]{2,1,0:T(8,128)} %param.34) | copy-start | bytes 221188
  467.7 30.7 %copy-start.20 = (f32[1,4,24]{2,1,0:T(4,128)S(1)}, f32[1,4,24]{2,1,0:T(4,128)}, u32[]{:S(2)}) copy-start(f32[1,4,24]{2,1,0:T(4,128)} %param.27) | copy-start | bytes 1156
  467.7 30.7 %copy-start.21 = (f32[1,4,24]{2,1,0:T(4,128)S(1)}, f32[1,4,24]{2,1,0:T(4,128)}, u32[]{:S(2)}) copy-start(f32[1,4,24]{2,1,0:T(4,128)} %param.32) | copy-start | bytes 1156
  467.7 30.7 %copy-start.22 = (f32[1,4,24]{2,1,0:T(4,128)S(1)}, f32[1,4,24]{2,1,0:T(4,128)}, u32[]{:S(2)}) copy-start(f32[1,4,24]{2,1,0:T(4,128)} %param.37) | copy-start | bytes 1156
  (17 other events, 32.6 us)
Sparse Core Ops, SparseCore 0:
  13.0 113.9 all-gather.1
  293.0 172.5 reduce-scatter.3

commit v6 on v5

--- a/solution.py
+++ b/solution.py
@@ -404,7 +404,7 @@
 NEG=-1e30
 BQ=512
 ROWS=256
-BK=512
+BK=384
 F32=jnp.float32
 BF=jnp.bfloat16
 
@@ -613,7 +613,7 @@
         name="attend_bwd",
     )(ctl,own,own,own,recv,recv,recv,d_own,d_recv,o_own,o_oth,lse,cos,sin)
 
-BLOCK=512
+BLOCK=256
 
 def spread_mean(x):
     return jnp.mean(x,axis=1,keepdims=True)
@@ -623,9 +623,10 @@
     r=ctl[0]*(block*pl.num_programs(0))+i*block+lax.broadcasted_iota(jnp.int32,(block,1),0)
     return (r>=ctl[1]).astype(jnp.int32)+(r>=ctl[2]).astype(jnp.int32)
 
-def ffn_fwd_kernel(ctl,ao,ax,tok,w_exp,w_con,w_out,norm,u1,u2,rs,yb,hb,pf,pooled):
+def ffn_fwd_kernel(ctl,ao,ax,tok,w_exp,w_con,w_out,norm,u1,u2,rs,yb,h0,h1,h2,h3,pf,pooled):
     block,width=tok.shape
-    hidden=hb.shape[1]
+    hidden=pf.shape[1]//2
+    kept=(h0,h1,h2,h3)
     share=width//2
     pos=ctl[0]
     mine=pl.multiple_of(pos*share,share)
@@ -640,16 +641,19 @@
     ylow=y.astype(BF)
     yb[...]=ylow
     acc=y
-    for c in range(hidden//width):
-        gc=slice(c*width,(c+1)*width)
-        uc=slice(hidden+c*width,hidden+(c+1)*width)
-        gate=nn(ylow,w_exp[:,gc])
-        up=nn(ylow,w_exp[:,uc])
+    count=hidden//width
+    spans=[(slice(c*width,(c+1)*width),slice(hidden+c*width,hidden+(c+1)*width)) for c in range(count)]
+    pre=lambda c: (nn(ylow,w_exp[:,spans[c][0]]),nn(ylow,w_exp[:,spans[c][1]]))
+    ahead=pre(0)
+    for c in range(count):
+        gate,up=ahead
+        if c+1<count: ahead=pre(c+1)
+        gc,uc=spans[c]
         sig=jax.nn.sigmoid(gate)
         act=gate*sig
         low=(act*up).astype(BF)
-        hb[:,gc]=low
-        pf[:,gc]=(up*sig*(1.0+gate*(1.0-sig))).astype(BF)
+        kept[c][...]=low
+        pf[:,gc]=(up*(sig+act*(1.0-sig))).astype(BF)
         pf[:,uc]=act.astype(BF)
         acc=acc+nn(low,w_con[:,gc])
     cent=acc-spread_mean(acc)
@@ -672,9 +676,9 @@
     return pl.pallas_call(ffn_fwd_kernel,
         grid_spec=pltpu.PrefetchScalarGridSpec(num_scalar_prefetch=1,grid=(rows//BLOCK,),
           in_specs=[row(width//2),row(width//2),row(width),held(2*hidden,0),held(hidden,2*hidden),held(width,3*hidden),flat],
-          out_specs=[row(width),row(width),row(256),row(width),row(hidden),row(2*hidden),flat]),
+          out_specs=[row(width),row(width),row(256),*[row(width)]*5,row(2*hidden),flat]),
         out_shape=[jax.ShapeDtypeStruct((rows,width),F32),jax.ShapeDtypeStruct((rows,width),F32),jax.ShapeDtypeStruct((rows,256),F32),
-          jax.ShapeDtypeStruct((rows,width),BF),jax.ShapeDtypeStruct((rows,hidden),BF),jax.ShapeDtypeStruct((rows,2*hidden),BF),
+          *[jax.ShapeDtypeStruct((rows,width),BF)]*5,jax.ShapeDtypeStruct((rows,2*hidden),BF),
           jax.ShapeDtypeStruct((8,width),F32)],
         compiler_params=pltpu.CompilerParams(vmem_limit_bytes=60<<20,dimension_semantics=("arbitrary",)),
         cost_estimate=pl.CostEstimate(flops=2*rows*width*(width+3*hidden),bytes_accessed=rows*(width*14+hidden*6)+2*width*(width+3*hidden),transcendentals=rows*hidden),
@@ -847,7 +851,7 @@
         out_specs=pl.BlockSpec(memory_space=pl.ANY),
         scratch_shapes=[pltpu.VMEM((share,cols),BF),pltpu.SemaphoreType.DMA,pltpu.SemaphoreType.DMA((4,8)),pltpu.SemaphoreType.DMA((4,8))],
         out_shape=jax.ShapeDtypeStruct((4,2,2,2,share,cols),BF),
-        compiler_params=pltpu.CompilerParams(collective_id=1,has_side_effects=True,vmem_limit_bytes=16<<20),
+        compiler_params=pltpu.CompilerParams(collective_id=1,has_side_effects=True,vmem_limit_bytes=60<<20),
         cost_estimate=pl.CostEstimate(flops=0,bytes_accessed=64*share*cols*20,transcendentals=0),
         name="comm_gather",
     )(w)
@@ -921,7 +925,7 @@
         out_specs=pl.BlockSpec(memory_space=pltpu.VMEM),
         scratch_shapes=[v(16),v(16),v(4,2),f(4,2),v(4,2),v(4),f(4),v(4),v(3),f(),v(3),pltpu.SemaphoreType.DMA,pltpu.SemaphoreType.DMA((4,6)),pltpu.SemaphoreType.DMA((4,6))],
         out_shape=jax.ShapeDtypeStruct((share,cols),F32),
-        compiler_params=pltpu.CompilerParams(collective_id=2,has_side_effects=True,vmem_limit_bytes=40<<20),
+        compiler_params=pltpu.CompilerParams(collective_id=2,has_side_effects=True,vmem_limit_bytes=60<<20),
         cost_estimate=pl.CostEstimate(flops=0,bytes_accessed=64*share*cols*20,transcendentals=0),
         name="comm_scatter",
     )(g.reshape(16,2,share,cols))
@@ -957,7 +961,7 @@
     return pl.pallas_call(bundle_kernel,
         out_shape=jax.ShapeDtypeStruct((share,total),BF),
         scratch_shapes=[pltpu.VMEM((width//128,4*share,128),F32)],
-        compiler_params=pltpu.CompilerParams(vmem_limit_bytes=24<<20),
+        compiler_params=pltpu.CompilerParams(vmem_limit_bytes=60<<20),
         cost_estimate=pl.CostEstimate(flops=2*share*512*exp.shape[1],bytes_accessed=6*share*total,transcendentals=0),
         name="make_bundle",
     )(exp,con,out,norm)
@@ -1002,7 +1006,7 @@
         out_specs=[import_vmem]*20,
         out_shape=shapes,
         scratch_shapes=[pltpu.VMEM((params[2][0].shape[1]//128,params[1][0].shape[0],128),F32)],
-        compiler_params=pltpu.CompilerParams(vmem_limit_bytes=40<<20),
+        compiler_params=pltpu.CompilerParams(vmem_limit_bytes=60<<20),
         cost_estimate=pl.CostEstimate(flops=2*24*512*6144,bytes_accessed=12<<20,transcendentals=0),
         name="update",
     )(sums,*flat)
@@ -1012,17 +1016,17 @@
     pos=ctl[0]
     i=pl.program_id(0)
     width=x.shape[1]
-    share=width//2
     turned=x[...].T
     total=df[...]
     @pl.when(i==0)
     def _(): acc[...]=jnp.zeros_like(acc)
-    for side,parts in ((pos,(qo,ko,vo)),(1-pos,(qr,kr,vr))):
-        for s,d in enumerate(parts):
-            cols=pl.ds(pl.multiple_of(s*width+side*share,128),share)
-            grad=d[...]
-            total=total+nt(grad,w[:,cols])
-            acc[:,cols]+=nn(turned,grad)
+    for s,(mine,theirs) in enumerate(((qo,qr),(ko,kr),(vo,vr))):
+        a=mine[...]
+        b=theirs[...]
+        grad=jnp.concatenate([jnp.where(pos==0,a,b),jnp.where(pos==0,b,a)],1)
+        cols=slice(s*width,(s+1)*width)
+        total=total+nt(grad,w[:,cols])
+        acc[:,cols]+=nn(turned,grad)
     tok[...]=total
     @pl.when(i==pl.num_programs(0)-1)
     def _(): gm[...]=acc[...].astype(BF)
@@ -1030,10 +1034,10 @@
 def tail(ctl,x,own,recv,w,df):
     rows,width=x.shape
     cols=w.shape[1]
-    row=lambda n: pl.BlockSpec((BLOCK,n),lambda i,c:(i,0))
+    row=lambda n: pl.BlockSpec((512,n),lambda i,c:(i,0))
     held=pl.BlockSpec((width,cols),lambda i,c:(0,0),pipeline_mode=pl.Buffered(1))
     return pl.pallas_call(tail_kernel,
-        grid_spec=pltpu.PrefetchScalarGridSpec(num_scalar_prefetch=1,grid=(rows//BLOCK,),
+        grid_spec=pltpu.PrefetchScalarGridSpec(num_scalar_prefetch=1,grid=(rows//512,),
           in_specs=[row(width)]+[row(width//2)]*6+[held,row(width)],
           out_specs=[row(width),pl.BlockSpec((width,cols),lambda i,c:(0,0))],
           scratch_shapes=[pltpu.VMEM((width,cols),F32)]),
@@ -1052,25 +1056,30 @@
     s=sin[...]
     lane=lax.broadcasted_iota(jnp.int32,c.shape,1)
     first=(lane%64)<32
-    for out,side in ((own,pos),(oth,1-pos)):
-        for part in range(3):
-            cols=pl.ds(pl.multiple_of(part*width+side*share,128),share)
-            y=nn(xb,w[:,cols])
-            for t in range(share//128):
-                z=y[:,t*128:(t+1)*128]
-                if part<2:
-                    swapped=jnp.where(first,pltpu.roll(z,96,1),pltpu.roll(z,32,1))
-                    z=z*c+swapped*s
-                out[:,part*share+t*128:part*share+(t+1)*128]=z.astype(BF)
+    for part in range(3):
+        y=nn(xb,w[:,part*width:(part+1)*width])
+        tiles=[]
+        for t in range(width//128):
+            z=y[:,t*128:(t+1)*128]
+            if part<2:
+                swapped=jnp.where(first,pltpu.roll(z,96,1),pltpu.roll(z,32,1))
+                z=z*c+swapped*s
+            tiles.append(z.astype(BF))
+        count=share//128
+        for t in range(count):
+            cols=slice(part*share+t*128,part*share+(t+1)*128)
+            own[:,cols]=jnp.where(pos==0,tiles[t],tiles[count+t])
+            oth[:,cols]=jnp.where(pos==0,tiles[count+t],tiles[t])
 
 def mix(ctl,x,w,cos,sin):
     rows,width=x.shape
     cols=w.shape[1]
     block=256
     row=lambda n: pl.BlockSpec((block,n),lambda i,c:(i,0))
+    angle=pl.BlockSpec((block,128),lambda i,c:(c[0]*(rows//block)+i,0))
     return pl.pallas_call(mix_kernel,
         grid_spec=pltpu.PrefetchScalarGridSpec(num_scalar_prefetch=1,grid=(rows//block,),
-          in_specs=[row(width),pl.BlockSpec((width,cols),lambda i,c:(0,0)),row(128),row(128)],
+          in_specs=[row(width),pl.BlockSpec((width,cols),lambda i,c:(0,0)),angle,angle],
           out_specs=[row(cols//2)]*2),
         out_shape=[jax.ShapeDtypeStruct((rows,cols//2),BF)]*2,
         compiler_params=pltpu.CompilerParams(vmem_limit_bytes=60<<20,dimension_semantics=("arbitrary",)),
@@ -1117,9 +1126,7 @@
     angles=(ids-begin).astype(F32)[:,None]*frequency[None,:]
     cos=jnp.cos(angles)
     sin=jnp.sin(angles)*jnp.where((lane%64)<32,-1.0,1.0)[None,:]
-    cos_own=lax.dynamic_slice_in_dim(cos,pos*local_rows,local_rows,0)
-    sin_own=lax.dynamic_slice_in_dim(sin,pos*local_rows,local_rows,0)
-    own,oth=mix(ctl,tokens,w_mix,cos_own,sin_own)
+    own,oth=mix(ctl,tokens,w_mix,cos,sin)
     recv=swap_cores(oth)
     pick=(pair_index[:,None]==jnp.arange(target_bank.shape[0],dtype=jnp.int32)[None,:]).astype(BF)
     some=matmul(pick,target_bank)
@@ -1127,19 +1134,18 @@
     o_own,o_oth,lse=attend_fwd(ctl,own,recv)
     o_recv=swap_cores(o_oth)
     norm_gains=jnp.pad(w_norm.astype(F32),((0,4),(0,0)))
-    u1,u2,rs,y_low,hidden,factors,pooled=ffn_fwd(ctl,o_own,o_recv,tokens,bundle,norm_gains,hidden_width)
+    u1,u2,rs,y_low,*hidden,factors,pooled=ffn_fwd(ctl,o_own,o_recv,tokens,bundle,norm_gains,hidden_width)
     embeds,grad_m_low,grad_both,grad_first,grad_a_low,d_own,d_oth,grad_norm=ffn_bwd(
         ctl,lengths.astype(F32),pooled,swap_cores(pooled),targets,u1,u2,rs,factors,bundle,norm_gains)
     share=model_width//2
     embeddings=lax.dynamic_slice(embeds,(0,pos*share),(doc_count,share))
     d_recv=swap_cores(d_oth)
     grad_exp=inner_rows(y_low,grad_both)
-    grad_con=inner_rows(hidden,grad_m_low)
+    grad_con=[inner_rows(h,grad_m_low).astype(BF) for h in hidden]
     grad_out=join(pos,inner_rows(o_own,grad_a_low),inner_rows(o_recv,grad_a_low),0)
     grad_norm=grad_norm[0:4].reshape(4,count,share_rows).transpose(1,0,2)
     grad_norm=jnp.pad(grad_norm,((0,0),(0,share_rows-4),(0,128-share_rows))).reshape(model_width,128)
-    fold_con=[grad_con[j*model_width:(j+1)*model_width].astype(BF) for j in range(per)]
-    terms=jnp.concatenate([grad_exp.astype(BF),*fold_con,grad_out.astype(BF),grad_norm.astype(BF)],1)
+    terms=jnp.concatenate([grad_exp.astype(BF),*grad_con,grad_out.astype(BF),grad_norm.astype(BF)],1)
     terms,d_own,d_recv=lax.optimization_barrier((terms,d_own,d_recv))
     sums=lax.psum_scatter(terms,("dp","dim"),scatter_dimension=0,tiled=True)
     backs=attend_bwd(ctl,own,recv,d_own,d_recv,o_own,o_oth,lse,cos,sin)

time: 519 us -> 517 us (level)
  local copies, waits for them, and re-layouts: 25.3 us -> 9.65 us
  waiting for transfers between devices: 19.3 us -> 33.2 us
  Pallas kernels: 403 us -> 394 us
  matrix products: 32 us -> 37.6 us
    optimization_barrier x1, waiting for transfers between devices: 7.77 us -> 21.8 us  [body(): grad_mix, sums = lax.optimization_barrier((grad_mix, sums))]
    unnamed x85 -> x49, local copies, waits for them, and re-layouts: 18 us -> 4.46 us
    pallas_call x1, Pallas kernels: 132 us -> 126 us  [attend_bwd(): pl.pallas_call(bwd_kernel, grid_spec=pltpu.PrefetchScalarGridSpec(num_sca...]
    dot_general x4 -> x7, matrix products: 31.9 us -> 37.4 us  [inner_rows(): lax.dot_general(left_op, right_op, (((0,), (0,)), ((), ())), preferred_el...]
  transfers between devices with their start and end apart: 10 -> 10, of which waited for: 7 -> 7; matrix products, arithmetic and copies ran while one was open for 10% -> 11% of each run, Pallas kernels for 64% -> 62%
where the time goes in v6:
time: 517 us; the launch traced here: 508 us
  Pallas kernels  394 us (76%)
  matrix products  37.6 us (7%)
  waiting for transfers between devices  33.2 us (6%)
  between operations  16.1 us (3%)
  other arithmetic  14.2 us (3%)
  local copies, waits for them, and re-layouts  9.65 us (2%)
    pallas_call x1, Pallas kernels, attend_bwd(): pl.pallas_call(bwd_kernel, grid_spec=pltpu.PrefetchScalarGridSpec(num_sca...  126 us
    pallas_call x1, Pallas kernels, attend_fwd(): pl.pallas_call(fwd_kernel, grid_spec=pltpu.PrefetchScalarGridSpec(num_sca...  79.4 us
    pallas_call x1, Pallas kernels, ffn_bwd(): pl.pallas_call(ffn_bwd_kernel, grid_spec=pltpu.PrefetchScalarGridSpec(num...  43.4 us
    pallas_call x1, Pallas kernels, ffn_fwd(): pl.pallas_call(ffn_fwd_kernel, grid_spec=pltpu.PrefetchScalarGridSpec(num...  41.9 us
    dot_general x7, matrix products, inner_rows(): lax.dot_general(left_op, right_op, (((0,), (0,)), ((), ())), preferred_el...  37.4 us
    pallas_call x1, Pallas kernels, ring_gather(): pl.pallas_call(gather_kernel, in_specs=[pl.BlockSpec(memory_space=pltpu.V...  33.8 us
    pallas_call x1, Pallas kernels, ring_scatter(): pl.pallas_call(scatter_kernel, in_specs=[pl.BlockSpec(memory_space=pl.ANY...  29.7 us
    optimization_barrier x1, waiting for transfers between devices, body(): grad_mix, sums = lax.optimization_barrier((grad_mix, sums))  21.8 us
  transfers between devices with their start and end apart: 10, of which 7 were waited for; matrix products, arithmetic and copies ran while one was open for 11% of the time, Pallas kernels for 62%

profile of v6, /device:TPU:0, one launch (start us, length us, event | category | flops | bytes accessed | tf_op | source)
XLA Modules:
  0.0 507.6 jit_solution(10006987707538041969)
XLA Ops:
  7.3 3.2 make_bundle.1
  10.5 33.8 %comm_gather.1 = bf16[4,2,2,2,24,2304]{5,4,3,2,1,0:T(8,128)(2,1)} custom-call(f32[24,2304]{1,0:T(8,128)} %bitcast.95), custom_call_target="tpu_custom_call" | custom-call | bytes 70778880 | tf_op jit(solution)/shard_map/comm_gather/pallas_call | solution.py:849
  46.2 1.2 pad_add_fusion.ctl
  48.1 7.1 %fusion.2 = (f32[3072,128]{1,0:T(8,128)}, f32[3072,128]{1,0:T(8,128)}) fusion(f32[128]{0:T(128)S(1)} %get-tuple-element.146, f32[128]{0:T(128)S(1)} %get-tuple-element.147, f32[3072]{0:T(1024)S(1)} %subtract_convert_fusion), kind=kLoop, calls=%fused_computation.6 | loop fusion | flops 786432 | bytes 3159040 | tf_op jit(solution)/shard_map/mul | solution.py:1128
  55.3 11.8 %mix.1 = (bf16[1536,1152]{1,0:T(8,128)(2,1)}, bf16[1536,1152]{1,0:T(8,128)(2,1)}) custom-call(s32[3]{0:T(128)} %pad_add_fusion.ctl, bf16[1536,768]{1,0:T(8,128)(2,1)} %x.9, bf16[768,2304]{1,0:T(8,128)(2,1)} %bitcast.86, f32[3072,128]{1,0:T(8,128)} %get-tuple-element.143.cos, f32[3072,128]{1,0:T(8,128)} %get-tuple-element.142.sin), custom_call_target="tpu_custom_call" | custom-call | flops 5435817984 | bytes 12976128 | tf_op jit(solution)/shard_map/mix/pallas_call | solution.py:1080
  67.5 6.2 %collective-permute-done.qr.kr.vr = bf16[1536,1152]{1,0:T(8,128)(2,1)} collective-permute-done((bf16[1536,1152]{1,0:T(8,128)(2,1)}, bf16[1536,1152]{1,0:T(8,128)(2,1)}, u32[]{:S(2)}, u32[]{:S(2)}) %collective-permute-start) | collective-permute-done | bytes 3538976 | tf_op jit(solution)/shard_map/ppermute | solution.py:1091
  73.7 79.4 %attend_fwd.1 = (bf16[1536,384]{1,0:T(8,128)(2,1)}, bf16[1536,384]{1,0:T(8,128)(2,1)}, f32[3,8,3072]{2,1,0:T(8,128)}) custom-call(s32[3]{0:T(128)} %pad_add_fusion.ctl, bf16[1536,1152]{1,0:T(8,128)(2,1)} %get-tuple-element.83.qo.ko.vo, bf16[1536,1152]{1,0:T(8,128)(2,1)} %get-tuple-element.83.qo.ko.vo, bf16[1536,1152]{1,0:T(8,128)(2,1)} %get-tuple-element.83.qo.ko.vo, ...), custom_call_target="tpu_custom_call" | custom-call | flops 7247757312 | bytes 17694720 | tf_op jit(solution)/shard_map/attend_fwd/pallas_call | solution.py:500
  154.4 0.9 slice.27
  156.2 1.0 copy-done.8
  157.2 41.9 %ffn_fwd.1 = (f32[1536,768]{1,0:T(8,128)}, f32[1536,768]{1,0:T(8,128)}, f32[1536,256]{1,0:T(8,128)}, bf16[1536,768]{1,0:T(8,128)(2,1)}, bf16[1536,768]{1,0:T(8,1...) custom-call(s32[3]{0:T(128)} %pad_add_fusion.ctl, ...), custom_call_target="tpu_custom_call" | custom-call | flops 23555211264 | bytes 60162048 | tf_op jit(solution)/shard_map/ffn_fwd/pallas_call | solution.py:676
  201.2 43.4 %ffn_bwd.1 = (f32[8,768]{1,0:T(8,128)}, bf16[1536,768]{1,0:T(8,128)(2,1)}, bf16[1536,6144]{1,0:T(8,128)(2,1)}, f32[1536,768]{1,0:T(8,128)}, bf16[1536,768]{1,0:T...) custom-call(s32[3]{0:T(128)} %pad_add_fusion.ctl, ...), custom_call_target="tpu_custom_call" | custom-call | flops 23555211264 | bytes 74317824 | tf_op jit(solution)/shard_map/ffn_bwd/pallas_call | solution.py:756
  244.9 20.9 %fusion = bf16[768,10112]{1,0:T(8,128)(2,1)} fusion(bf16[1536,768]{1,0:T(8,128)(2,1)} %get-tuple-element.93, bf16[1536,6144]{1,0:T(8,128)(2,1)} %get-tuple-element.94), kind=kOutput, calls=%fused_computation.1 | convolution fusion | flops 14500233216 | bytes 30670848 | tf_op jit(solution)/shard_map/dot_general | solution.py:30
  265.8 3.1 fusion.6
  268.9 3.2 fusion.5
  272.0 3.1 fusion.4
  275.2 1.1 fusion.23
  276.3 0.7 slice.31
  277.2 2.9 fusion.24
  280.3 3.2 fusion.3
  283.5 1.5 fusion.7
  285.0 0.8 constant_dynamic-update-slice_fusion
  285.8 1.0 copy-done.10
  286.8 125.7 %attend_bwd.1 = (bf16[1536,384]{1,0:T(8,128)(2,1)}, bf16[1536,384]{1,0:T(8,128)(2,1)}, bf16[1536,384]{1,0:T(8,128)(2,1)}, bf16[1536,384]{1,0:T(8,128)(2,1)}, bf1...) custom-call(s32[3]{0:T(128)} %pad_add_fusion.ctl, bf16[1536,1152]{1,0:T(8,128)(2,1)} %get-tuple-element.83.qo.ko.vo, ...), custom_call_target="tpu_custom_call" | custom-call | flops 18119393280 | bytes 35389440 | tf_op jit(solution)/shard_map/attend_bwd/pallas_call | solution.py:603
  413.4 1.3 constant_dynamic-slice_fusion
  414.7 1.0 collective-permute-done.5.qr
  415.6 3.4 collective-permute-done.6.kr
  419.1 0.9 copy-done.12
  420.1 20.3 %tail.1 = (f32[1536,768]{1,0:T(8,128)}, bf16[768,2304]{1,0:T(8,128)(2,1)}) custom-call(s32[3]{0:T(128)} %pad_add_fusion.ctl, bf16[1536,768]{1,0:T(8,128)(2,1)} %x.9, bf16[1536,384]{1,0:T(8,128)(2,1)} %get-tuple-element.107.qo, bf16[1536,384]{1,0:T(8,128)(2,1)} %get-tuple-element.108.ko, bf16[1536,384]{1,0:T(8,128)(2,1)} %get-tuple-element.109.vo, ...), custom_call_target="tpu_custom_call" | custom-call | flops 10871635968 | bytes 33030144 | tf_op jit(solution)/shard_map/tail/pallas_call | solution.py:1039
  440.4 21.8 %reduce-scatter.4.cloned.1.call-done.refs_0_ = bf16[24,10112]{1,0:T(8,128)(2,1)} async-done(((bf16[768,10112]{1,0:T(8,128)(2,1)}), bf16[24,10112]{1,0:T(8,128)(2,1)}) %reduce-scatter.4.cloned.1.call-update) | async-done | bytes 485392 | tf_op jit(solution)/shard_map/optimization_barrier | solution.py:1153
  462.2 29.7 %comm_scatter.1 = f32[24,2304]{1,0:T(8,128)} custom-call(bf16[16,2,24,2304]{3,2,1,0:T(8,128)(2,1)} %bitcast.88), custom_call_target="tpu_custom_call" | custom-call | bytes 70778880 | tf_op jit(solution)/shard_map/comm_scatter/pallas_call | solution.py:923
  492.0 1.8 convert_bitcast_fusion
  494.5 5.2 %update.1 = (f32[24,6144]{1,0:T(8,128)}, f32[24,6144]{1,0:T(8,128)}, f32[24,6144]{1,0:T(8,128)}, f32[24,6144]{1,0:T(8,128)}, bf16[24,6144]{1,0:T(8,128)(2,1)}, /...) custom-call(bf16[24,10112]{1,0:T(8,128)(2,1)} %reduce-scatter.4.clon, ...), custom_call_target="tpu_custom_call" | custom-call | flops 150994944 | bytes 12582912 | tf_op jit(solution)/shard_map/update/pallas_call | solution.py:1004
  (77 shorter events, 9.0 us)
Async XLA Ops:
  7.2 146.2 %copy-start = (bf16[256,384]{1,0:T(8,128)(2,1)S(1)}, bf16[256,384]{1,0:T(8,128)(2,1)}, u32[]{:S(2)}) copy-start(bf16[256,384]{1,0:T(8,128)(2,1)} %param.22) | copy-start | bytes 589828
  7.2 147.1 %all-gather.2.cloned.1.call-start = ((), (), s32[]{:S(2)}) async-start(), calls=%async_computation.1 | async-start | bytes 16017408 | tf_op jit(solution)/shard_map/all_gather | solution.py:1112
  10.4 33.9 %copy-start.7 = (s32[1,2]{1,0:T(1,128)S(1)}, s32[1,2]{1,0:T(1,128)}, u32[]{:S(2)}) copy-start(s32[1,2]{1,0:T(1,128)} %param.20) | copy-start | bytes 28
  10.5 451.8 %reduce-scatter.4.cloned.1.call-start = ((), (), s32[]{:S(2)}) async-start(), calls=%async_computation.2 | async-start | bytes 16017408
  67.1 6.6 %collective-permute-start = (bf16[1536,1152]{1,0:T(8,128)(2,1)}, bf16[1536,1152]{1,0:T(8,128)(2,1)}, u32[]{:S(2)}, u32[]{:S(2)}) collective-permute-start(bf16[1536,1152]{1,0:T(8,128)(2,1)} %get-tuple-element.84), channel_id=1, source_target_pairs={{0,1},{1,0},{2,3},{3,2},{4,5},{5,4},{6,7},{7,6},{8,9},{9,8},{10,11... | collective-permute-start | bytes 10616840 | tf_op jit(solution)/shard_map/ppermute | solution.py:1091
  73.7 79.7 %copy-start.14 = (s32[2]{0:T(128)S(1)}, s32[2]{0:T(128)}, u32[]{:S(2)}) copy-start(s32[2]{0:T(128)} %param.21) | copy-start | bytes 28
  153.1 3.1 collective-permute-start.1
  153.6 45.9 %collective-permute-start.3 = (f32[2,384]{1,0:T(2,128)S(1)}, f32[2,384]{1,0:T(2,128)S(1)}, u32[]{:S(2)}, u32[]{:S(2)}) collective-permute-start(f32[2,384]{1,0:T(2,128)S(1)} %fusion.13), channel_id=1, source_target_pairs={{0,1},{1,0},{2,3},{3,2},{4,5},{5,4},{6,7},{7,6},{8,9},{9,8},{10,11... | collective-permute-start | bytes 9224 | tf_op jit(solution)/shard_map/ppermute | solution.py:1091
  156.2 1.0 copy-start.8
  199.1 1.5 collective-permute-start.2
  244.6 41.2 %collective-permute-start.4 = (bf16[1536,384]{1,0:T(8,128)(2,1)}, bf16[1536,384]{1,0:T(8,128)(2,1)S(1)}, u32[]{:S(2)}, u32[]{:S(2)}) collective-permute-start(bf16[1536,384]{1,0:T(8,128)(2,1)} %get-tuple-element.103), channel_id=1, source_target_pairs={{0,1},{1,0},{2,3},{3,2},{4,5},{5,4},{6,7},{7,6},{8,9},{9,8},{10,11... | collective-permute-start | bytes 3538952 | tf_op jit(solution)/shard_map/ppermute | solution.py:1091
  244.9 20.9 %copy-start.18 = (bf16[1536,768]{1,0:T(8,128)(2,1)S(1)}, bf16[1536,768]{1,0:T(8,128)(2,1)}, u32[]{:S(2)}) copy-start(bf16[1536,768]{1,0:T(8,128)(2,1)} %get-tuple-element.95) | copy-start | bytes 7077892
  244.9 20.9 %copy-start.19 = (bf16[1536,768]{1,0:T(8,128)(2,1)S(1)}, bf16[1536,768]{1,0:T(8,128)(2,1)}, u32[]{:S(2)}) copy-start(bf16[1536,768]{1,0:T(8,128)(2,1)} %get-tuple-element.96) | copy-start | bytes 7077892
  265.7 3.1 copy-start.17
  268.9 3.2 copy-start.16
  272.0 3.1 copy-start.21
  272.0 3.1 copy-start.22
  275.2 2.0 copy-start.9
  277.2 3.0 copy-start.15
  277.2 3.1 copy-start.20
  285.8 1.0 copy-start.10
  412.5 3.1 collective-permute-start.5
  412.9 6.2 %collective-permute-start.6 = (bf16[1536,384]{1,0:T(8,128)(2,1)}, bf16[1536,384]{1,0:T(8,128)(2,1)S(1)}, u32[]{:S(2)}, u32[]{:S(2)}) collective-permute-start(bf16[1536,384]{1,0:T(8,128)(2,1)} %get-tuple-element.111), channel_id=1, source_target_pairs={{0,1},{1,0},{2,3},{3,2},{4,5},{5,4},{6,7},{7,6},{8,9},{9,8},{10,11... | collective-permute-start | bytes 3538952 | tf_op jit(solution)/shard_map/ppermute | solution.py:1091
  413.1 6.1 %collective-permute-start.7 = (bf16[1536,384]{1,0:T(8,128)(2,1)}, bf16[1536,384]{1,0:T(8,128)(2,1)}, u32[]{:S(2)}, u32[]{:S(2)}) collective-permute-start(bf16[1536,384]{1,0:T(8,128)(2,1)} %get-tuple-element.112), channel_id=1, source_target_pairs={{0,1},{1,0},{2,3},{3,2},{4,5},{5,4},{6,7},{7,6},{8,9},{9,8},{10,11... | collective-permute-start | bytes 3538952 | tf_op jit(solution)/shard_map/ppermute | solution.py:1091
  415.6 3.5 copy-start.11
  419.0 1.0 copy-start.12
  440.4 51.5 %copy-start.4 = (f32[1,24,2304]{2,1,0:T(8,128)S(1)}, f32[1,24,2304]{2,1,0:T(8,128)}, u32[]{:S(2)}) copy-start(f32[1,24,2304]{2,1,0:T(8,128)} %param.23) | copy-start | bytes 663556
  440.4 51.5 %copy-start.5 = (f32[1,24,2304]{2,1,0:T(8,128)S(1)}, f32[1,24,2304]{2,1,0:T(8,128)}, u32[]{:S(2)}) copy-start(f32[1,24,2304]{2,1,0:T(8,128)} %param.28) | copy-start | bytes 663556
  462.2 31.5 %copy-start.6 = (f32[1,24,2304]{2,1,0:T(8,128)S(1)}, f32[1,24,2304]{2,1,0:T(8,128)}, u32[]{:S(2)}) copy-start(f32[1,24,2304]{2,1,0:T(8,128)} %param.33) | copy-start | bytes 663556
  492.0 8.4 %copy-start.1 = (bf16[256,384]{1,0:T(8,128)(2,1)S(1)}, bf16[256,384]{1,0:T(8,128)(2,1)}, u32[]{:S(2)}) copy-start(bf16[256,384]{1,0:T(8,128)(2,1)} %param.22) | copy-start | bytes 589828
  493.7 6.6 %copy-start.3 = (f32[24,2304]{1,0:T(8,128)}, f32[24,2304]{1,0:T(8,128)S(1)}, u32[]{:S(2)}) copy-start(f32[24,2304]{1,0:T(8,128)S(1)} %get-tuple-element.140) | copy-start | bytes 663556
  493.7 5.9 %copy-start.2 = (f32[24,2304]{1,0:T(8,128)S(1)}, f32[24,2304]{1,0:T(8,128)}, u32[]{:S(2)}) copy-start(f32[24,2304]{1,0:T(8,128)} %comm_scatter.1) | copy-start | bytes 663556
  (1 other events, 0.6 us)
Sparse Core Ops, SparseCore 0:
  11.6 113.5 all-gather.1
  285.9 176.2 reduce-scatter.3

commit v7 on v6

--- a/solution.py
+++ b/solution.py
@@ -438,6 +438,11 @@
         fill_masks(e0,e1,kaug,q0,q1,rows,BK)
         kaug[rows:,0:128]=jnp.zeros((BK,128),BF)
         vt[:,:]=jnp.where(lax.broadcasted_iota(jnp.int32,vt.shape,0)%80>=64,1.0,0.0).astype(BF)
+    pick_r=lax.broadcasted_iota(jnp.int32,(16,128),0)
+    pick_l=lax.broadcasted_iota(jnp.int32,(16,128),1)
+    pick=jnp.where(pick_l//64==pick_r,1.0,0.0).astype(BF)
+    q_top=jnp.zeros((16,1),F32)
+    k_top=jnp.zeros((16,1),F32)
     lane=lax.broadcasted_iota(jnp.int32,(half,128),1)
     for own,(q,k,v) in ((True,(qo,ko,vo)),(False,(qr,kr,vr))):
         at=pl.multiple_of((pos if own else 1-pos)*half,half)
@@ -445,10 +450,32 @@
         zero=jnp.zeros_like(scaled)
         q0[pl.ds(at,half),0:128]=jnp.where(lane<64,scaled,zero)
         q1[pl.ds(at,half),0:128]=jnp.where(lane<64,zero,scaled)
-        kaug[pl.ds(at,half),0:128]=k[...]
+        kb=k[...]
+        kaug[pl.ds(at,half),0:128]=kb
+        q_top=jnp.maximum(q_top,jnp.max(nt(pick,scaled*scaled),axis=1,keepdims=True))
+        k_top=jnp.maximum(k_top,jnp.max(nt(pick,kb*kb),axis=1,keepdims=True))
         turned=v[...].T
         vt[0:64,pl.ds(at,half)]=turned[0:64]
         vt[80:144,pl.ds(at,half)]=turned[64:128]
+    narrow=jnp.max(q_top*k_top)*1.05<=1600.0
+    def qnarrow(i,_):
+        r0=pl.multiple_of(i*BQ,BQ)
+        base,count=key_range(i,e0,e1)
+        qs=(q0[pl.ds(r0,BQ),:],q1[pl.ds(r0,BQ),:])
+        def step(j,carry):
+            k0=pl.multiple_of(base+j*BK,128)
+            kb=kaug[pl.ds(k0,BK),:]
+            pt=[jnp.exp(nt(kb,qs[h])).astype(BF) for h in range(2)]
+            return tuple(carry[h]+nn(vt[80*h:80*h+80,pl.ds(k0,BK)],pt[h]) for h in range(2))
+        init=jnp.zeros((80,BQ),F32)
+        res=lax.fori_loop(0,count,step,(init,init))
+        outs=[]
+        for h in range(2):
+            l=jnp.maximum(res[h][64:65],1e-30)
+            outs.append(res[h][0:64]/l)
+            lse[0,h:h+1,pl.ds(r0,BQ)]=jnp.log(l)
+        put(i,jnp.concatenate(outs,axis=0).T.astype(BF))
+        return 0
     def qblock(i,_):
         r0=pl.multiple_of(i*BQ,BQ)
         base,count=key_range(i,e0,e1)
@@ -483,7 +510,10 @@
         @pl.when((local<0)|(local>=half))
         def _(): ox[pl.ds(pl.multiple_of(i*BQ-(1-pos)*half,BQ),BQ),:]=ob
     used=(e1+BQ-1)//BQ
-    lax.fori_loop(0,used,qblock,0)
+    @pl.when(narrow)
+    def _(): lax.fori_loop(0,used,qnarrow,0)
+    @pl.when(jnp.logical_not(narrow))
+    def _(): lax.fori_loop(0,used,qblock,0)
     def blank(i,_):
         r0=pl.multiple_of(i*BQ,BQ)
         lse[0,:,pl.ds(r0,BQ)]=jnp.zeros((8,BQ),F32)
@@ -1150,7 +1180,6 @@
     sums=lax.psum_scatter(terms,("dp","dim"),scatter_dimension=0,tiled=True)
     backs=attend_bwd(ctl,own,recv,d_own,d_recv,o_own,o_oth,lse,cos,sin)
     token_grads,grad_mix=tail(ctl,tokens,backs[0:3],[swap_cores(g) for g in backs[3:6]],w_mix,grad_first)
-    grad_mix,sums=lax.optimization_barrier((grad_mix,sums))
     total_rows=group_rows*lax.axis_size("dp")
     matrix_rate=1.0/math.sqrt(total_rows)
     norm_rate=0.3/math.sqrt(total_rows)

time: 517 us -> 508 us (0.983)
  waiting for transfers between devices: 33.2 us -> 11.4 us
  Pallas kernels: 394 us -> 408 us
    optimization_barrier x1 -> x0, waiting for transfers between devices: 21.8 us -> none  [body(): grad_mix, sums = lax.optimization_barrier((grad_mix, sums))]
    pallas_call x1, Pallas kernels: 29.7 us -> 43 us  [ring_scatter(): pl.pallas_call(scatter_kernel, in_specs=[pl.BlockSpec(memory_space=pl.ANY...]
  transfers between devices with their start and end apart: 10 -> 10, of which waited for: 7 -> 6; matrix products, arithmetic and copies ran while one was open for 11% -> 11% of each run, Pallas kernels for 62% -> 71%
where the time goes in v7:
time: 508 us; the launch traced here: 499 us
  Pallas kernels  408 us (80%)
  matrix products  37.6 us (7%)
  between operations  16.1 us (3%)
  other arithmetic  14.2 us (3%)
  waiting for transfers between devices  11.4 us (2%)
  local copies, waits for them, and re-layouts  9.65 us (2%)
    pallas_call x1, Pallas kernels, attend_bwd(): pl.pallas_call(bwd_kernel, grid_spec=pltpu.PrefetchScalarGridSpec(num_sca...  126 us
    pallas_call x1, Pallas kernels, attend_fwd(): pl.pallas_call(fwd_kernel, grid_spec=pltpu.PrefetchScalarGridSpec(num_sca...  79.3 us
    pallas_call x1, Pallas kernels, ffn_bwd(): pl.pallas_call(ffn_bwd_kernel, grid_spec=pltpu.PrefetchScalarGridSpec(num...  43.4 us
    pallas_call x1, Pallas kernels, ring_scatter(): pl.pallas_call(scatter_kernel, in_specs=[pl.BlockSpec(memory_space=pl.ANY...  43 us
    pallas_call x1, Pallas kernels, ffn_fwd(): pl.pallas_call(ffn_fwd_kernel, grid_spec=pltpu.PrefetchScalarGridSpec(num...  41.8 us
    dot_general x7, matrix products, inner_rows(): lax.dot_general(left_op, right_op, (((0,), (0,)), ((), ())), preferred_el...  37.4 us
    pallas_call x1, Pallas kernels, ring_gather(): pl.pallas_call(gather_kernel, in_specs=[pl.BlockSpec(memory_space=pltpu.V...  33.8 us
    pallas_call x1, Pallas kernels, tail(): pl.pallas_call(tail_kernel, grid_spec=pltpu.PrefetchScalarGridSpec(num_sc...  20.4 us
  transfers between devices with their start and end apart: 10, of which 6 were waited for; matrix products, arithmetic and copies ran while one was open for 11% of the time, Pallas kernels for 71%

profile of v7, /device:TPU:0, one launch (start us, length us, event | category | flops | bytes accessed | tf_op | source)
XLA Modules:
  0.0 499.3 jit_solution(15329882110698294585)
XLA Ops:
  7.3 3.2 make_bundle.1
  10.5 33.8 %comm_gather.1 = bf16[4,2,2,2,24,2304]{5,4,3,2,1,0:T(8,128)(2,1)} custom-call(f32[24,2304]{1,0:T(8,128)} %bitcast.95), custom_call_target="tpu_custom_call" | custom-call | bytes 70778880 | tf_op jit(solution)/shard_map/comm_gather/pallas_call | solution.py:879
  46.2 1.2 pad_add_fusion.ctl
  48.1 7.1 %fusion.2 = (f32[3072,128]{1,0:T(8,128)}, f32[3072,128]{1,0:T(8,128)}) fusion(f32[128]{0:T(128)S(1)} %get-tuple-element.142, f32[128]{0:T(128)S(1)} %get-tuple-element.143, f32[3072]{0:T(1024)S(1)} %subtract_convert_fusion), kind=kLoop, calls=%fused_computation.6 | loop fusion | flops 786432 | bytes 3159040 | tf_op jit(solution)/shard_map/mul | solution.py:1158
  55.3 11.8 %mix.1 = (bf16[1536,1152]{1,0:T(8,128)(2,1)}, bf16[1536,1152]{1,0:T(8,128)(2,1)}) custom-call(s32[3]{0:T(128)} %pad_add_fusion.ctl, bf16[1536,768]{1,0:T(8,128)(2,1)} %x.9, bf16[768,2304]{1,0:T(8,128)(2,1)} %bitcast.86, f32[3072,128]{1,0:T(8,128)} %get-tuple-element.139.cos, f32[3072,128]{1,0:T(8,128)} %get-tuple-element.138.sin), custom_call_target="tpu_custom_call" | custom-call | flops 5435817984 | bytes 12976128 | tf_op jit(solution)/shard_map/mix/pallas_call | solution.py:1110
  67.5 6.2 %collective-permute-done.qr.kr.vr = bf16[1536,1152]{1,0:T(8,128)(2,1)} collective-permute-done((bf16[1536,1152]{1,0:T(8,128)(2,1)}, bf16[1536,1152]{1,0:T(8,128)(2,1)}, u32[]{:S(2)}, u32[]{:S(2)}) %collective-permute-start) | collective-permute-done | bytes 3538976 | tf_op jit(solution)/shard_map/ppermute | solution.py:1121
  73.7 79.3 %attend_fwd.1 = (bf16[1536,384]{1,0:T(8,128)(2,1)}, bf16[1536,384]{1,0:T(8,128)(2,1)}, f32[3,8,3072]{2,1,0:T(8,128)}) custom-call(s32[3]{0:T(128)} %pad_add_fusion.ctl, bf16[1536,1152]{1,0:T(8,128)(2,1)} %get-tuple-element.81.qo.ko.vo, bf16[1536,1152]{1,0:T(8,128)(2,1)} %get-tuple-element.81.qo.ko.vo, bf16[1536,1152]{1,0:T(8,128)(2,1)} %get-tuple-element.81.qo.ko.vo, ...), custom_call_target="tpu_custom_call" | custom-call | flops 7247757312 | bytes 17694720 | tf_op jit(solution)/shard_map/attend_fwd/pallas_call | solution.py:530
  154.3 0.9 slice.27
  156.1 1.0 copy-done.8
  157.2 41.8 %ffn_fwd.1 = (f32[1536,768]{1,0:T(8,128)}, f32[1536,768]{1,0:T(8,128)}, f32[1536,256]{1,0:T(8,128)}, bf16[1536,768]{1,0:T(8,128)(2,1)}, bf16[1536,768]{1,0:T(8,1...) custom-call(s32[3]{0:T(128)} %pad_add_fusion.ctl, ...), custom_call_target="tpu_custom_call" | custom-call | flops 23555211264 | bytes 60162048 | tf_op jit(solution)/shard_map/ffn_fwd/pallas_call | solution.py:706
  201.2 43.4 %ffn_bwd.1 = (f32[8,768]{1,0:T(8,128)}, bf16[1536,768]{1,0:T(8,128)(2,1)}, bf16[1536,6144]{1,0:T(8,128)(2,1)}, f32[1536,768]{1,0:T(8,128)}, bf16[1536,768]{1,0:T...) custom-call(s32[3]{0:T(128)} %pad_add_fusion.ctl, ...), custom_call_target="tpu_custom_call" | custom-call | flops 23555211264 | bytes 74317824 | tf_op jit(solution)/shard_map/ffn_bwd/pallas_call | solution.py:786
  244.9 20.9 %fusion = bf16[768,10112]{1,0:T(8,128)(2,1)} fusion(bf16[1536,768]{1,0:T(8,128)(2,1)} %get-tuple-element.91, bf16[1536,6144]{1,0:T(8,128)(2,1)} %get-tuple-element.92), kind=kOutput, calls=%fused_computation.1 | convolution fusion | flops 14500233216 | bytes 30670848 | tf_op jit(solution)/shard_map/dot_general | solution.py:30
  265.8 3.1 fusion.6
  269.0 3.2 fusion.5
  272.1 3.1 fusion.4
  275.2 1.1 fusion.23
  276.4 0.7 slice.31
  277.3 2.9 fusion.24
  280.4 3.2 fusion.3
  283.5 1.5 fusion.7
  285.1 0.8 constant_dynamic-update-slice_fusion
  285.9 1.0 copy-done.10
  286.9 125.7 %attend_bwd.1 = (bf16[1536,384]{1,0:T(8,128)(2,1)}, bf16[1536,384]{1,0:T(8,128)(2,1)}, bf16[1536,384]{1,0:T(8,128)(2,1)}, bf16[1536,384]{1,0:T(8,128)(2,1)}, bf1...) custom-call(s32[3]{0:T(128)} %pad_add_fusion.ctl, bf16[1536,1152]{1,0:T(8,128)(2,1)} %get-tuple-element.81.qo.ko.vo, ...), custom_call_target="tpu_custom_call" | custom-call | flops 18119393280 | bytes 35389440 | tf_op jit(solution)/shard_map/attend_bwd/pallas_call | solution.py:633
  413.3 1.3 constant_dynamic-slice_fusion
  414.6 1.1 collective-permute-done.5.qr
  415.7 3.4 collective-permute-done.6.kr
  419.2 0.9 copy-done.12
  420.1 20.4 %tail.1 = (f32[1536,768]{1,0:T(8,128)}, bf16[768,2304]{1,0:T(8,128)(2,1)}) custom-call(s32[3]{0:T(128)} %pad_add_fusion.ctl, bf16[1536,768]{1,0:T(8,128)(2,1)} %x.9, bf16[1536,384]{1,0:T(8,128)(2,1)} %get-tuple-element.105.qo, bf16[1536,384]{1,0:T(8,128)(2,1)} %get-tuple-element.106.ko, bf16[1536,384]{1,0:T(8,128)(2,1)} %get-tuple-element.107.vo, ...), custom_call_target="tpu_custom_call" | custom-call | flops 10871635968 | bytes 33030144 | tf_op jit(solution)/shard_map/tail/pallas_call | solution.py:1069
  440.6 43.0 %comm_scatter.1 = f32[24,2304]{1,0:T(8,128)} custom-call(bf16[16,2,24,2304]{3,2,1,0:T(8,128)(2,1)} %bitcast.88), custom_call_target="tpu_custom_call" | custom-call | bytes 70778880 | tf_op jit(solution)/shard_map/comm_scatter/pallas_call | solution.py:953
  483.6 1.8 convert_bitcast_fusion
  485.4 0.7 fusion.9
  486.1 5.2 %update.1 = (f32[24,6144]{1,0:T(8,128)}, f32[24,6144]{1,0:T(8,128)}, f32[24,6144]{1,0:T(8,128)}, f32[24,6144]{1,0:T(8,128)}, bf16[24,6144]{1,0:T(8,128)(2,1)}, /...) custom-call(bf16[24,10112]{1,0:T(8,128)(2,1)} %reduce-scatter.4.clon, ...), custom_call_target="tpu_custom_call" | custom-call | flops 150994944 | bytes 12582912 | tf_op jit(solution)/shard_map/update/pallas_call | solution.py:1034
  (77 shorter events, 8.4 us)
Async XLA Ops:
  7.2 146.3 %copy-start = (bf16[256,384]{1,0:T(8,128)(2,1)S(1)}, bf16[256,384]{1,0:T(8,128)(2,1)}, u32[]{:S(2)}) copy-start(bf16[256,384]{1,0:T(8,128)(2,1)} %param.22) | copy-start | bytes 589828
  7.2 147.0 %all-gather.2.cloned.1.call-start = ((), (), s32[]{:S(2)}) async-start(), calls=%async_computation.1 | async-start | bytes 16017408 | tf_op jit(solution)/shard_map/all_gather | solution.py:1142
  10.4 33.9 %copy-start.7 = (s32[1,2]{1,0:T(1,128)S(1)}, s32[1,2]{1,0:T(1,128)}, u32[]{:S(2)}) copy-start(s32[1,2]{1,0:T(1,128)} %param.20) | copy-start | bytes 28
  10.5 475.6 %reduce-scatter.4.cloned.1.call-start = ((), (), s32[]{:S(2)}) async-start(), calls=%async_computation.2 | async-start | bytes 16017408
  67.1 6.6 %collective-permute-start = (bf16[1536,1152]{1,0:T(8,128)(2,1)}, bf16[1536,1152]{1,0:T(8,128)(2,1)}, u32[]{:S(2)}, u32[]{:S(2)}) collective-permute-start(bf16[1536,1152]{1,0:T(8,128)(2,1)} %get-tuple-element.82), channel_id=1, source_target_pairs={{0,1},{1,0},{2,3},{3,2},{4,5},{5,4},{6,7},{7,6},{8,9},{9,8},{10,11... | collective-permute-start | bytes 10616840 | tf_op jit(solution)/shard_map/ppermute | solution.py:1121
  73.7 79.8 %copy-start.14 = (s32[2]{0:T(128)S(1)}, s32[2]{0:T(128)}, u32[]{:S(2)}) copy-start(s32[2]{0:T(128)} %param.21) | copy-start | bytes 28
  153.0 3.2 collective-permute-start.1
  153.6 45.9 %collective-permute-start.3 = (f32[2,384]{1,0:T(2,128)S(1)}, f32[2,384]{1,0:T(2,128)S(1)}, u32[]{:S(2)}, u32[]{:S(2)}) collective-permute-start(f32[2,384]{1,0:T(2,128)S(1)} %fusion.13), channel_id=1, source_target_pairs={{0,1},{1,0},{2,3},{3,2},{4,5},{5,4},{6,7},{7,6},{8,9},{9,8},{10,11... | collective-permute-start | bytes 9224 | tf_op jit(solution)/shard_map/ppermute | solution.py:1121
  156.1 1.0 copy-start.8
  199.0 1.5 collective-permute-start.2
  244.5 41.3 %collective-permute-start.4 = (bf16[1536,384]{1,0:T(8,128)(2,1)}, bf16[1536,384]{1,0:T(8,128)(2,1)S(1)}, u32[]{:S(2)}, u32[]{:S(2)}) collective-permute-start(bf16[1536,384]{1,0:T(8,128)(2,1)} %get-tuple-element.101), channel_id=1, source_target_pairs={{0,1},{1,0},{2,3},{3,2},{4,5},{5,4},{6,7},{7,6},{8,9},{9,8},{10,11... | collective-permute-start | bytes 3538952 | tf_op jit(solution)/shard_map/ppermute | solution.py:1121
  244.9 20.9 %copy-start.18 = (bf16[1536,768]{1,0:T(8,128)(2,1)S(1)}, bf16[1536,768]{1,0:T(8,128)(2,1)}, u32[]{:S(2)}) copy-start(bf16[1536,768]{1,0:T(8,128)(2,1)} %get-tuple-element.93) | copy-start | bytes 7077892
  244.9 20.9 %copy-start.19 = (bf16[1536,768]{1,0:T(8,128)(2,1)S(1)}, bf16[1536,768]{1,0:T(8,128)(2,1)}, u32[]{:S(2)}) copy-start(bf16[1536,768]{1,0:T(8,128)(2,1)} %get-tuple-element.94) | copy-start | bytes 7077892
  265.8 3.1 copy-start.17
  269.0 3.2 copy-start.16
  272.1 3.1 copy-start.21
  272.1 3.1 copy-start.22
  275.2 2.0 copy-start.9
  277.3 3.0 copy-start.15
  277.3 3.1 copy-start.20
  285.9 1.0 copy-start.10
  412.6 3.1 collective-permute-start.5
  412.8 6.3 %collective-permute-start.6 = (bf16[1536,384]{1,0:T(8,128)(2,1)}, bf16[1536,384]{1,0:T(8,128)(2,1)S(1)}, u32[]{:S(2)}, u32[]{:S(2)}) collective-permute-start(bf16[1536,384]{1,0:T(8,128)(2,1)} %get-tuple-element.109), channel_id=1, source_target_pairs={{0,1},{1,0},{2,3},{3,2},{4,5},{5,4},{6,7},{7,6},{8,9},{9,8},{10,11... | collective-permute-start | bytes 3538952 | tf_op jit(solution)/shard_map/ppermute | solution.py:1121
  413.2 6.1 %collective-permute-start.7 = (bf16[1536,384]{1,0:T(8,128)(2,1)}, bf16[1536,384]{1,0:T(8,128)(2,1)}, u32[]{:S(2)}, u32[]{:S(2)}) collective-permute-start(bf16[1536,384]{1,0:T(8,128)(2,1)} %get-tuple-element.110), channel_id=1, source_target_pairs={{0,1},{1,0},{2,3},{3,2},{4,5},{5,4},{6,7},{7,6},{8,9},{9,8},{10,11... | collective-permute-start | bytes 3538952 | tf_op jit(solution)/shard_map/ppermute | solution.py:1121
  415.7 3.5 copy-start.11
  419.1 1.0 copy-start.12
  440.5 43.1 %copy-start.4 = (f32[1,24,2304]{2,1,0:T(8,128)S(1)}, f32[1,24,2304]{2,1,0:T(8,128)}, u32[]{:S(2)}) copy-start(f32[1,24,2304]{2,1,0:T(8,128)} %param.23) | copy-start | bytes 663556
  440.5 43.1 %copy-start.5 = (f32[1,24,2304]{2,1,0:T(8,128)S(1)}, f32[1,24,2304]{2,1,0:T(8,128)}, u32[]{:S(2)}) copy-start(f32[1,24,2304]{2,1,0:T(8,128)} %param.28) | copy-start | bytes 663556
  440.5 44.8 %copy-start.6 = (f32[1,24,2304]{2,1,0:T(8,128)S(1)}, f32[1,24,2304]{2,1,0:T(8,128)}, u32[]{:S(2)}) copy-start(f32[1,24,2304]{2,1,0:T(8,128)} %param.33) | copy-start | bytes 663556
  483.6 8.4 %copy-start.1 = (bf16[256,384]{1,0:T(8,128)(2,1)S(1)}, bf16[256,384]{1,0:T(8,128)(2,1)}, u32[]{:S(2)}) copy-start(bf16[256,384]{1,0:T(8,128)(2,1)} %param.22) | copy-start | bytes 589828
  485.4 6.6 %copy-start.3 = (f32[24,2304]{1,0:T(8,128)}, f32[24,2304]{1,0:T(8,128)S(1)}, u32[]{:S(2)}) copy-start(f32[24,2304]{1,0:T(8,128)S(1)} %get-tuple-element.136) | copy-start | bytes 663556
  485.4 5.9 %copy-start.2 = (f32[24,2304]{1,0:T(8,128)S(1)}, f32[24,2304]{1,0:T(8,128)}, u32[]{:S(2)}) copy-start(f32[24,2304]{1,0:T(8,128)} %comm_scatter.1) | copy-start | bytes 663556
  (1 other events, 0.6 us)
Sparse Core Ops, SparseCore 0:
  11.6 113.5 all-gather.1
  286.0 177.1 reduce-scatter.3

commit v8 on v7

--- a/solution.py
+++ b/solution.py
@@ -1,3 +1,4 @@
+import functools
 import math
 
 import jax
@@ -405,6 +406,7 @@
 BQ=512
 ROWS=256
 BK=384
+FK=512
 F32=jnp.float32
 BF=jnp.bfloat16
 
@@ -420,23 +422,23 @@
     q0[:,128:256]=qm
     q1[:,128:256]=qm
 
-def key_range(i,e0,e1):
+def key_range(i,e0,e1,step):
     first=i*BQ
     last=jnp.minimum(first+BQ,e1)-1
     lo=jnp.where(first>=e0,e0,0)
     hi=jnp.where(last>=e0,e1,e0)
     base=(lo//128)*128
-    return pl.multiple_of(base,128),(hi-base+BK-1)//BK
+    return pl.multiple_of(base,128),(hi-base+step-1)//step
 
 def fwd_kernel(ctl,qo,ko,vo,qr,kr,vr,oo,ox,lse,kaug,q0,q1,vt):
-    rows=kaug.shape[0]-BK
+    rows=kaug.shape[0]-FK
     half=rows//2
     pos,e0,e1=ctl[0],ctl[1],ctl[2]
     p=pl.program_id(0)
     @pl.when(p==0)
     def _():
-        fill_masks(e0,e1,kaug,q0,q1,rows,BK)
-        kaug[rows:,0:128]=jnp.zeros((BK,128),BF)
+        fill_masks(e0,e1,kaug,q0,q1,rows,FK)
+        kaug[rows:,0:128]=jnp.zeros((FK,128),BF)
         vt[:,:]=jnp.where(lax.broadcasted_iota(jnp.int32,vt.shape,0)%80>=64,1.0,0.0).astype(BF)
     pick_r=lax.broadcasted_iota(jnp.int32,(16,128),0)
     pick_l=lax.broadcasted_iota(jnp.int32,(16,128),1)
@@ -460,36 +462,36 @@
     narrow=jnp.max(q_top*k_top)*1.05<=1600.0
     def qnarrow(i,_):
         r0=pl.multiple_of(i*BQ,BQ)
-        base,count=key_range(i,e0,e1)
+        base,count=key_range(i,e0,e1,FK)
         qs=(q0[pl.ds(r0,BQ),:],q1[pl.ds(r0,BQ),:])
         def step(j,carry):
-            k0=pl.multiple_of(base+j*BK,128)
-            kb=kaug[pl.ds(k0,BK),:]
+            k0=pl.multiple_of(base+j*FK,128)
+            kb=kaug[pl.ds(k0,FK),:]
             pt=[jnp.exp(nt(kb,qs[h])).astype(BF) for h in range(2)]
-            return tuple(carry[h]+nn(vt[80*h:80*h+80,pl.ds(k0,BK)],pt[h]) for h in range(2))
+            return tuple(carry[h]+nn(vt[80*h:80*h+80,pl.ds(k0,FK)],pt[h]) for h in range(2))
         init=jnp.zeros((80,BQ),F32)
         res=lax.fori_loop(0,count,step,(init,init))
         outs=[]
         for h in range(2):
             l=jnp.maximum(res[h][64:65],1e-30)
             outs.append(res[h][0:64]/l)
-            lse[0,h:h+1,pl.ds(r0,BQ)]=jnp.log(l)
+            lse[0,h:h+1,pl.ds(r0,BQ)]=jnp.where(l>1e-30,jnp.log(l),1e30)
         put(i,jnp.concatenate(outs,axis=0).T.astype(BF))
         return 0
     def qblock(i,_):
         r0=pl.multiple_of(i*BQ,BQ)
-        base,count=key_range(i,e0,e1)
+        base,count=key_range(i,e0,e1,FK)
         qs=(q0[pl.ds(r0,BQ),:],q1[pl.ds(r0,BQ),:])
         def step(j,carry):
-            k0=pl.multiple_of(base+j*BK,128)
-            kb=kaug[pl.ds(k0,BK),:]
+            k0=pl.multiple_of(base+j*FK,128)
+            kb=kaug[pl.ds(k0,FK),:]
             scores=[nt(kb,qs[h]) for h in range(2)]
             out=[]
             for h in range(2):
                 m,acc=carry[h]
                 mn=jnp.maximum(m,jnp.max(scores[h],axis=0,keepdims=True))
                 pt=jnp.exp(scores[h]-mn).astype(BF)
-                acc=acc*jnp.exp(m-mn)+nn(vt[80*h:80*h+80,pl.ds(k0,BK)],pt)
+                acc=acc*jnp.exp(m-mn)+nn(vt[80*h:80*h+80,pl.ds(k0,FK)],pt)
                 out.append((mn,acc))
             return tuple(out)
         init=(jnp.full((1,BQ),-jnp.inf,F32),jnp.zeros((80,BQ),F32))
@@ -499,7 +501,7 @@
             m,acc=res[h]
             l=acc[64:65]
             outs.append(acc[0:64]/l)
-            lse[0,h:h+1,pl.ds(r0,BQ)]=m+jnp.log(l)
+            lse[0,h:h+1,pl.ds(r0,BQ)]=jnp.where(m>-1e29,m+jnp.log(l),1e30)
         ob=jnp.concatenate(outs,axis=0).T.astype(BF)
         put(i,ob)
         return 0
@@ -531,7 +533,7 @@
         grid_spec=pltpu.PrefetchScalarGridSpec(num_scalar_prefetch=1,grid=(pairs,),
           in_specs=sp+sp,
           out_specs=[pl.BlockSpec((half,128),lambda p,c:(0,p))]*2+[pl.BlockSpec((1,8,rows),lambda p,c:(p,0,0))],
-          scratch_shapes=[pltpu.VMEM((rows+BK,256),BF),pltpu.VMEM((rows,256),BF),pltpu.VMEM((rows,256),BF),pltpu.VMEM((160,rows+BK),BF)]),
+          scratch_shapes=[pltpu.VMEM((rows+FK,256),BF),pltpu.VMEM((rows,256),BF),pltpu.VMEM((rows,256),BF),pltpu.VMEM((160,rows+FK),BF)]),
         out_shape=[jax.ShapeDtypeStruct((half,outw),BF)]*2+[jax.ShapeDtypeStruct((pairs,8,rows),F32)],
         compiler_params=pltpu.CompilerParams(vmem_limit_bytes=60<<20,dimension_semantics=("arbitrary",)),
         cost_estimate=pl.CostEstimate(flops=4*rows*rows*64*2*pairs//2,bytes_accessed=10*half*width,transcendentals=rows*rows*pairs),
@@ -545,7 +547,7 @@
     p=pl.program_id(0)
     @pl.when(p==0)
     def _():
-        fill_masks(e0,e1,kaug,q0,q1,rows,BK)
+        fill_masks(e0,e1,kaug,q0,q1,rows,kaug.shape[0]-rows)
         kaug[rows:,0:128]=jnp.zeros((BK,128),BF)
         vs[rows:,:]=jnp.zeros((BK,128),BF)
         kt[:,rows:]=jnp.zeros((128,BK),BF)
@@ -584,7 +586,7 @@
         return x*cos[pl.ds(r0,ROWS),:]-swapped*sin[pl.ds(r0,ROWS),:]
     def qblock(i,_):
         r0=pl.multiple_of(i*BQ,BQ)
-        base,count=key_range(i,e0,e1)
+        base,count=key_range(i,e0,e1,BK)
         qs=(q0[pl.ds(r0,BQ),:],q1[pl.ds(r0,BQ),:])
         ds_=(d0[pl.ds(r0,BQ),:],d1[pl.ds(r0,BQ),:])
         ls=[lse[0,h:h+1,pl.ds(r0,BQ)] for h in range(2)]

time: 508 us -> 505 us (level)
  no operation moved by 1% of the time
where the time goes in v8:
time: 505 us; the launch traced here: 497 us
  Pallas kernels  405 us (80%)
  matrix products  37.6 us (7%)
  between operations  16.1 us (3%)
  other arithmetic  14.2 us (3%)
  waiting for transfers between devices  11.4 us (2%)
  local copies, waits for them, and re-layouts  9.65 us (2%)
    pallas_call x1, Pallas kernels, attend_bwd(): pl.pallas_call(bwd_kernel, grid_spec=pltpu.PrefetchScalarGridSpec(num_sca...  126 us
    pallas_call x1, Pallas kernels, attend_fwd(): pl.pallas_call(fwd_kernel, grid_spec=pltpu.PrefetchScalarGridSpec(num_sca...  80 us
    pallas_call x1, Pallas kernels, ffn_bwd(): pl.pallas_call(ffn_bwd_kernel, grid_spec=pltpu.PrefetchScalarGridSpec(num...  43.4 us
    pallas_call x1, Pallas kernels, ffn_fwd(): pl.pallas_call(ffn_fwd_kernel, grid_spec=pltpu.PrefetchScalarGridSpec(num...  41.9 us
    pallas_call x1, Pallas kernels, ring_scatter(): pl.pallas_call(scatter_kernel, in_specs=[pl.BlockSpec(memory_space=pl.ANY...  39.4 us
    dot_general x7, matrix products, inner_rows(): lax.dot_general(left_op, right_op, (((0,), (0,)), ((), ())), preferred_el...  37.4 us
    pallas_call x1, Pallas kernels, ring_gather(): pl.pallas_call(gather_kernel, in_specs=[pl.BlockSpec(memory_space=pltpu.V...  33.8 us
    pallas_call x1, Pallas kernels, tail(): pl.pallas_call(tail_kernel, grid_spec=pltpu.PrefetchScalarGridSpec(num_sc...  20.6 us
  transfers between devices with their start and end apart: 10, of which 6 were waited for; matrix products, arithmetic and copies ran while one was open for 11% of the time, Pallas kernels for 71%

profile of v8, /device:TPU:0, one launch (start us, length us, event | category | flops | bytes accessed | tf_op | source)
XLA Modules:
  0.0 496.7 jit_solution(2147235506603880277)
XLA Ops:
  7.3 3.2 make_bundle.1
  10.5 33.8 %comm_gather.1 = bf16[4,2,2,2,24,2304]{5,4,3,2,1,0:T(8,128)(2,1)} custom-call(f32[24,2304]{1,0:T(8,128)} %bitcast.95), custom_call_target="tpu_custom_call" | custom-call | bytes 70778880 | tf_op jit(solution)/shard_map/comm_gather/pallas_call | solution.py:881
  46.2 1.2 pad_add_fusion.ctl
  48.1 7.1 %fusion.2 = (f32[3072,128]{1,0:T(8,128)}, f32[3072,128]{1,0:T(8,128)}) fusion(f32[128]{0:T(128)S(1)} %get-tuple-element.142, f32[128]{0:T(128)S(1)} %get-tuple-element.143, f32[3072]{0:T(1024)S(1)} %subtract_convert_fusion), kind=kLoop, calls=%fused_computation.6 | loop fusion | flops 786432 | bytes 3159040 | tf_op jit(solution)/shard_map/mul | solution.py:1160
  55.3 11.8 %mix.1 = (bf16[1536,1152]{1,0:T(8,128)(2,1)}, bf16[1536,1152]{1,0:T(8,128)(2,1)}) custom-call(s32[3]{0:T(128)} %pad_add_fusion.ctl, bf16[1536,768]{1,0:T(8,128)(2,1)} %x.9, bf16[768,2304]{1,0:T(8,128)(2,1)} %bitcast.86, f32[3072,128]{1,0:T(8,128)} %get-tuple-element.139.cos, f32[3072,128]{1,0:T(8,128)} %get-tuple-element.138.sin), custom_call_target="tpu_custom_call" | custom-call | flops 5435817984 | bytes 12976128 | tf_op jit(solution)/shard_map/mix/pallas_call | solution.py:1112
  67.5 6.2 %collective-permute-done.qr.kr.vr = bf16[1536,1152]{1,0:T(8,128)(2,1)} collective-permute-done((bf16[1536,1152]{1,0:T(8,128)(2,1)}, bf16[1536,1152]{1,0:T(8,128)(2,1)}, u32[]{:S(2)}, u32[]{:S(2)}) %collective-permute-start) | collective-permute-done | bytes 3538976 | tf_op jit(solution)/shard_map/ppermute | solution.py:1123
  73.7 80.0 %attend_fwd.1 = (bf16[1536,384]{1,0:T(8,128)(2,1)}, bf16[1536,384]{1,0:T(8,128)(2,1)}, f32[3,8,3072]{2,1,0:T(8,128)}) custom-call(s32[3]{0:T(128)} %pad_add_fusion.ctl, bf16[1536,1152]{1,0:T(8,128)(2,1)} %get-tuple-element.81.qo.ko.vo, bf16[1536,1152]{1,0:T(8,128)(2,1)} %get-tuple-element.81.qo.ko.vo, bf16[1536,1152]{1,0:T(8,128)(2,1)} %get-tuple-element.81.qo.ko.vo, ...), custom_call_target="tpu_custom_call" | custom-call | flops 7247757312 | bytes 17694720 | tf_op jit(solution)/shard_map/attend_fwd/pallas_call | solution.py:532
  154.9 0.9 slice.27
  156.8 1.0 copy-done.8
  157.8 41.9 %ffn_fwd.1 = (f32[1536,768]{1,0:T(8,128)}, f32[1536,768]{1,0:T(8,128)}, f32[1536,256]{1,0:T(8,128)}, bf16[1536,768]{1,0:T(8,128)(2,1)}, bf16[1536,768]{1,0:T(8,1...) custom-call(s32[3]{0:T(128)} %pad_add_fusion.ctl, ...), custom_call_target="tpu_custom_call" | custom-call | flops 23555211264 | bytes 60162048 | tf_op jit(solution)/shard_map/ffn_fwd/pallas_call | solution.py:708
  201.8 43.4 %ffn_bwd.1 = (f32[8,768]{1,0:T(8,128)}, bf16[1536,768]{1,0:T(8,128)(2,1)}, bf16[1536,6144]{1,0:T(8,128)(2,1)}, f32[1536,768]{1,0:T(8,128)}, bf16[1536,768]{1,0:T...) custom-call(s32[3]{0:T(128)} %pad_add_fusion.ctl, ...), custom_call_target="tpu_custom_call" | custom-call | flops 23555211264 | bytes 74317824 | tf_op jit(solution)/shard_map/ffn_bwd/pallas_call | solution.py:788
  245.6 20.9 %fusion = bf16[768,10112]{1,0:T(8,128)(2,1)} fusion(bf16[1536,768]{1,0:T(8,128)(2,1)} %get-tuple-element.91, bf16[1536,6144]{1,0:T(8,128)(2,1)} %get-tuple-element.92), kind=kOutput, calls=%fused_computation.1 | convolution fusion | flops 14500233216 | bytes 30670848 | tf_op jit(solution)/shard_map/dot_general | solution.py:31
  266.4 3.1 fusion.6
  269.6 3.2 fusion.5
  272.7 3.1 fusion.4
  275.8 1.1 fusion.23
  277.0 0.7 slice.31
  277.9 2.9 fusion.24
  281.0 3.2 fusion.3
  284.2 1.5 fusion.7
  285.7 0.8 constant_dynamic-update-slice_fusion
  286.5 1.0 copy-done.10
  287.5 126.0 %attend_bwd.1 = (bf16[1536,384]{1,0:T(8,128)(2,1)}, bf16[1536,384]{1,0:T(8,128)(2,1)}, bf16[1536,384]{1,0:T(8,128)(2,1)}, bf16[1536,384]{1,0:T(8,128)(2,1)}, bf1...) custom-call(s32[3]{0:T(128)} %pad_add_fusion.ctl, bf16[1536,1152]{1,0:T(8,128)(2,1)} %get-tuple-element.81.qo.ko.vo, ...), custom_call_target="tpu_custom_call" | custom-call | flops 18119393280 | bytes 35389440 | tf_op jit(solution)/shard_map/attend_bwd/pallas_call | solution.py:635
  414.2 1.3 constant_dynamic-slice_fusion
  415.5 1.1 collective-permute-done.5.qr
  416.6 3.4 collective-permute-done.6.kr
  420.1 0.9 copy-done.12
  421.1 20.6 %tail.1 = (f32[1536,768]{1,0:T(8,128)}, bf16[768,2304]{1,0:T(8,128)(2,1)}) custom-call(s32[3]{0:T(128)} %pad_add_fusion.ctl, bf16[1536,768]{1,0:T(8,128)(2,1)} %x.9, bf16[1536,384]{1,0:T(8,128)(2,1)} %get-tuple-element.105.qo, bf16[1536,384]{1,0:T(8,128)(2,1)} %get-tuple-element.106.ko, bf16[1536,384]{1,0:T(8,128)(2,1)} %get-tuple-element.107.vo, ...), custom_call_target="tpu_custom_call" | custom-call | flops 10871635968 | bytes 33030144 | tf_op jit(solution)/shard_map/tail/pallas_call | solution.py:1071
  441.7 39.4 %comm_scatter.1 = f32[24,2304]{1,0:T(8,128)} custom-call(bf16[16,2,24,2304]{3,2,1,0:T(8,128)(2,1)} %bitcast.88), custom_call_target="tpu_custom_call" | custom-call | bytes 70778880 | tf_op jit(solution)/shard_map/comm_scatter/pallas_call | solution.py:955
  481.1 1.8 convert_bitcast_fusion
  482.9 0.7 fusion.9
  483.6 5.2 %update.1 = (f32[24,6144]{1,0:T(8,128)}, f32[24,6144]{1,0:T(8,128)}, f32[24,6144]{1,0:T(8,128)}, f32[24,6144]{1,0:T(8,128)}, bf16[24,6144]{1,0:T(8,128)(2,1)}, /...) custom-call(bf16[24,10112]{1,0:T(8,128)(2,1)} %reduce-scatter.4.clon, ...), custom_call_target="tpu_custom_call" | custom-call | flops 150994944 | bytes 12582912 | tf_op jit(solution)/shard_map/update/pallas_call | solution.py:1036
  (77 shorter events, 8.3 us)
Async XLA Ops:
  7.2 146.9 %copy-start = (bf16[256,384]{1,0:T(8,128)(2,1)S(1)}, bf16[256,384]{1,0:T(8,128)(2,1)}, u32[]{:S(2)}) copy-start(bf16[256,384]{1,0:T(8,128)(2,1)} %param.22) | copy-start | bytes 589828
  7.2 147.7 %all-gather.2.cloned.1.call-start = ((), (), s32[]{:S(2)}) async-start(), calls=%async_computation.1 | async-start | bytes 16017408 | tf_op jit(solution)/shard_map/all_gather | solution.py:1144
  10.4 33.9 %copy-start.7 = (s32[1,2]{1,0:T(1,128)S(1)}, s32[1,2]{1,0:T(1,128)}, u32[]{:S(2)}) copy-start(s32[1,2]{1,0:T(1,128)} %param.20) | copy-start | bytes 28
  10.5 473.1 %reduce-scatter.4.cloned.1.call-start = ((), (), s32[]{:S(2)}) async-start(), calls=%async_computation.2 | async-start | bytes 16017408
  67.1 6.6 %collective-permute-start = (bf16[1536,1152]{1,0:T(8,128)(2,1)}, bf16[1536,1152]{1,0:T(8,128)(2,1)}, u32[]{:S(2)}, u32[]{:S(2)}) collective-permute-start(bf16[1536,1152]{1,0:T(8,128)(2,1)} %get-tuple-element.82), channel_id=1, source_target_pairs={{0,1},{1,0},{2,3},{3,2},{4,5},{5,4},{6,7},{7,6},{8,9},{9,8},{10,11... | collective-permute-start | bytes 10616840 | tf_op jit(solution)/shard_map/ppermute | solution.py:1123
  73.7 80.4 %copy-start.14 = (s32[2]{0:T(128)S(1)}, s32[2]{0:T(128)}, u32[]{:S(2)}) copy-start(s32[2]{0:T(128)} %param.21) | copy-start | bytes 28
  153.6 3.1 collective-permute-start.1
  154.3 45.8 %collective-permute-start.3 = (f32[2,384]{1,0:T(2,128)S(1)}, f32[2,384]{1,0:T(2,128)S(1)}, u32[]{:S(2)}, u32[]{:S(2)}) collective-permute-start(f32[2,384]{1,0:T(2,128)S(1)} %fusion.13), channel_id=1, source_target_pairs={{0,1},{1,0},{2,3},{3,2},{4,5},{5,4},{6,7},{7,6},{8,9},{9,8},{10,11... | collective-permute-start | bytes 9224 | tf_op jit(solution)/shard_map/ppermute | solution.py:1123
  156.8 1.0 copy-start.8
  199.7 1.5 collective-permute-start.2
  245.1 41.3 %collective-permute-start.4 = (bf16[1536,384]{1,0:T(8,128)(2,1)}, bf16[1536,384]{1,0:T(8,128)(2,1)S(1)}, u32[]{:S(2)}, u32[]{:S(2)}) collective-permute-start(bf16[1536,384]{1,0:T(8,128)(2,1)} %get-tuple-element.101), channel_id=1, source_target_pairs={{0,1},{1,0},{2,3},{3,2},{4,5},{5,4},{6,7},{7,6},{8,9},{9,8},{10,11... | collective-permute-start | bytes 3538952 | tf_op jit(solution)/shard_map/ppermute | solution.py:1123
  245.5 20.9 %copy-start.18 = (bf16[1536,768]{1,0:T(8,128)(2,1)S(1)}, bf16[1536,768]{1,0:T(8,128)(2,1)}, u32[]{:S(2)}) copy-start(bf16[1536,768]{1,0:T(8,128)(2,1)} %get-tuple-element.93) | copy-start | bytes 7077892
  245.6 20.9 %copy-start.19 = (bf16[1536,768]{1,0:T(8,128)(2,1)S(1)}, bf16[1536,768]{1,0:T(8,128)(2,1)}, u32[]{:S(2)}) copy-start(bf16[1536,768]{1,0:T(8,128)(2,1)} %get-tuple-element.94) | copy-start | bytes 7077892
  266.4 3.1 copy-start.17
  269.6 3.2 copy-start.16
  272.7 3.1 copy-start.21
  272.7 3.1 copy-start.22
  275.8 2.0 copy-start.9
  277.9 3.0 copy-start.15
  277.9 3.1 copy-start.20
  286.5 1.0 copy-start.10
  413.5 3.1 collective-permute-start.5
  413.7 6.3 %collective-permute-start.6 = (bf16[1536,384]{1,0:T(8,128)(2,1)}, bf16[1536,384]{1,0:T(8,128)(2,1)S(1)}, u32[]{:S(2)}, u32[]{:S(2)}) collective-permute-start(bf16[1536,384]{1,0:T(8,128)(2,1)} %get-tuple-element.109), channel_id=1, source_target_pairs={{0,1},{1,0},{2,3},{3,2},{4,5},{5,4},{6,7},{7,6},{8,9},{9,8},{10,11... | collective-permute-start | bytes 3538952 | tf_op jit(solution)/shard_map/ppermute | solution.py:1123
  414.1 6.1 %collective-permute-start.7 = (bf16[1536,384]{1,0:T(8,128)(2,1)}, bf16[1536,384]{1,0:T(8,128)(2,1)}, u32[]{:S(2)}, u32[]{:S(2)}) collective-permute-start(bf16[1536,384]{1,0:T(8,128)(2,1)} %get-tuple-element.110), channel_id=1, source_target_pairs={{0,1},{1,0},{2,3},{3,2},{4,5},{5,4},{6,7},{7,6},{8,9},{9,8},{10,11... | collective-permute-start | bytes 3538952 | tf_op jit(solution)/shard_map/ppermute | solution.py:1123
  416.6 3.5 copy-start.11
  420.0 1.0 copy-start.12
  441.6 39.4 %copy-start.4 = (f32[1,24,2304]{2,1,0:T(8,128)S(1)}, f32[1,24,2304]{2,1,0:T(8,128)}, u32[]{:S(2)}) copy-start(f32[1,24,2304]{2,1,0:T(8,128)} %param.23) | copy-start | bytes 663556
  441.6 39.4 %copy-start.5 = (f32[1,24,2304]{2,1,0:T(8,128)S(1)}, f32[1,24,2304]{2,1,0:T(8,128)}, u32[]{:S(2)}) copy-start(f32[1,24,2304]{2,1,0:T(8,128)} %param.28) | copy-start | bytes 663556
  441.7 41.2 %copy-start.6 = (f32[1,24,2304]{2,1,0:T(8,128)S(1)}, f32[1,24,2304]{2,1,0:T(8,128)}, u32[]{:S(2)}) copy-start(f32[1,24,2304]{2,1,0:T(8,128)} %param.33) | copy-start | bytes 663556
  481.1 8.4 %copy-start.1 = (bf16[256,384]{1,0:T(8,128)(2,1)S(1)}, bf16[256,384]{1,0:T(8,128)(2,1)}, u32[]{:S(2)}) copy-start(bf16[256,384]{1,0:T(8,128)(2,1)} %param.22) | copy-start | bytes 589828
  482.8 6.6 %copy-start.3 = (f32[24,2304]{1,0:T(8,128)}, f32[24,2304]{1,0:T(8,128)S(1)}, u32[]{:S(2)}) copy-start(f32[24,2304]{1,0:T(8,128)S(1)} %get-tuple-element.136) | copy-start | bytes 663556
  482.8 5.9 %copy-start.2 = (f32[24,2304]{1,0:T(8,128)S(1)}, f32[24,2304]{1,0:T(8,128)}, u32[]{:S(2)}) copy-start(f32[24,2304]{1,0:T(8,128)} %comm_scatter.1) | copy-start | bytes 663556
  (1 other events, 0.6 us)
Sparse Core Ops, SparseCore 0:
  11.6 113.5 all-gather.1
  286.6 171.3 reduce-scatter.3
